TPU v7x, 32 devices: a whole 2x2x4 slice. The times are simulated.
32 devices in a mesh: seq: 8 (over y, x, core), tile: 4 (over z).
Axes of the slice: x: 2, y: 2, z: 4, core: 2. Of those that a mesh axis runs over, the one named last changes fastest.
Arguments:
- inputs: bfloat16 [8, 13, 256, 1024], P('seq', None, 'tile'), may hold values from -6 to 6
- actions: int32 [8, 13], P('seq'), may hold values from 0 to 7
- segments: int32 [8, 13], P('seq'), may hold values from 0 to 3, never falling along the last dimension, each value on 1 to 6 neighbouring positions
- cotangent: bfloat16 [8, 13, 256, 1024], P('seq', None, 'tile'), may hold values from -6 to 6
- action_table: bfloat16 [8, 1024], P(None, 'seq'), may hold values from -6 to 6
- spatial_inward: bfloat16 [1024, 3072], P('seq'), may hold values from -0.1875 to 0.1875
- spatial_outward: bfloat16 [1024, 1024], P('seq'), may hold values from -3 to 3
- temporal_inward: bfloat16 [1024, 3072], P('seq'), may hold values from -0.1875 to 0.1875
- temporal_outward: bfloat16 [1024, 1024], P('seq'), may hold values from -0.375 to 0.375
- expand_weight: bfloat16 [1024, 4096], P('seq'), may hold values from -0.1875 to 0.1875
- contract_weight: bfloat16 [4096, 1024], P('seq'), may hold values from -0.09375 to 0.09375
- expand_bias: bfloat16 [4096], P('seq'), may hold values from -3 to 3
- contract_bias: bfloat16 [1024], P('seq'), may hold values from -3 to 3
- norm_gain: bfloat16 [3, 1024], P(None, 'seq'), may hold values from 0.5 to 1.5
- norm_shift: bfloat16 [3, 1024], P(None, 'seq'), may hold values from -3 to 3
Outputs:
- outputs: bfloat16 [8, 13, 256, 1024], P('seq', None, 'tile')
- input_grad: bfloat16 [8, 13, 256, 1024], P('seq', None, 'tile')
- action_table_grad: float32 [8, 1024], P(None, 'seq')
- spatial_inward_grad: float32 [1024, 3072], P('seq')
- spatial_outward_grad: float32 [1024, 1024], P('seq')
- temporal_inward_grad: float32 [1024, 3072], P('seq')
- temporal_outward_grad: float32 [1024, 1024], P('seq')
- expand_weight_grad: float32 [1024, 4096], P('seq')
- contract_weight_grad: float32 [4096, 1024], P('seq')
- expand_bias_grad: float32 [4096], P('seq')
- contract_bias_grad: float32 [1024], P('seq')
- norm_gain_grad: float32 [3, 1024], P(None, 'seq')
- norm_shift_grad: float32 [3, 1024], P(None, 'seq')
Inputs may be any that keep to these rules, and one draw needn't show every extreme that they name: Within a packed sequence the segment ids never fall from frame to frame; each sequence holds 4 segments of at most 6 frames each.
All inputs are finite; a program needn't handle non-finite values.
Results may differ from a plain program's by a relative error of at most 0.018.
Values may be sent and summed in bfloat16 or wider, within the bound.
No kernel may reach another device: no remote copies, remote signals or barrier semaphores. Data moves between devices by JAX's collectives and lax.ppermute only.
A program may use at most 320 MiB of HBM per device.

v0:
```python
import jax
import jax.numpy as jnp
from jax import lax
from jax.sharding import PartitionSpec as P

HEAD = 64


epsilon = 1e-05
masked_score = -1e30


def gelu_tanh(hidden):
    return jax.nn.gelu(hidden, approximate=True)


def norm_parts(hidden, gain_row, shift_row):
    centre = jnp.mean(hidden, axis=-1, keepdims=True)
    centred = hidden - centre
    spread = jnp.mean(centred * centred, axis=-1, keepdims=True)
    inverse = lax.rsqrt(spread + epsilon)
    normed = centred * inverse
    return ((normed * gain_row + shift_row).astype(jnp.bfloat16), normed, inverse)


def norm_back(upstream, normed, inverse, gain_row):
    scaled = upstream * gain_row
    mean_first = jnp.mean(scaled, axis=-1, keepdims=True)
    mean_second = jnp.mean(scaled * normed, axis=-1, keepdims=True)
    grad_back = inverse * (scaled - mean_first - normed * mean_second)
    return (grad_back, jnp.sum(upstream * normed, axis=0), jnp.sum(upstream, axis=0))


def soft_rows(scores):
    row_top = jnp.max(scores, axis=-1, keepdims=True)
    powered = jnp.exp(scores - row_top)
    row_total = jnp.sum(powered, axis=-1, keepdims=True)
    return (powered / row_total, row_top + jnp.log(row_total))


def score_grads(softmaxed, grad_soft):
    inner_sum = jnp.sum(grad_soft * softmaxed, axis=-1, keepdims=True)
    return (softmaxed * (grad_soft - inner_sum)).astype(jnp.bfloat16)


def body(
    inputs,
    actions,
    segments,
    cotangent,
    action_table,
    spatial_inward,
    spatial_outward,
    temporal_inward,
    temporal_outward,
    expand_weight,
    contract_weight,
    expand_bias,
    contract_bias,
    norm_gain,
    norm_shift,
):
    (
        table_full,
        space_in,
        space_out,
        time_in,
        time_out,
        expand_full,
        contract_full,
        expand_shift,
        contract_shift,
        gain_full,
        shift_full,
    ) = (
        lax.all_gather(action_table, "seq", axis=1, tiled=True),
        lax.all_gather(spatial_inward, "seq", axis=0, tiled=True),
        lax.all_gather(spatial_outward, "seq", axis=0, tiled=True),
        lax.all_gather(temporal_inward, "seq", axis=0, tiled=True),
        lax.all_gather(temporal_outward, "seq", axis=0, tiled=True),
        lax.all_gather(expand_weight, "seq", axis=0, tiled=True),
        lax.all_gather(contract_weight, "seq", axis=0, tiled=True),
        lax.all_gather(expand_bias, "seq", axis=0, tiled=True),
        lax.all_gather(contract_bias, "seq", axis=0, tiled=True),
        lax.all_gather(norm_gain, "seq", axis=1, tiled=True),
        lax.all_gather(norm_shift, "seq", axis=1, tiled=True),
    )
    packed_count, frames, tile_cells, model_width = inputs.shape
    row_count = packed_count * frames * tile_cells
    head_count = model_width // HEAD
    score_scale = HEAD ** (-0.5)
    frame_width = tile_cells * lax.axis_size("tile")
    gain_rows = gain_full.astype(jnp.float32)
    shift_rows = shift_full.astype(jnp.float32)
    f32 = jnp.float32
    bf16 = jnp.bfloat16
    onehot = (
        actions[:, :, None] == jnp.arange(table_full.shape[0], dtype=jnp.int32)[None, None, :]
    ).astype(bf16)
    embedded = jnp.einsum("sfa,ad->sfd", onehot, table_full, preferred_element_type=f32)
    embed_sum = (inputs.astype(f32) + embedded[:, :, None, :]).reshape(row_count, model_width)
    normed_one, unit_one, inverse_one = norm_parts(embed_sum, gain_rows[0], shift_rows[0])
    projected = jnp.dot(normed_one, space_in, preferred_element_type=f32).astype(bf16)
    space_query = projected[:, :model_width].reshape(
        packed_count, frames, tile_cells, head_count, HEAD
    )
    own_keys = projected[:, model_width : 2 * model_width].reshape(
        packed_count, frames, tile_cells, model_width
    )
    own_values = projected[:, 2 * model_width :].reshape(
        packed_count, frames, tile_cells, model_width
    )
    frame_keys, frame_values = (
        lax.all_gather(own_keys, "tile", axis=2, tiled=True),
        lax.all_gather(own_values, "tile", axis=2, tiled=True),
    )
    key_heads = frame_keys.reshape(packed_count, frames, frame_width, head_count, HEAD)
    value_heads = frame_values.reshape(packed_count, frames, frame_width, head_count, HEAD)

    def space_scores():
        return (
            jnp.einsum("sfqhd,sfkhd->sfhqk", space_query, key_heads, preferred_element_type=f32)
            * score_scale
        )

    space_soft, space_lse = soft_rows(space_scores())
    space_mixed = jnp.einsum(
        "sfhqk,sfkhd->sfqhd", space_soft.astype(bf16), value_heads, preferred_element_type=f32
    )
    space_mixed = space_mixed.astype(bf16).reshape(row_count, model_width)
    space_sum = embed_sum + jnp.dot(space_mixed, space_out, preferred_element_type=f32)
    normed_two, unit_two, inverse_two = norm_parts(space_sum, gain_rows[1], shift_rows[1])
    time_proj = jnp.dot(normed_two, time_in, preferred_element_type=f32).astype(bf16)
    time_proj = time_proj.reshape(packed_count, frames, tile_cells, 3, head_count, HEAD)
    time_query = time_proj[:, :, :, 0]
    time_keys = time_proj[:, :, :, 1]
    time_values = time_proj[:, :, :, 2]
    frame_index = jnp.arange(frames, dtype=jnp.int32)
    allowed = (frame_index[None, None, :] <= frame_index[None, :, None]) & (
        segments[:, None, :] == segments[:, :, None]
    )
    allowed_heads = allowed[:, None, None, :, :]

    def time_scores():
        raw_scores = (
            jnp.einsum("sfphd,sgphd->sphfg", time_query, time_keys, preferred_element_type=f32)
            * score_scale
        )
        return jnp.where(allowed_heads, raw_scores, masked_score)

    time_soft, time_lse = soft_rows(time_scores())
    time_mixed = jnp.einsum(
        "sphfg,sgphd->sfphd", time_soft.astype(bf16), time_values, preferred_element_type=f32
    )
    time_mixed = time_mixed.astype(bf16).reshape(row_count, model_width)
    time_sum = space_sum + jnp.dot(time_mixed, time_out, preferred_element_type=f32)
    normed_three, unit_three, inverse_three = norm_parts(time_sum, gain_rows[2], shift_rows[2])
    expanded = jnp.dot(normed_three, expand_full, preferred_element_type=f32) + expand_shift.astype(
        f32
    )
    activated, gelu_pull = jax.vjp(gelu_tanh, expanded)
    activated_low = activated.astype(bf16)
    block_out = (
        time_sum
        + jnp.dot(activated_low, contract_full, preferred_element_type=f32)
        + contract_shift.astype(f32)
    )
    outputs = block_out.astype(bf16).reshape(inputs.shape)
    upstream = cotangent.astype(f32).reshape(row_count, model_width)
    grad_contract_shift = jnp.sum(upstream, axis=0)
    upstream_low = upstream.astype(bf16)
    grad_contract = jnp.einsum("rf,rd->fd", activated_low, upstream_low, preferred_element_type=f32)
    grad_activated = jnp.einsum(
        "rd,fd->rf", upstream_low, contract_full, preferred_element_type=f32
    )
    grad_expanded = gelu_pull(grad_activated)[0].astype(bf16)
    grad_expand_shift = jnp.sum(grad_expanded.astype(f32), axis=0)
    grad_expand = jnp.einsum("rd,rf->df", normed_three, grad_expanded, preferred_element_type=f32)
    grad_normed_three = jnp.einsum(
        "rf,df->rd", grad_expanded, expand_full, preferred_element_type=f32
    )
    back_three, gain_three, shift_three = norm_back(
        grad_normed_three, unit_three, inverse_three, gain_rows[2]
    )
    grad_time_sum = upstream + back_three
    time_low = grad_time_sum.astype(bf16)
    grad_time_out = jnp.einsum("rd,re->de", time_mixed, time_low, preferred_element_type=f32)
    grad_time_mixed = jnp.einsum(
        "re,de->rd", time_low, time_out, preferred_element_type=f32
    ).astype(bf16)
    grad_time_mixed = grad_time_mixed.reshape(packed_count, frames, tile_cells, head_count, HEAD)
    time_again = jnp.exp(time_scores() - time_lse)
    grad_time_values = jnp.einsum(
        "sphfg,sfphd->sgphd", time_again.astype(bf16), grad_time_mixed, preferred_element_type=f32
    )
    grad_time_soft = jnp.einsum(
        "sfphd,sgphd->sphfg", grad_time_mixed, time_values, preferred_element_type=f32
    )
    grad_time_scores = score_grads(time_again, grad_time_soft)
    grad_time_query = (
        jnp.einsum("sphfg,sgphd->sfphd", grad_time_scores, time_keys, preferred_element_type=f32)
        * score_scale
    )
    grad_time_keys = (
        jnp.einsum("sphfg,sfphd->sgphd", grad_time_scores, time_query, preferred_element_type=f32)
        * score_scale
    )
    grad_time_proj = jnp.stack([grad_time_query, grad_time_keys, grad_time_values], axis=3).astype(
        bf16
    )
    grad_time_proj = grad_time_proj.reshape(row_count, 3 * model_width)
    grad_time_in = jnp.einsum("rd,re->de", normed_two, grad_time_proj, preferred_element_type=f32)
    grad_normed_two = jnp.einsum("re,de->rd", grad_time_proj, time_in, preferred_element_type=f32)
    back_two, gain_two, shift_two = norm_back(grad_normed_two, unit_two, inverse_two, gain_rows[1])
    grad_space_sum = grad_time_sum + back_two
    space_low = grad_space_sum.astype(bf16)
    grad_space_out = jnp.einsum("rd,re->de", space_mixed, space_low, preferred_element_type=f32)
    grad_space_mixed = jnp.einsum(
        "re,de->rd", space_low, space_out, preferred_element_type=f32
    ).astype(bf16)
    grad_space_mixed = grad_space_mixed.reshape(packed_count, frames, tile_cells, head_count, HEAD)
    space_again = jnp.exp(space_scores() - space_lse)
    grad_space_soft = jnp.einsum(
        "sfqhd,sfkhd->sfhqk", grad_space_mixed, value_heads, preferred_element_type=f32
    )
    grad_space_scores = score_grads(space_again, grad_space_soft)
    grad_space_query = (
        jnp.einsum("sfhqk,sfkhd->sfqhd", grad_space_scores, key_heads, preferred_element_type=f32)
        * score_scale
    )
    grad_frame_values = jnp.einsum(
        "sfhqk,sfqhd->sfkhd", space_again.astype(bf16), grad_space_mixed, preferred_element_type=f32
    )
    grad_frame_keys = (
        jnp.einsum("sfhqk,sfqhd->sfkhd", grad_space_scores, space_query, preferred_element_type=f32)
        * score_scale
    )
    grad_frame_keys = grad_frame_keys.reshape(packed_count, frames, frame_width, model_width)
    grad_frame_values = grad_frame_values.reshape(packed_count, frames, frame_width, model_width)
    own_grad_keys, own_grad_values = (
        lax.psum_scatter(
            grad_frame_keys.astype(jnp.bfloat16), "tile", scatter_dimension=2, tiled=True
        ).astype(jnp.float32),
        lax.psum_scatter(
            grad_frame_values.astype(jnp.bfloat16), "tile", scatter_dimension=2, tiled=True
        ).astype(jnp.float32),
    )
    grad_space_proj = jnp.concatenate(
        [
            grad_space_query.reshape(row_count, model_width),
            own_grad_keys.reshape(row_count, model_width),
            own_grad_values.reshape(row_count, model_width),
        ],
        axis=1,
    ).astype(bf16)
    grad_space_in = jnp.einsum("rd,re->de", normed_one, grad_space_proj, preferred_element_type=f32)
    grad_normed_one = jnp.einsum("re,de->rd", grad_space_proj, space_in, preferred_element_type=f32)
    back_one, gain_one, shift_one = norm_back(grad_normed_one, unit_one, inverse_one, gain_rows[0])
    grad_embed_sum = grad_space_sum + back_one
    input_grad = grad_embed_sum.astype(bf16).reshape(inputs.shape)
    per_frame = jnp.sum(
        grad_embed_sum.reshape(packed_count, frames, tile_cells, model_width), axis=2
    )
    grad_table = jnp.einsum(
        "sfa,sfd->ad", onehot.astype(f32), per_frame, precision=lax.Precision.HIGHEST
    )
    grad_gains = jnp.stack([gain_one, gain_two, gain_three], axis=0)
    grad_shifts = jnp.stack([shift_one, shift_two, shift_three], axis=0)
    local_grads = (
        grad_table,
        grad_space_in,
        grad_space_out,
        grad_time_in,
        grad_time_out,
        grad_expand,
        grad_contract,
        grad_expand_shift,
        grad_contract_shift,
        grad_gains,
        grad_shifts,
    )
    shards = (
        lax.psum_scatter(
            local_grads[0].astype(jnp.bfloat16), "seq", scatter_dimension=1, tiled=True
        ).astype(jnp.float32),
        lax.psum_scatter(
            local_grads[1].astype(jnp.bfloat16), "seq", scatter_dimension=0, tiled=True
        ).astype(jnp.float32),
        lax.psum_scatter(
            local_grads[2].astype(jnp.bfloat16), "seq", scatter_dimension=0, tiled=True
        ).astype(jnp.float32),
        lax.psum_scatter(
            local_grads[3].astype(jnp.bfloat16), "seq", scatter_dimension=0, tiled=True
        ).astype(jnp.float32),
        lax.psum_scatter(
            local_grads[4].astype(jnp.bfloat16), "seq", scatter_dimension=0, tiled=True
        ).astype(jnp.float32),
        lax.psum_scatter(
            local_grads[5].astype(jnp.bfloat16), "seq", scatter_dimension=0, tiled=True
        ).astype(jnp.float32),
        lax.psum_scatter(
            local_grads[6].astype(jnp.bfloat16), "seq", scatter_dimension=0, tiled=True
        ).astype(jnp.float32),
        lax.psum_scatter(
            local_grads[7].astype(jnp.bfloat16), "seq", scatter_dimension=0, tiled=True
        ).astype(jnp.float32),
        lax.psum_scatter(
            local_grads[8].astype(jnp.bfloat16), "seq", scatter_dimension=0, tiled=True
        ).astype(jnp.float32),
        lax.psum_scatter(
            local_grads[9].astype(jnp.bfloat16), "seq", scatter_dimension=1, tiled=True
        ).astype(jnp.float32),
        lax.psum_scatter(
            local_grads[10].astype(jnp.bfloat16), "seq", scatter_dimension=1, tiled=True
        ).astype(jnp.float32),
    )
    summed = (
        lax.psum(shards[0].astype(jnp.bfloat16), "tile").astype(jnp.float32),
        lax.psum(shards[1].astype(jnp.bfloat16), "tile").astype(jnp.float32),
        lax.psum(shards[2].astype(jnp.bfloat16), "tile").astype(jnp.float32),
        lax.psum(shards[3].astype(jnp.bfloat16), "tile").astype(jnp.float32),
        lax.psum(shards[4].astype(jnp.bfloat16), "tile").astype(jnp.float32),
        lax.psum(shards[5].astype(jnp.bfloat16), "tile").astype(jnp.float32),
        lax.psum(shards[6].astype(jnp.bfloat16), "tile").astype(jnp.float32),
        lax.psum(shards[7].astype(jnp.bfloat16), "tile").astype(jnp.float32),
        lax.psum(shards[8].astype(jnp.bfloat16), "tile").astype(jnp.float32),
        lax.psum(shards[9].astype(jnp.bfloat16), "tile").astype(jnp.float32),
        lax.psum(shards[10].astype(jnp.bfloat16), "tile").astype(jnp.float32),
    )
    return (
        outputs,
        input_grad,
        summed[0],
        summed[1],
        summed[2],
        summed[3],
        summed[4],
        summed[5],
        summed[6],
        summed[7],
        summed[8],
        summed[9],
        summed[10],
    )


def solution(mesh):
    placed = (
        P("seq", None, "tile", None),
        P("seq", None),
        P("seq", None),
        P("seq", None, "tile", None),
        P(None, "seq"),
        P("seq", None),
        P("seq", None),
        P("seq", None),
        P("seq", None),
        P("seq", None),
        P("seq", None),
        P("seq"),
        P("seq"),
        P(None, "seq"),
        P(None, "seq"),
    )
    return jax.shard_map(
        body,
        mesh=mesh,
        in_specs=placed,
        out_specs=(
            P("seq", None, "tile", None),
            P("seq", None, "tile", None),
            P(None, "seq"),
            P("seq", None),
            P("seq", None),
            P("seq", None),
            P("seq", None),
            P("seq", None),
            P("seq", None),
            P("seq"),
            P("seq"),
            P(None, "seq"),
            P(None, "seq"),
        ),
        check_vma=False,
    )
```

profile of v0, /device:TPU:0, one launch (start us, length us, event | category | flops | bytes accessed | tf_op | source)
XLA Modules:
  0.0 1584.4 jit_solution(6852255820230631596)
XLA Ops:
  8.0 10.5 all_gather.39
  23.7 8.9 all_gather.40
  32.5 7.9 all_gather.41
  42.3 15.9 %all-gather.11.cloned.1.call-done = bf16[1024,3072]{1,0:T(8,128)(2,1)} async-done(((bf16[128,3072]{1,0:T(8,128)(2,1)}), bf16[1024,3072]{1,0:T(8,128)(2,1)}) %all-gather.11.cloned.1.call-update) | async-done | bytes 6291472 | tf_op jit(solution)/shard_map/all_gather | solution.py:77
  58.2 8.0 convolution_convert_fusion.6
  72.9 9.3 all-gather
  86.6 4.8 copy.75
  91.4 101.4 %all-gather.15.cloned.1.call-done = bf16[1,13,256,1024]{3,2,1,0:T(8,128)(2,1)} async-done(((bf16[1,13,64,1024]{3,2,1,0:T(8,128)(2,1)}), bf16[1,13,256,1024]{3,2,1,0:T(8,128)(2,1)}) %all-gather.15.cloned.1.call-update) | async-done | bytes 6815760 | tf_op jit(solution)/shard_map/all_gather | solution.py:114
  192.8 10.3 copy.61
  203.2 114.0 %all-gather.13.cloned.1.call-done = bf16[1,13,256,1024]{3,2,1,0:T(8,128)(2,1)} async-done(((bf16[1,13,64,1024]{3,2,1,0:T(8,128)(2,1)}), bf16[1,13,256,1024]{3,2,1,0:T(8,128)(2,1)}) %all-gather.13.cloned.1.call-update) | async-done | bytes 6815760 | tf_op jit(solution)/shard_map/all_gather | solution.py:115
  317.1 10.3 copy.60
  327.4 6.9 multiply_reduce_fusion.1
  339.3 8.1 convert_bitcast_fusion.2
  347.4 6.1 copy.63
  353.6 6.0 reshape.500
  365.9 26.4 %all-gather.19.cloned.1.call-done = bf16[1024,3072]{1,0:T(8,128)(2,1)} async-done(((bf16[128,3072]{1,0:T(8,128)(2,1)}), bf16[1024,3072]{1,0:T(8,128)(2,1)}) %all-gather.19.cloned.1.call-update) | async-done | bytes 6291472 | tf_op jit(solution)/shard_map/all_gather | solution.py:79
  392.3 10.5 convolution_convert_fusion.5
  402.7 13.3 reshape.501
  416.0 6.5 fusion.55
  422.6 5.8 fusion.27
  433.2 4.8 convert_bitcast_fusion.1
  442.2 5.2 fusion.60
  450.0 28.3 %all-gather.23.cloned.1.call-done = bf16[1024,4096]{1,0:T(8,128)(2,1)} async-done(((bf16[128,4096]{1,0:T(8,128)(2,1)}), bf16[1024,4096]{1,0:T(8,128)(2,1)}) %all-gather.23.cloned.1.call-update) | async-done | bytes 8388624 | tf_op jit(solution)/shard_map/all_gather | solution.py:81
  478.3 13.9 fusion.51
  492.1 42.4 %all-gather.25.cloned.1.call-done = bf16[4096,1024]{1,0:T(8,128)(2,1)} async-done(((bf16[512,1024]{1,0:T(8,128)(2,1)}), bf16[4096,1024]{1,0:T(8,128)(2,1)}) %all-gather.25.cloned.1.call-update) | async-done | bytes 8388624 | tf_op jit(solution)/shard_map/all_gather | solution.py:82
  534.6 22.6 %fusion.52 = (bf16[4096]{0:T(1024)(128)(2,1)}, bf16[832,4096]{1,0:T(8,128)(2,1)}) fusion(f32[832,4096]{1,0:T(8,128)} %fusion.51, f32[4096]{0:T(1024)S(1)} %bitcast.176, bf16[832,1024]{1,0:T(8,128)(2,1)} %bitcast.155, bf16[4096,1024]{1,0:T(8,128)(2,1)} %all-gather.25.cloned.1.call-done), kind=kOutput, calls=%fused_computation.128 | convolution fusion | flops 7054290944 | bytes 30564352 | tf_op jit(solution)/shard_map/rd,fd->rf/dot_general | solution.py:173
  557.1 13.3 multiply_reduce_fusion.3
  581.3 8.9 convert_bitcast_fusion
  590.2 12.0 multiply_reduce_fusion.2
  602.2 7.9 multiply_convert_fusion.5
  620.4 5.3 copy.72
  625.7 13.8 convert_element_type.256
  639.5 10.2 multiply_reduce_fusion.4
  658.3 5.8 copy.77
  664.1 8.1 convolution_convert_fusion.2
  672.2 10.3 copy.78
  682.6 13.3 multiply_reduce_fusion
  695.9 10.4 multiply_convert_fusion.1
  706.3 5.0 multiply_convert_fusion
  711.4 10.2 copy.76
  721.7 6.3 convolution_convert_fusion.7
  728.3 5.2 convolution_convert_fusion.8
  733.5 12.1 convolution_convert_fusion.3
  747.1 16.9 %convolution_convert_fusion = bf16[4096,1024]{1,0:T(8,128)(2,1)} fusion(bf16[832,1024]{1,0:T(8,128)(2,1)S(1)} %bitcast.156, f32[832,4096]{1,0:T(8,128)} %fusion.51, f32[4096]{0:T(1024)S(1)} %bitcast.177), kind=kOutput, calls=%fused_computation.28 | convolution fusion | flops 7017594880 | bytes 23740416 | tf_op jit(solution)/shard_map/rf,rd->fd/dot_general | solution.py:172
  766.0 14.6 convolution_convert_fusion.1
  780.6 8.7 fusion.28
  789.3 5.4 copy.74
  801.9 121.9 %reduce-scatter.18.cloned.1.call-done = bf16[1,13,64,1024]{3,2,1,0:T(8,128)(2,1)} async-done(((bf16[1,13,256,1024]{3,2,1,0:T(8,128)(2,1)}), bf16[1,13,64,1024]{3,2,1,0:T(8,128)(2,1)}) %reduce-scatter.18.cloned.1.call-update) | async-done | bytes 1703952 | tf_op jit(solution)/shard_map/reduce_scatter | solution.py:241
  923.9 11.4 convolution_convert_fusion.4
  937.5 12.5 multiply_reduce_fusion.5
  950.9 5.1 fusion.54
  960.7 8.8 reduce-scatter.28.cloned.1.call-done
  969.5 45.3 %reduce-scatter.24.cloned.1.call-done = bf16[128,1024]{1,0:T(8,128)(2,1)} async-done(((bf16[1024,1024]{1,0:T(8,128)(2,1)}), bf16[128,1024]{1,0:T(8,128)(2,1)}) %reduce-scatter.24.cloned.1.call-update) | async-done | bytes 262160 | tf_op jit(solution)/shard_map/reduce_scatter | solution.py:289
  1014.8 65.2 %reduce-scatter.26.cloned.1.call-done = bf16[128,3072]{1,0:T(8,128)(2,1)} async-done(((bf16[1024,3072]{1,0:T(8,128)(2,1)}), bf16[128,3072]{1,0:T(8,128)(2,1)}) %reduce-scatter.26.cloned.1.call-update) | async-done | bytes 786448 | tf_op jit(solution)/shard_map/reduce_scatter | solution.py:292
  1080.0 75.0 %reduce-scatter.32.cloned.1.call-done = bf16[512,1024]{1,0:T(8,128)(2,1)} async-done(((bf16[4096,1024]{1,0:T(8,128)(2,1)}), bf16[512,1024]{1,0:T(8,128)(2,1)}) %reduce-scatter.32.cloned.1.call-update) | async-done | bytes 1048592 | tf_op jit(solution)/shard_map/reduce_scatter | solution.py:301
  1155.0 74.6 %reduce-scatter.30.cloned.1.call-done = bf16[128,4096]{1,0:T(8,128)(2,1)} async-done(((bf16[1024,4096]{1,0:T(8,128)(2,1)}), bf16[128,4096]{1,0:T(8,128)(2,1)}) %reduce-scatter.30.cloned.1.call-update) | async-done | bytes 1048592 | tf_op jit(solution)/shard_map/reduce_scatter | solution.py:298
  1229.6 65.4 %reduce-scatter.22.cloned.1.call-done = bf16[128,3072]{1,0:T(8,128)(2,1)} async-done(((bf16[1024,3072]{1,0:T(8,128)(2,1)}), bf16[128,3072]{1,0:T(8,128)(2,1)}) %reduce-scatter.22.cloned.1.call-update) | async-done | bytes 786448 | tf_op jit(solution)/shard_map/reduce_scatter | solution.py:286
  1298.6 8.6 all-gather.1
  1307.3 23.7 %all-reduce.2 = (bf16[4096]{0:T(1024)(128)(2,1)S(1)}, bf16[1024]{0:T(1024)(128)(2,1)S(1)}) all-reduce(bf16[4096]{0:T(1024)(128)(2,1)S(1)} %copy-done.54, bf16[1024]{0:T(1024)(128)(2,1)S(1)} %reduce_sum.249), channel_id=11, replica_groups=mesh['seq'=8,'tile'=4] {'seq'}, use_global_device_ids=true, to_apply=%region_36.37.clone | all-reduce | flops 5120 | bytes 20480
  1331.2 15.2 add_convert_fusion
  1347.2 22.3 %reduce-scatter.36.cloned.1.call-done = bf16[128,3]{1,0:T(8,128)(2,1)} async-done(((bf16[1024,3]{1,0:T(8,128)(2,1)}), bf16[128,3]{1,0:T(8,128)(2,1)}) %reduce-scatter.36.cloned.1.call-update) | async-done | bytes 784
  1370.3 36.5 %reduce-scatter.34.cloned.1.call-done = bf16[128,8]{1,0:T(8,128)(2,1)} async-done(((bf16[1024,8]{1,0:T(8,128)(2,1)}), bf16[128,8]{1,0:T(8,128)(2,1)}) %reduce-scatter.34.cloned.1.call-update) | async-done | bytes 2064
  1407.5 12.0 all-reduce.3
  1422.4 144.1 %all-reduce.7.cloned.1.call-done = (bf16[128,3072]{1,0:T(8,128)(2,1)}, bf16[128,1024]{1,0:T(8,128)(2,1)}, bf16[128,3072]{1,0:T(8,128)(2,1)}, bf16[128,1024]{1,0:...) async-done(((bf16[128,3072]{1,0:T(8,128)(2,1)}, bf16[128,1024]{1,0:T(8,128)(2,1)}, bf16[128,3072]{1,0:T(8,128)(2,1)}, bf16[128,1024]{1,0:T(8,128)(2,1)}, ...) | async-done | bytes 4194320 | tf_op jit(solution)/shard_map/psum | solution.py:319
  (259 shorter events, 108.1 us)
Async XLA Ops:
  7.2 16.5 %copy-start.63 = (bf16[3,128]{1,0:T(4,128)(2,1)S(1)}, bf16[3,128]{1,0:T(4,128)(2,1)}, u32[]{:S(2)}) copy-start(bf16[3,128]{1,0:T(4,128)(2,1)} %param.28) | copy-start | bytes 2308
  7.2 25.4 %copy-start.64 = (bf16[3,128]{1,0:T(4,128)(2,1)S(1)}, bf16[3,128]{1,0:T(4,128)(2,1)}, u32[]{:S(2)}) copy-start(bf16[3,128]{1,0:T(4,128)(2,1)} %param.29) | copy-start | bytes 2308
  7.2 51.0 %all-gather.11.cloned.1.call-start = ((), (), s32[]{:S(2)}) async-start(), calls=%async_computation.11 | async-start | bytes 7077888 | tf_op jit(solution)/shard_map/all_gather | solution.py:77
  7.9 184.9 %all-gather.15.cloned.1.call-start = ((), (), s32[]{:S(2)}) async-start(), calls=%async_computation.13 | async-start | bytes 8519680 | tf_op jit(solution)/shard_map/all_gather | solution.py:114
  21.5 20.9 %copy-start.36 = (f32[832]{0:T(1024)}, f32[832]{0:T(1024)S(1)}, u32[]{:S(2)}) copy-start(f32[832]{0:T(1024)S(1)} %div.57) | copy-start | bytes 9988
  23.6 42.7 %copy-start.4 = (f32[1,13,64,1024]{3,2,1,0:T(8,128)}, f32[1,13,64,1024]{3,2,1,0:T(8,128)S(1)}, u32[]{:S(2)}) copy-start(f32[1,13,64,1024]{3,2,1,0:T(8,128)S(1)} %get-tuple-element.49) | copy-start | bytes 10223620
  23.7 42.6 %copy-start.38 = (f32[832]{0:T(1024)}, f32[832]{0:T(1024)S(1)}, u32[]{:S(2)}) copy-start(f32[832]{0:T(1024)S(1)} %rsqrt.28) | copy-start | bytes 9988
  40.5 25.8 %copy-start.42 = (f32[1,1024]{1,0:T(1,128)}, f32[1,1024]{1,0:T(1,128)S(1)}, u32[]{:S(2)}) copy-start(f32[1,1024]{1,0:T(1,128)S(1)} %get-tuple-element.52) | copy-start | bytes 12292
  40.5 351.8 %copy-start.46 = (f32[1,1024]{1,0:T(1,128)}, f32[1,1024]{1,0:T(1,128)S(1)}, u32[]{:S(2)}) copy-start(f32[1,1024]{1,0:T(1,128)S(1)} %get-tuple-element.51) | copy-start | bytes 12292
  40.5 530.0 %copy-start.50 = (f32[1,1024]{1,0:T(1,128)}, f32[1,1024]{1,0:T(1,128)S(1)}, u32[]{:S(2)}) copy-start(f32[1,1024]{1,0:T(1,128)S(1)} %get-tuple-element.50) | copy-start | bytes 12292
  40.5 351.8 %copy-start.57 = (f32[1,1024]{1,0:T(1,128)}, f32[1,1024]{1,0:T(1,128)S(1)}, u32[]{:S(2)}) copy-start(f32[1,1024]{1,0:T(1,128)S(1)} %get-tuple-element.54) | copy-start | bytes 12292
  40.5 437.7 %copy-start.55 = (f32[1,1024]{1,0:T(1,128)}, f32[1,1024]{1,0:T(1,128)S(1)}, u32[]{:S(2)}) copy-start(f32[1,1024]{1,0:T(1,128)S(1)} %get-tuple-element.53) | copy-start | bytes 12292
  68.8 248.4 %all-gather.13.cloned.1.call-start = ((), (), s32[]{:S(2)}) async-start(), calls=%async_computation.12 | async-start | bytes 8519680 | tf_op jit(solution)/shard_map/all_gather | solution.py:115
  69.5 290.1 %all-gather.17.cloned.1.call-start = ((), (), s32[]{:S(2)}) async-start(), calls=%async_computation.14 | async-start | bytes 2359296 | tf_op jit(solution)/shard_map/all_gather | solution.py:78
  70.1 322.2 %all-gather.19.cloned.1.call-start = ((), (), s32[]{:S(2)}) async-start(), calls=%async_computation.15 | async-start | bytes 7077888 | tf_op jit(solution)/shard_map/all_gather | solution.py:79
  70.7 371.5 %all-gather.21.cloned.1.call-start = ((), (), s32[]{:S(2)}) async-start(), calls=%async_computation.16 | async-start | bytes 2359296 | tf_op jit(solution)/shard_map/all_gather | solution.py:80
  71.2 407.0 %all-gather.23.cloned.1.call-start = ((), (), s32[]{:S(2)}) async-start(), calls=%async_computation.17 | async-start | bytes 9437184 | tf_op jit(solution)/shard_map/all_gather | solution.py:81
  72.0 462.6 %all-gather.25.cloned.1.call-start = ((), (), s32[]{:S(2)}) async-start(), calls=%async_computation.18 | async-start | bytes 9437184 | tf_op jit(solution)/shard_map/all_gather | solution.py:82
  72.7 729.2 %reduce-scatter.20.cloned.1.call-start = ((), (), s32[]{:S(2)}) async-start(), calls=%async_computation.20 | async-start | bytes 8519680 | tf_op jit(solution)/shard_map/reduce_scatter | solution.py:244
  82.2 452.4 %copy-start.52 = (f32[8,1,512]{2,1,0:T(1,128)}, f32[8,1,512]{2,1,0:T(1,128)S(1)}, u32[]{:S(2)}) copy-start(f32[8,1,512]{2,1,0:T(1,128)S(1)} %convert_element_type.288) | copy-start | bytes 49156
  334.3 5.0 copy-start
  338.4 9.0 copy-start.32
  353.5 6.0 copy-start.5
  363.7 39.0 %copy-start.34 = (f32[832]{0:T(1024)}, f32[832]{0:T(1024)S(1)}, u32[]{:S(2)}) copy-start(f32[832]{0:T(1024)S(1)} %broadcast_multiply_fusion.8) | copy-start | bytes 9988
  365.9 36.8 %copy-start.44 = (f32[832]{0:T(1024)}, f32[832]{0:T(1024)S(1)}, u32[]{:S(2)}) copy-start(f32[832]{0:T(1024)S(1)} %add_rsqrt_fusion.2) | copy-start | bytes 9988
  422.6 5.8 copy-start.7
  422.6 5.8 copy-start.9
  442.2 5.8 copy-start.33
  442.2 6.9 copy-start.26
  442.2 6.9 copy-start.28
  447.4 123.0 %copy-start.15 = (f32[832,1024]{1,0:T(8,128)}, f32[832,1024]{1,0:T(8,128)S(1)}, u32[]{:S(2)}) copy-start(f32[832,1024]{1,0:T(8,128)S(1)} %get-tuple-element.63) | copy-start | bytes 10223620
  447.5 123.0 %copy-start.40 = (f32[832]{0:T(1024)}, f32[832]{0:T(1024)S(1)}, u32[]{:S(2)}) copy-start(f32[832]{0:T(1024)S(1)} %broadcast_multiply_fusion.7) | copy-start | bytes 9988
  448.0 122.5 %copy-start.48 = (f32[832]{0:T(1024)}, f32[832]{0:T(1024)S(1)}, u32[]{:S(2)}) copy-start(f32[832]{0:T(1024)S(1)} %add_rsqrt_fusion.1) | copy-start | bytes 9988
  557.1 13.4 copy-start.22
  602.2 7.9 copy-start.10
  625.6 13.9 copy-start.19
  625.7 13.9 copy-start.35
  625.7 13.9 copy-start.45
  625.7 13.9 copy-start.47
  639.5 10.3 copy-start.21
  658.3 5.9 copy-start.24
  682.5 241.3 %reduce-scatter.18.cloned.1.call-start = ((), (), s32[]{:S(2)}) async-start(), calls=%async_computation.19 | async-start | bytes 8519680 | tf_op jit(solution)/shard_map/reduce_scatter | solution.py:241
  695.9 10.4 copy-start.3
  706.3 5.0 copy-start.2
  721.6 6.7 copy-start.14
  721.6 247.8 %reduce-scatter.28.cloned.1.call-start = ((), (), s32[]{:S(2)}) async-start(), calls=%async_computation.24 | async-start | bytes 2359296 | tf_op jit(solution)/shard_map/reduce_scatter | solution.py:295
  728.1 5.5 copy-start.58
  728.1 286.8 %reduce-scatter.24.cloned.1.call-start = ((), (), s32[]{:S(2)}) async-start(), calls=%async_computation.22 | async-start | bytes 2359296 | tf_op jit(solution)/shard_map/reduce_scatter | solution.py:289
  733.5 346.5 %reduce-scatter.26.cloned.1.call-start = ((), (), s32[]{:S(2)}) async-start(), calls=%async_computation.23 | async-start | bytes 7077888 | tf_op jit(solution)/shard_map/reduce_scatter | solution.py:292
  745.7 409.3 %reduce-scatter.32.cloned.1.call-start = ((), (), s32[]{:S(2)}) async-start(), calls=%async_computation.26 | async-start | bytes 9437184 | tf_op jit(solution)/shard_map/reduce_scatter | solution.py:301
  764.1 465.5 %reduce-scatter.30.cloned.1.call-start = ((), (), s32[]{:S(2)}) async-start(), calls=%async_computation.25 | async-start | bytes 9437184 | tf_op jit(solution)/shard_map/reduce_scatter | solution.py:298
  780.6 514.4 %reduce-scatter.22.cloned.1.call-start = ((), (), s32[]{:S(2)}) async-start(), calls=%async_computation.21 | async-start | bytes 7077888 | tf_op jit(solution)/shard_map/reduce_scatter | solution.py:286
  935.3 411.0 %reduce-scatter.38.cloned.1.call-start = ((), (), s32[]{:S(2)}) async-start(), calls=%async_computation.29 | async-start | bytes 294912
  950.9 418.6 %reduce-scatter.36.cloned.1.call-start = ((), (), s32[]{:S(2)}) async-start(), calls=%async_computation.28 | async-start | bytes 294912
  950.9 8.6 copy-start.59
  956.9 338.1 %copy-start.69 = (u32[32]{0:T(128)S(1)}, u32[32]{0:T(128)}, u32[]{:S(2)}) copy-start(u32[32]{0:T(128)} %constant.48) | copy-start | bytes 388
  959.4 339.3 %copy-start.66 = (bf16[128]{0:T(256)(128)(2,1)S(1)}, bf16[128]{0:T(256)(128)(2,1)}, u32[]{:S(2)}) copy-start(bf16[128]{0:T(256)(128)(2,1)} %param.27) | copy-start | bytes 772
  959.4 347.9 %copy-start.54 = (bf16[4096]{0:T(1024)(128)(2,1)S(1)}, bf16[4096]{0:T(1024)(128)(2,1)}, u32[]{:S(2)}) copy-start(bf16[4096]{0:T(1024)(128)(2,1)} %get-tuple-element.38) | copy-start | bytes 24580
  959.4 371.8 %copy-start.17 = (f32[832,1024]{1,0:T(8,128)S(1)}, f32[832,1024]{1,0:T(8,128)}, u32[]{:S(2)}) copy-start(f32[832,1024]{1,0:T(8,128)} %copy-done.15) | copy-start | bytes 10223620
  959.5 447.3 %reduce-scatter.34.cloned.1.call-start = ((), (), s32[]{:S(2)}) async-start(), calls=%async_computation.27 | async-start | bytes 294912
  960.7 605.8 %all-reduce.7.cloned.1.call-start = ((), (), s32[]{:S(2)}) async-start(), calls=%async_computation.30 | async-start | bytes 8388608 | tf_op jit(solution)/shard_map/psum | solution.py:319
  1566.4 6.2 copy-start.31
  1566.4 7.5 copy-start.30
  1568.4 7.1 copy-start.29
  (26 other events, 63.6 us)
Sparse Core Ops, SparseCore 0:
  9.9 48.2 all-gather.10
  68.9 123.9 all-gather.14
  195.0 122.0 all-gather.12
  318.9 26.0 all-gather.16
  346.7 45.5 all-gather.18
  394.0 27.8 all-gather.20
  423.8 54.3 all-gather.22
  480.2 54.3 all-gather.24
  682.7 119.2 reduce-scatter.19
  804.1 119.7 reduce-scatter.17
  927.7 41.6 reduce-scatter.27
  973.6 41.2 reduce-scatter.23
  1018.2 61.7 reduce-scatter.25
  1083.7 71.2 reduce-scatter.31
  1158.3 71.2 reduce-scatter.29
  1233.2 61.7 reduce-scatter.21
  1298.4 33.6 reduce-scatter.37
  1335.8 33.5 reduce-scatter.35
  1373.1 33.6 reduce-scatter.33
  1409.6 156.7 all-reduce.6
where the time goes:
time: 1590 us; the launch traced here: 1580 us
  waiting for transfers between devices  996 us (63%)
  matrix products  276 us (17%)
  local copies, waits for them, and re-layouts  149 us (9%)
  blocking collectives  80.9 us (5%)
  other arithmetic  64.6 us (4%)
  between operations  16.9 us (1%)
    psum x1, waiting for transfers between devices, body(): lax.psum(shards[1].astype(jnp.bfloat16), 'tile').astype(jnp.float32)  144 us
    reduce_scatter x1, waiting for transfers between devices, body(): lax.psum_scatter(grad_frame_keys.astype(jnp.bfloat16), 'tile', scatter_di...  122 us
    all_gather x1, waiting for transfers between devices, body(): lax.all_gather(own_values, 'tile', axis=2, tiled=True)  114 us
    all_gather x1, waiting for transfers between devices, body(): lax.all_gather(own_keys, 'tile', axis=2, tiled=True)  101 us
    reduce_scatter x1, waiting for transfers between devices, body(): lax.psum_scatter(local_grads[6].astype(jnp.bfloat16), 'seq', scatter_dime...  75 us
    reduce_scatter x1, waiting for transfers between devices, body(): lax.psum_scatter(local_grads[5].astype(jnp.bfloat16), 'seq', scatter_dime...  74.6 us
    reduce_scatter x1, waiting for transfers between devices, body(): lax.psum_scatter(local_grads[1].astype(jnp.bfloat16), 'seq', scatter_dime...  65.4 us
    reduce_scatter x1, waiting for transfers between devices, body(): lax.psum_scatter(local_grads[3].astype(jnp.bfloat16), 'seq', scatter_dime...  65.2 us
  transfers between devices with their start and end apart: 20, of which 17 were waited for; matrix products, arithmetic and copies ran while one was open for 20% of the time, Pallas kernels for 0%

commit v1 on v0

v1 whole, which is shorter than its diff:
```python
import functools
import math

import jax
import jax.numpy as jnp
from jax import lax
from jax.experimental import pallas as pl
from jax.experimental.pallas import tpu as pltpu
from jax.sharding import PartitionSpec as P

HEAD = 64
PAIR = 2 * HEAD
BLOCKS = 8
GROUP = 16
CHUNK = 1024
SET = 4
WIDE = 512
VMEM = 64000 * 1024

epsilon = 1e-05
masked_score = -1e30
score_scale = HEAD ** (-0.5)
f32 = jnp.float32
bf16 = jnp.bfloat16
ANY = pl.BlockSpec(memory_space=pl.ANY)


def dot_nn(left, right):
    return lax.dot_general(left, right, (((1,), (0,)), ((), ())), preferred_element_type=f32)


def dot_nt(left, right):
    return lax.dot_general(left, right, (((1,), (1,)), ((), ())), preferred_element_type=f32)


def dot_tn(left, right):
    return lax.dot_general(left, right, (((0,), (0,)), ((), ())), preferred_element_type=f32)


def flipped(block):
    return block.astype(f32).T.astype(block.dtype)


def norm_unit(hidden):
    centred = hidden - jnp.mean(hidden, axis=-1, keepdims=True)
    inverse = lax.rsqrt(jnp.mean(centred * centred, axis=-1, keepdims=True) + epsilon)
    return centred * inverse, inverse


def norm_back(upstream, unit, inverse, gain_row):
    scaled = upstream * gain_row
    mean_first = jnp.mean(scaled, axis=-1, keepdims=True)
    mean_second = jnp.mean(scaled * unit, axis=-1, keepdims=True)
    return inverse * (scaled - mean_first - unit * mean_second)


def column_sum(block):
    return jnp.sum(block, axis=0, keepdims=True)


def half_lanes(block, half):
    lanes = lax.broadcasted_iota(jnp.int32, block.shape, 1)
    return jnp.where((lanes < HEAD) == (half == 0), block, jnp.zeros_like(block))


def pair_rows(block):
    return jnp.concatenate([half_lanes(block, 0), half_lanes(block, 1)], axis=0)


def pick_lanes(stacked):
    size = stacked.shape[0] // 2
    lanes = lax.broadcasted_iota(jnp.int32, (size, stacked.shape[1]), 1)
    return jnp.where(lanes < HEAD, stacked[:size], stacked[size:])


def attend(query, key, value, mask):
    scores = dot_nt(pair_rows(query * jnp.asarray(score_scale, bf16)), key)
    if mask is not None:
        scores = jnp.where(mask, scores, masked_score)
    top = jnp.max(scores, axis=1, keepdims=True)
    powered = jnp.exp(scores - top)
    total = jnp.sum(powered, axis=1, keepdims=True)
    mixed = dot_nn(powered.astype(bf16), value) / total
    return pick_lanes(mixed).astype(bf16), top + jnp.log(total)


def attend_back(query, key, value, upstream, sums, mask):
    query = pair_rows(query * jnp.asarray(score_scale, bf16))
    upstream = pair_rows(upstream)
    scores = dot_nt(key, query)
    if mask is not None:
        scores = jnp.where(mask, scores, masked_score)
    soft = jnp.exp(scores - sums)
    grad_soft = dot_nt(value, upstream)
    inner = jnp.sum(soft * grad_soft, axis=0, keepdims=True)
    grad_scores = (soft * (grad_soft - inner)).astype(bf16)
    grad_value = dot_nn(soft.astype(bf16), upstream)
    grad_key = dot_nn(grad_scores, query)
    grad_query = pick_lanes(dot_tn(grad_scores, key)) * score_scale
    return grad_query.astype(bf16), grad_key.astype(bf16), grad_value.astype(bf16)


def lane_slices(index, width):
    base = pl.multiple_of(index * SET * PAIR, SET * PAIR)
    return [
        [pl.ds(base + (pair * PAIR + part * width), PAIR) for part in range(3)]
        for pair in range(SET)
    ]


def attend_set(index, width, load, store, mask, sums_store):
    columns = None
    for pair, lanes in enumerate(lane_slices(index, width)):
        out, sums = attend(*(load(lane) for lane in lanes), mask)
        store(lanes[0], out)
        size = out.shape[0]
        if columns is None:
            columns = jnp.zeros((size, PAIR), f32)
            spots = lax.broadcasted_iota(jnp.int32, columns.shape, 1)
        for half in (0, 1):
            part = sums[half * size : (half + 1) * size]
            columns = jnp.where(spots == 2 * pair + half, part, columns)
    sums_store(columns.T[: 2 * SET])


def attend_back_set(index, width, load, load_up, store, mask, sums):
    for pair, lanes in enumerate(lane_slices(index, width)):
        row = jnp.concatenate([sums[2 * pair : 2 * pair + 1], sums[2 * pair + 1 : 2 * pair + 2]], axis=1)
        grads = attend_back(*(load(lane) for lane in lanes), load_up(lanes[0]), row, mask)
        for lane, grad in zip(lanes, grads):
            store(lane, grad)


def piece_copies(scalars, places, refs, whole, sems, rows):
    copies = []
    for index, ((owner, offset), ref) in enumerate(zip(places, refs)):
        start = pl.multiple_of((owner ^ scalars[0]) * rows + offset, 16)
        copies.append(
            pltpu.make_async_copy(ref, whole.at[pl.ds(start, ref.shape[0])], sems.at[index])
        )
    return copies


def call(kernel, grid, in_specs, out_specs, out_shape, scratch, flops, moved, name):
    return pl.pallas_call(
        kernel,
        out_shape=out_shape,
        grid_spec=pltpu.PrefetchScalarGridSpec(
            num_scalar_prefetch=1,
            grid=grid,
            in_specs=in_specs,
            out_specs=out_specs,
            scratch_shapes=scratch,
        ),
        compiler_params=pltpu.CompilerParams(vmem_limit_bytes=VMEM),
        cost_estimate=pl.CostEstimate(flops=flops, bytes_accessed=moved, transcendentals=0),
        name=name,
    )


def shape(dims, dtype=bf16):
    return jax.ShapeDtypeStruct(tuple(dims), dtype)


def full(dims):
    return pl.BlockSpec(tuple(dims), lambda i, s: (0,) * len(dims))


def spatial_forward(scalars, tokens, embed, gain, shift, weight):
    arrays, places, rows = weight
    tiles, (frames, cells, width) = len(tokens), tokens[0].shape
    length, count = tiles * cells, len(arrays)
    heads, sets = width // HEAD, width // (PAIR * SET)

    def kernel(scalars_ref, *refs):
        token_refs, refs = refs[:tiles], refs[tiles:]
        embed_ref, gain_ref, shift_ref, *refs = refs
        pieces, refs = refs[:count], refs[count:]
        normed_ref, proj_ref, refs = refs[0], refs[1], refs[2:]
        mixed_refs, (sums_ref, whole, sems, mixed) = refs[:tiles], refs[tiles:]
        copies = piece_copies(scalars_ref, places, pieces, whole, sems, rows)
        for copy in copies:
            copy.start()
        for frame in range(frames):
            hidden = jnp.concatenate([ref[frame] for ref in token_refs], axis=0).astype(f32)
            unit, _ = norm_unit(hidden + embed_ref[frame])
            normed_ref[frame] = (unit * gain_ref[...] + shift_ref[...]).astype(bf16)
        for copy in copies:
            copy.wait()
        for start in range(0, 3 * width, CHUNK):
            part = dot_nn(rows_of(normed_ref[...]), whole[:, start : start + CHUNK])
            proj_ref[:, :, start : start + CHUNK] = part.astype(bf16).reshape(frames, length, CHUNK)

        def run(index, carry):
            frame, part = index // sets, index % sets

            def store(lane, value):
                mixed[:, lane] = value
                for tile, ref in enumerate(mixed_refs):
                    ref[frame, :, lane] = value[tile * cells : (tile + 1) * cells]

            def sums_store(value):
                spot = pl.multiple_of(part * 2 * SET, 2 * SET)
                sums_ref[frame, pl.ds(spot, 2 * SET)] = value

            attend_set(part, width, lambda lane: proj_ref[frame, :, lane], store, None, sums_store)
            return carry

        lax.fori_loop(0, frames * sets, run, 0)

    outs = call(
        kernel,
        (1,),
        [full((frames, cells, width))] * tiles
        + [full((frames, 1, width)), full((1, width)), full((1, width))]
        + [ANY] * count,
        [full((frames, length, width)), full((frames, length, 3 * width))]
        + [full((frames, cells, width))] * tiles
        + [full((frames, heads, length))],
        [shape((frames, length, width)), shape((frames, length, 3 * width))]
        + [shape((frames, cells, width))] * tiles
        + [shape((frames, heads, length), f32)],
        [
            pltpu.VMEM((width, 3 * width), bf16),
            pltpu.SemaphoreType.DMA((count,)),
            pltpu.VMEM((length, width), bf16),
        ],
        2 * frames * length * width * (3 * width + 2 * length) * 2,
        20 << 20,
        "spatial_forward",
    )(scalars, *tokens, embed, gain, shift, *arrays)
    return outs[0], outs[1], outs[2 : 2 + tiles], outs[2 + tiles]


def spatial_backward(scalars, upstreams, tokens, embed, gain, proj, sums, weight):
    arrays, places, rows = weight
    tiles, (frames, cells, width) = len(tokens), tokens[0].shape
    length, count = tiles * cells, len(arrays)
    heads, sets = width // HEAD, width // (PAIR * SET)

    def kernel(scalars_ref, *refs):
        up_refs, refs = refs[:tiles], refs[tiles:]
        token_refs, refs = refs[:tiles], refs[tiles:]
        embed_ref, gain_ref, proj_ref, sums_ref, *refs = refs
        pieces, refs = refs[:count], refs[count:]
        grad_ref, refs = refs[0], refs[1:]
        back_refs, refs = refs[:tiles], refs[tiles:]
        gain_grad, shift_grad, frame_sum, whole, sems, upstream = refs
        copies = piece_copies(scalars_ref, places, pieces, whole, sems, rows)
        for copy in copies:
            copy.start()
        for tile, ref in enumerate(up_refs):
            upstream[:, tile * cells : (tile + 1) * cells] = ref[...]

        def run(index, carry):
            frame, part = index // sets, index % sets

            def store(lane, value):
                grad_ref[frame, :, lane] = value

            spot = pl.multiple_of(part * 2 * SET, 2 * SET)
            attend_back_set(
                part,
                width,
                lambda lane: proj_ref[frame, :, lane],
                lambda lane: upstream[frame, :, lane],
                store,
                None,
                sums_ref[frame, pl.ds(spot, 2 * SET)],
            )
            return carry

        lax.fori_loop(0, frames * sets, run, 0)
        for copy in copies:
            copy.wait()
        grad_normed = dot_nt(rows_of(grad_ref[...]), whole[...])
        gains, shifts = 0, 0
        for frame in range(frames):
            hidden = jnp.concatenate([ref[frame] for ref in token_refs], axis=0).astype(f32)
            unit, inverse = norm_unit(hidden + embed_ref[frame])
            grad = grad_normed[frame * length : (frame + 1) * length]
            back = norm_back(grad, unit, inverse, gain_ref[...])
            gains, shifts = gains + column_sum(grad * unit), shifts + column_sum(grad)
            frame_sum[frame] = column_sum(back)
            for tile, ref in enumerate(back_refs):
                ref[frame] = back[tile * cells : (tile + 1) * cells].astype(bf16)
        gain_grad[...], shift_grad[...] = gains, shifts

    tile_spec = full((frames, cells, width))
    outs = call(
        kernel,
        (1,),
        [tile_spec] * (2 * tiles)
        + [full((frames, 1, width)), full((1, width)), full((frames, length, 3 * width))]
        + [full((frames, heads, length))]
        + [ANY] * count,
        [full((frames, length, 3 * width))]
        + [tile_spec] * tiles
        + [full((1, width)), full((1, width)), full((frames, 1, width))],
        [shape((frames, length, 3 * width))]
        + [shape((frames, cells, width))] * tiles
        + [shape((1, width), f32)] * 2
        + [shape((frames, 1, width), f32)],
        [
            pltpu.VMEM((width, 3 * width), bf16),
            pltpu.SemaphoreType.DMA((count,)),
            pltpu.VMEM((frames, length, width), bf16),
        ],
        2 * frames * length * width * (3 * width + 5 * length) * 2,
        24 << 20,
        "spatial_backward",
    )(scalars, *upstreams, *tokens, embed, gain, proj, sums, *arrays)
    return outs[0], outs[1 : 1 + tiles], outs[1 + tiles], outs[2 + tiles], outs[3 + tiles]


def rows_of(block):
    return block.reshape(block.shape[0] * block.shape[1], block.shape[2])


def temporal_forward(scalars, tokens, embed, mixed_parts, share, gains, shifts, mask, weight):
    arrays, places, rows = weight
    frames, cells, width = tokens.shape
    tiles, count = len(mixed_parts[0][0]), len(arrays)
    parts = [(array, tile, first) for part, first in mixed_parts for tile, array in enumerate(part)]
    heads, sets, size = width // HEAD, width // (PAIR * SET), frames * GROUP
    groups = cells // GROUP

    def kernel(scalars_ref, *refs):
        token_ref, embed_ref, *refs = refs
        part_refs, refs = refs[: len(parts)], refs[len(parts) :]
        gain_ref, shift_ref, mask_ref, *refs = refs
        pieces, refs = refs[:count], refs[count:]
        outs, kept, (sums_ref,), refs = refs[:7], refs[8:15], refs[7:8], refs[15:]
        whole, sems, gathered, out_sems = refs
        space, first, normed, proj, mixed, second, last = kept
        copies = piece_copies(scalars_ref, places, pieces, whole, sems, rows)
        flushes = [
            pltpu.make_async_copy(ref, out, out_sems.at[index])
            for index, (ref, out) in enumerate(zip(kept, outs))
        ]
        for copy in copies:
            copy.start()
        for ref, (_, tile, start) in zip(part_refs, parts):
            spot = (tile ^ scalars_ref[1]) * share + start
            gathered[pl.ds(spot, ref.shape[0])] = ref[...]
        space[...] = gathered[:frames]
        flushes[0].start()
        for copy in copies:
            copy.wait()
        hidden = rows_of(token_ref[...].astype(f32) + embed_ref[...])
        hidden = hidden + dot_nn(rows_of(space[...]), whole[:, :width])
        first[...] = hidden.reshape(first.shape)
        flushes[1].start()
        unit, _ = norm_unit(hidden)
        normed[...] = (unit * gain_ref[1:2] + shift_ref[1:2]).astype(bf16).reshape(normed.shape)
        flushes[2].start()
        for start in range(0, 3 * width, CHUNK):
            part = dot_nn(rows_of(normed[...]), whole[:, width + start : width + start + CHUNK])
            proj[:, :, start : start + CHUNK] = part.astype(bf16).reshape(frames, cells, CHUNK)
        flushes[3].start()
        allowed = mask_ref[...] > 0

        def run(index, carry):
            group, part = index // sets, index % sets
            places_here = pl.ds(pl.multiple_of(group * GROUP, GROUP), GROUP)

            def store(lane, value):
                mixed[:, places_here, lane] = value.reshape(frames, GROUP, PAIR)

            def sums_store(value):
                spot = pl.multiple_of(part * 2 * SET, 2 * SET)
                sums_ref[group, pl.ds(spot, 2 * SET)] = value

            attend_set(
                part,
                width,
                lambda lane: rows_of(proj[:, places_here, lane]),
                store,
                allowed,
                sums_store,
            )
            return carry

        lax.fori_loop(0, groups * sets, run, 0)
        flushes[4].start()
        hidden = rows_of(first[...]) + dot_nn(rows_of(mixed[...]), whole[:, 4 * width :])
        second[...] = hidden.reshape(second.shape)
        flushes[5].start()
        unit, _ = norm_unit(hidden)
        last[...] = (unit * gain_ref[2:3] + shift_ref[2:3]).astype(bf16).reshape(last.shape)
        flushes[6].start()
        for flush in flushes:
            flush.wait()

    wide = (frames, cells, width)
    kept = [
        (wide, bf16),
        (wide, f32),
        (wide, bf16),
        ((frames, cells, 3 * width), bf16),
        (wide, bf16),
        (wide, f32),
        (wide, bf16),
    ]
    return call(
        kernel,
        (1,),
        [full(wide), full((frames, 1, width))]
        + [full(array.shape) for array, _, _ in parts]
        + [full((3, width)), full((3, width)), full((2 * size, size))]
        + [ANY] * count,
        [ANY] * 7 + [full((groups, heads, size))],
        [shape(*k) for k in kept] + [shape((groups, heads, size), f32)],
        [pltpu.VMEM(*k) for k in kept]
        + [
            pltpu.VMEM((width, 5 * width), bf16),
            pltpu.SemaphoreType.DMA((count,)),
            pltpu.VMEM((share * tiles, cells, width), bf16),
            pltpu.SemaphoreType.DMA((7,)),
        ],
        2 * frames * cells * width * (5 * width + 2 * size) * 2,
        40 << 20,
        "temporal_forward",
    )(scalars, tokens, embed, *[p[0] for p in parts], gains, shifts, mask, *arrays)


def temporal_backward(
    scalars, upstream, upstream_low, hidden, proj, sums, gains, mask, weight, tiles, share, splits
):
    arrays, places, rows = weight
    frames, cells, width = upstream.shape
    count = len(arrays)
    heads, sets, size = width // HEAD, width // (PAIR * SET), frames * GROUP
    groups = cells // GROUP
    parts = [(tile, start, many) for start, many in splits for tile in range(tiles)]

    def kernel(scalars_ref, *refs):
        up_ref, low_ref, hidden_ref, proj_ref, sums_ref, gain_ref, mask_ref, *refs = refs
        pieces, refs = refs[:count], refs[count:]
        grad_out, first_out, low_out, *refs = refs
        space_refs, refs = refs[: len(parts)], refs[len(parts) :]
        gain_grad, shift_grad, frame_sum, grads, first, first_low, *refs = refs
        whole, sems, mixed, spread, out_sems = refs
        copies = piece_copies(scalars_ref, places, pieces, whole, sems, rows)
        flushes = [
            pltpu.make_async_copy(ref, out, out_sems.at[index])
            for index, (ref, out) in enumerate(
                ((grads, grad_out), (first, first_out), (first_low, low_out))
            )
        ]
        for copy in copies:
            copy.start()
        spread[frames:] = jnp.zeros((spread.shape[0] - frames, cells, width), bf16)
        for copy in copies:
            copy.wait()
        part = dot_nt(rows_of(low_ref[...]), whole[:, 4 * width :])
        mixed[...] = part.astype(bf16).reshape(mixed.shape)
        allowed = mask_ref[...] > 0

        def run(index, carry):
            group, part = index // sets, index % sets
            places_here = pl.ds(pl.multiple_of(group * GROUP, GROUP), GROUP)

            def store(lane, value):
                grads[:, places_here, lane] = value.reshape(frames, GROUP, PAIR)

            spot = pl.multiple_of(part * 2 * SET, 2 * SET)
            attend_back_set(
                part,
                width,
                lambda lane: rows_of(proj_ref[:, places_here, lane]),
                lambda lane: rows_of(mixed[:, places_here, lane]),
                store,
                allowed,
                sums_ref[group, pl.ds(spot, 2 * SET)],
            )
            return carry

        lax.fori_loop(0, groups * sets, run, 0)
        flushes[0].start()
        grad_normed = dot_nt(rows_of(grads[...]), whole[:, width : 4 * width])
        unit, inverse = norm_unit(rows_of(hidden_ref[...]))
        gain_grad[...] = column_sum(grad_normed * unit)
        shift_grad[...] = column_sum(grad_normed)
        out = rows_of(up_ref[...]) + norm_back(grad_normed, unit, inverse, gain_ref[1:2])
        out = out.reshape(first.shape)
        first[...] = out
        first_low[...] = out.astype(bf16)
        flushes[1].start()
        flushes[2].start()
        frame_sum[...] = jnp.sum(out, axis=1, keepdims=True)
        space = dot_nt(rows_of(first_low[...]), whole[:, :width]).astype(bf16)
        spread[:frames] = space.reshape(frames, cells, width)
        for ref, (tile, start, many) in zip(space_refs, parts):
            spot = (tile ^ scalars_ref[1]) * share + start
            ref[...] = spread[pl.ds(spot, many)]
        for flush in flushes:
            flush.wait()

    wide = (frames, cells, width)
    kept = [((frames, cells, 3 * width), bf16), (wide, f32), (wide, bf16)]
    outs = call(
        kernel,
        (1,),
        [full(wide)] * 3
        + [full((frames, cells, 3 * width)), full((groups, heads, size))]
        + [full((3, width)), full((size, 2 * size))]
        + [ANY] * count,
        [ANY] * 3
        + [full((many, cells, width)) for _, _, many in parts]
        + [full((1, width)), full((1, width)), full((frames, 1, width))],
        [shape(*k) for k in kept]
        + [shape((many, cells, width)) for _, _, many in parts]
        + [shape((1, width), f32)] * 2
        + [shape((frames, 1, width), f32)],
        [pltpu.VMEM(*k) for k in kept]
        + [
            pltpu.VMEM((width, 5 * width), bf16),
            pltpu.SemaphoreType.DMA((count,)),
            pltpu.VMEM(wide, bf16),
            pltpu.VMEM((max(share * tiles, frames + 1), cells, width), bf16),
            pltpu.SemaphoreType.DMA((3,)),
        ],
        2 * frames * cells * width * (5 * width + 5 * size) * 2,
        40 << 20,
        "temporal_backward",
    )(scalars, upstream, upstream_low, hidden, proj, sums, gains, mask, *arrays)
    ups = outs[3 : 3 + len(parts)]
    ups = [ups[i : i + tiles] for i in range(0, len(parts), tiles)]
    return outs[0], outs[1], outs[2], ups, *outs[3 + len(parts) :]


def expand_forward(scalars, normed, bias, weight):
    arrays, places, rows = weight
    size, width = normed.shape
    hidden, count = arrays[0].shape[1], len(arrays)
    root = math.sqrt(2 / math.pi)

    def kernel(scalars_ref, normed_ref, bias_ref, *refs):
        pieces, (act_ref, slope_ref, whole) = refs[:count], refs[count:]
        for (owner, offset), ref in zip(places, pieces):
            start = pl.multiple_of((owner ^ scalars_ref[0]) * rows + offset, 16)
            whole[pl.ds(start, ref.shape[0])] = ref[...]
        value = dot_nn(normed_ref[...], whole[...]) + bias_ref[...]
        square = value * value
        gate = 0.5 + 0.5 * jnp.tanh(value * (root + (root * 0.044715) * square))
        act = value * gate
        act_ref[...] = act.astype(bf16)
        slope = gate + act * (1.0 - gate) * (2 * root + (6 * root * 0.044715) * square)
        slope_ref[...] = slope.astype(bf16)

    out_spec = pl.BlockSpec((size, WIDE), lambda n, s: (0, n))
    return call(
        kernel,
        (hidden // WIDE,),
        [
            pl.BlockSpec((size, width), lambda n, s: (0, 0)),
            pl.BlockSpec((1, WIDE), lambda n, s: (0, n)),
        ]
        + [pl.BlockSpec((array.shape[0], WIDE), lambda n, s: (0, n)) for array in arrays],
        [out_spec, out_spec],
        [shape((size, hidden)), shape((size, hidden))],
        [pltpu.VMEM((width, WIDE), bf16)],
        2 * size * width * hidden,
        25 << 20,
        "expand_forward",
    )(scalars, normed, bias, *arrays)


def half_pieces(places, step, count):
    if count == 1:
        return [0] if step == 0 else []
    return [i for i, (owner, _) in enumerate(places) if owner // 2 == step]


def expand_backward(scalars, upstream, slope, hidden, gain, expand, contract):
    arrays, places, rows = expand
    arrays_c, places_c, rows_c = contract
    size, width = upstream.shape
    inner, count, count_c = slope.shape[1], len(arrays), len(arrays_c)
    steps = BLOCKS // 2
    chunk = inner // steps

    def kernel(scalars_ref, up_ref, slope_ref, hidden_ref, gain_ref, *refs):
        pieces, refs = refs[:count], refs[count:]
        pieces_c, refs = refs[:count_c], refs[count_c:]
        grad_ref, out_ref, low_ref, gain_grad, shift_grad, bias_grad, out_bias, *refs = refs
        whole, sems, whole_c, sems_c, total = refs
        step = pl.program_id(0)

        def columns(spot):
            start = pl.multiple_of((spot ^ (scalars_ref[0] // 2)) * chunk, chunk)
            return pl.ds(start, chunk)

        copies_c = piece_copies(scalars_ref, places_c, pieces_c, whole_c, sems_c, rows_c)
        copies = []
        for spot in range(steps):
            lanes = columns(spot)
            copies.append(
                piece_copies(
                    scalars_ref,
                    places,
                    [ref.at[:, lanes] for ref in pieces],
                    whole.at[:, lanes],
                    sems.at[spot],
                    rows,
                )
            )

        @pl.when(step == 0)
        def _():
            for spot in range(steps):
                for index in half_pieces(places_c, spot, count_c):
                    copies_c[index].start()
                for copy in copies[spot]:
                    copy.start()
            total[...] = jnp.zeros_like(total)

        for spot in range(steps):

            @pl.when(step == spot)
            def _(spot=spot):
                for index in half_pieces(places_c, spot, count_c):
                    copies_c[index].wait()
                for copy in copies[spot]:
                    copy.wait()

        lanes = columns(step)
        grad = dot_nt(up_ref[...], whole_c[lanes]) * slope_ref[...].astype(f32)
        grad_ref[...] = grad.astype(bf16)
        bias_grad[...] = column_sum(grad)
        total[...] += dot_nt(grad_ref[...], whole[:, lanes])

        @pl.when(step == steps - 1)
        def _():
            unit, inverse = norm_unit(hidden_ref[...])
            gain_grad[...] = column_sum(total[...] * unit)
            shift_grad[...] = column_sum(total[...])
            up = up_ref[...].astype(f32)
            out_bias[...] = column_sum(up)
            out = up + norm_back(total[...], unit, inverse, gain_ref[2:3])
            out_ref[...] = out
            low_ref[...] = out.astype(bf16)

    def part_spec(lines):
        return pl.BlockSpec((lines, chunk), lambda n, s: (0, n ^ (s[0] // 2)))

    once = pl.Buffered(1)
    return call(
        kernel,
        (steps,),
        [
            pl.BlockSpec((size, width), lambda n, s: (0, 0), pipeline_mode=once),
            part_spec(size),
            pl.BlockSpec((size, width), lambda n, s: (0, 0), pipeline_mode=once),
            full((3, width)),
        ]
        + [ANY] * (count + count_c),
        [part_spec(size), full((size, width)), full((size, width))]
        + [full((1, width)), full((1, width)), part_spec(1), full((1, width))],
        [
            shape((size, inner)),
            shape((size, width), f32),
            shape((size, width)),
            shape((1, width), f32),
            shape((1, width), f32),
            shape((1, inner), f32),
            shape((1, width), f32),
        ],
        [
            pltpu.VMEM((width, inner), bf16),
            pltpu.SemaphoreType.DMA((steps, count)),
            pltpu.VMEM((inner, width), bf16),
            pltpu.SemaphoreType.DMA((count_c,)),
            pltpu.VMEM((size, width), f32),
        ],
        4 * size * width * inner,
        40 << 20,
        "expand_backward",
    )(scalars, upstream, slope, hidden, gain, *arrays, *arrays_c)


def contract_forward(scalars, act, hidden, bias, contract):
    arrays, places, rows = contract
    size, inner = act.shape
    width, count = hidden.shape[1], len(arrays)
    steps = BLOCKS // 2
    chunk = inner // steps

    def kernel(scalars_ref, act_ref, hidden_ref, bias_ref, *refs):
        pieces, (out_ref, whole, sems, total) = refs[:count], refs[count:]
        step = pl.program_id(0)
        copies = piece_copies(scalars_ref, places, pieces, whole, sems, rows)

        @pl.when(step == 0)
        def _():
            for spot in range(steps):
                for index in half_pieces(places, spot, count):
                    copies[index].start()
            total[...] = hidden_ref[...] + bias_ref[...]

        for spot in range(steps):

            @pl.when(step == spot)
            def _(spot=spot):
                for index in half_pieces(places, spot, count):
                    copies[index].wait()

        lines = pl.ds(pl.multiple_of((step ^ (scalars_ref[0] // 2)) * chunk, chunk), chunk)
        total[...] += dot_nn(act_ref[...], whole[lines])

        @pl.when(step == steps - 1)
        def _():
            out_ref[...] = total[...].astype(bf16)

    return call(
        kernel,
        (steps,),
        [
            pl.BlockSpec((size, chunk), lambda n, s: (0, n ^ (s[0] // 2))),
            full((size, width)),
            full((1, width)),
        ]
        + [ANY] * count,
        [full((size, width))],
        [shape((size, width))],
        [
            pltpu.VMEM((inner, width), bf16),
            pltpu.SemaphoreType.DMA((count,)),
            pltpu.VMEM((size, width), f32),
        ],
        2 * size * width * inner,
        20 << 20,
        "contract_forward",
    )(scalars, act, hidden, bias, *arrays)[0]


def weight_grad(scalars, left, right, name):
    size, height = left.shape
    width = right.shape[1]
    rows, half = height // BLOCKS, BLOCKS // 2
    outs = [shape((half * rows, width))] * 2
    cost = (2 * size * height * width, (size * (height + width) + height * width) * 2, name)
    if rows >= 512:

        def kernel(scalars_ref, keep_left, send_left, right_ref, keep_ref, send_ref):
            keep_ref[...] = dot_tn(keep_left[...], right_ref[...]).astype(bf16)
            send_ref[...] = dot_tn(send_left[...], right_ref[...]).astype(bf16)

        def left_spec(flip):
            return pl.BlockSpec((size, rows), lambda j, s: (0, (2 * j + flip) ^ s[0]))

        out_spec = pl.BlockSpec((rows, width), lambda j, s: (j, 0))
        right_spec = pl.BlockSpec((size, width), lambda j, s: (0, 0))
        specs = [left_spec(0), left_spec(1), right_spec]
        return call(kernel, (half,), specs, [out_spec] * 2, outs, [], *cost)(
            scalars, left, left, right
        )

    chunk = min(CHUNK, width)

    def kernel(scalars_ref, left_ref, right_ref, keep_ref, send_ref, turned):
        @pl.when(pl.program_id(0) == 0)
        def _():
            for spot in range(BLOCKS):
                owner = 2 * (spot % half) + spot // half
                lanes = pl.ds(pl.multiple_of((owner ^ scalars_ref[0]) * rows, rows), rows)
                turned[spot * rows : (spot + 1) * rows] = flipped(left_ref[:, lanes])

        out = dot_nn(turned[...], right_ref[...]).astype(bf16)
        keep_ref[...] = out[: half * rows]
        send_ref[...] = out[half * rows :]

    out_spec = pl.BlockSpec((half * rows, chunk), lambda n, s: (0, n))
    return call(
        kernel,
        (width // chunk,),
        [
            pl.BlockSpec((size, height), lambda n, s: (0, 0)),
            pl.BlockSpec((size, chunk), lambda n, s: (0, n)),
        ],
        [out_spec, out_spec],
        outs,
        [pltpu.VMEM((height, size), bf16)],
        *cost,
    )(scalars, left, right)


def input_back(scalars, upstream, back_parts, share):
    frames, cells, width = upstream.shape
    tiles = len(back_parts[0][0])
    parts = [(array, tile, first) for part, first in back_parts for tile, array in enumerate(part)]

    def kernel(scalars_ref, up_ref, *refs):
        part_refs, (out_ref, gathered) = refs[: len(parts)], refs[len(parts) :]
        for ref, (_, tile, start) in zip(part_refs, parts):
            spot = (tile ^ scalars_ref[1]) * share + start
            gathered[pl.ds(spot, ref.shape[0])] = ref[...]
        out_ref[...] = (up_ref[...] + gathered[:frames].astype(f32)).astype(bf16)

    def spec(lines):
        return pl.BlockSpec((lines, GROUP, width), lambda g, s: (0, g, 0))

    return call(
        kernel,
        (cells // GROUP,),
        [spec(frames)] + [spec(array.shape[0]) for array, _, _ in parts],
        [spec(frames)],
        [shape(upstream.shape)],
        [pltpu.VMEM((share * tiles, GROUP, width), bf16)],
        0,
        8 * frames * cells * width,
        "input_back",
    )(scalars, upstream, *[p[0] for p in parts])[0]


CORE, XCHIP, YCHIP = 1, 2, 4


def gate(value, *after):
    return lax.optimization_barrier((value, after))[0]


def across(array, flip):
    return lax.ppermute(array, "seq", [(i, i ^ flip) for i in range(BLOCKS)])


def gather_pieces(shard, after=()):
    half = shard.shape[0] // 2
    shard = gate(shard, *after)
    from_x, from_y = across(shard, XCHIP), across(shard, YCHIP)
    far_low = across(from_y[:half], XCHIP)
    far_high = across(from_x[half:], YCHIP)
    mine = [
        (shard, 0, 0),
        (from_x, XCHIP, 0),
        (from_y, YCHIP, 0),
        (far_low, XCHIP | YCHIP, 0),
        (far_high, XCHIP | YCHIP, half),
    ]
    theirs = [(across(array, CORE), owner | CORE, offset) for array, owner, offset in mine]
    pieces = mine + theirs
    weight = ([p[0] for p in pieces], [p[1:] for p in pieces], shard.shape[0])
    return weight, (from_x, from_y), (far_low, far_high)


class SeqSum:
    def __init__(self, keep, send):
        self.cut = (2, 2, 2, keep.shape[0] // 8, keep.shape[1])
        self.keep, self.received = keep.reshape(self.cut), across(send, CORE).reshape(self.cut)

    def both(self, index):
        return self.keep[index].astype(f32) + self.received[index].astype(f32)

    def first(self):
        send_x = self.both((slice(None), 1, 0)).astype(bf16)
        send_y = self.both((1, slice(None), 1)).astype(bf16)
        self.from_x, self.from_y = across(send_x, XCHIP), across(send_y, YCHIP)
        return send_x, send_y

    def second(self):
        send_y = (self.both((1, 0, 0)) + self.from_x[1].astype(f32)).astype(bf16)
        send_x = (self.both((0, 1, 1)) + self.from_y[1].astype(f32)).astype(bf16)
        self.low, self.high = across(send_y, YCHIP), across(send_x, XCHIP)
        return send_x, send_y

    def total(self):
        low = self.both((0, 0, 0)) + self.from_x[0].astype(f32) + self.low.astype(f32)
        high = self.both((0, 0, 1)) + self.from_y[0].astype(f32) + self.high.astype(f32)
        return jnp.concatenate([low, high], axis=0).astype(bf16)


class LineSum:
    def __init__(self, block):
        self.block, self.sum, self.hop = block, block.astype(f32), 0
        self.up = self.down = block

    def step(self):
        last = lax.axis_size("tile") - 1
        up = lax.ppermute(self.up, "tile", [(self.hop, self.hop + 1)])
        down = lax.ppermute(self.down, "tile", [(last - self.hop, last - self.hop - 1)])
        self.hop += 1
        self.sum = self.sum + up.astype(f32) + down.astype(f32)
        self.up = (self.block.astype(f32) + up.astype(f32)).astype(bf16)
        self.down = (self.block.astype(f32) + down.astype(f32)).astype(bf16)
        return up, down


def plain_total(keep, send):
    width, rows = keep.shape[1], keep.shape[0] // (BLOCKS // 2)
    cut = (BLOCKS // 2, rows, width)
    whole = jnp.stack([keep.reshape(cut), send.reshape(cut)], axis=1).reshape(-1, width)
    shard = lax.psum_scatter(whole, "seq", scatter_dimension=0, tiled=True)
    return lax.psum(shard, "tile").astype(f32)


def exchange(chunks, direct):
    if direct:
        count = len(chunks)
        return [chunks[0]] + [
            lax.ppermute(chunks[k], "tile", [(i, i ^ k) for i in range(count)])
            for k in range(1, count)
        ]
    mixed = lax.all_to_all(jnp.stack(chunks), "tile", 0, 0)
    return [mixed[k] for k in range(len(chunks))]


def sum_everywhere(array):
    for flip in (CORE, XCHIP, YCHIP):
        array = array + across(array, flip)
    for flip in (1, 2):
        array = array + lax.ppermute(array, "tile", [(i, i ^ flip) for i in range(4)])
    return array


def body(
    inputs,
    actions,
    segments,
    cotangent,
    action_table,
    spatial_inward,
    spatial_outward,
    temporal_inward,
    temporal_outward,
    expand_weight,
    contract_weight,
    expand_bias,
    contract_bias,
    norm_gain,
    norm_shift,
):
    seqs, tiles = lax.axis_size("seq"), lax.axis_size("tile")
    direct = seqs == BLOCKS and tiles == 4
    _, frames, cells, width = inputs.shape
    share = -(-frames // tiles)
    splits = [(0, share // 2), (share // 2, share // 2)] if share % 2 == 0 else [(0, share)]
    kinds = action_table.shape[0]
    lanes = action_table.shape[1]
    me = lax.axis_index("seq").astype(jnp.int32) if direct else jnp.int32(0)
    spot = lax.axis_index("tile").astype(jnp.int32)
    scalars = jnp.stack([me, spot if direct else jnp.int32(0)])

    tokens = inputs[0]
    padded = jnp.pad(tokens, ((0, share * tiles - frames), (0, 0), (0, 0)))
    frame_tokens = []
    for first, many in splits:
        chunks = [
            lax.dynamic_slice_in_dim(padded, (spot ^ k if direct else k) * share + first, many, 0)
            for k in range(tiles)
        ]
        frame_tokens.append(exchange(chunks, direct))

    small = jnp.concatenate(
        [
            action_table,
            norm_gain,
            norm_shift,
            expand_bias.reshape(-1, lanes),
            contract_bias.reshape(1, lanes),
        ],
        axis=0,
    )
    small = lax.all_gather(small, "seq", axis=0)
    small = small.astype(f32)

    def joined(start, stop):
        return small[:, start:stop].transpose(1, 0, 2).reshape(stop - start, -1)

    table = joined(0, kinds)
    gains = joined(kinds, kinds + 3)
    shifts = joined(kinds + 3, kinds + 6)
    wide_bias = small[:, kinds + 6 : -1].reshape(1, -1)
    out_bias = small[:, -1].reshape(1, -1)

    middle = jnp.concatenate([spatial_outward, temporal_inward, temporal_outward], axis=1)
    if direct:
        space_in, near_one, far_one = gather_pieces(spatial_inward)
        middle, near_two, far_two = gather_pieces(middle, near_one)
        expand, near_three, far_three = gather_pieces(expand_weight, near_two)
        contract, near_four, far_four = gather_pieces(contract_weight, near_three)
    else:
        near_one = near_two = near_three = near_four = ()
        far_one = far_two = far_three = far_four = ()
        space_in, middle, expand, contract = (
            ([whole], [(0, 0)], whole.shape[0] // BLOCKS)
            for whole in (
                lax.all_gather(shard, "seq", axis=0, tiled=True)
                for shard in (spatial_inward, middle, expand_weight, contract_weight)
            )
        )

    onehot = (actions[0][:, None] == jnp.arange(kinds, dtype=jnp.int32)[None, :]).astype(f32)
    embed = jnp.dot(onehot, table, precision=lax.Precision.HIGHEST)
    onehot_own = lax.dynamic_slice_in_dim(
        jnp.pad(onehot, ((0, share * tiles - frames), (0, 0))), spot * share, share, 0
    )
    embed_own = jnp.dot(onehot_own, table, precision=lax.Precision.HIGHEST)
    embed, embed_own = embed[:, None, :], embed_own[:, None, :]

    index = jnp.arange(frames * GROUP, dtype=jnp.int32)
    frame_of, place_of = index // GROUP, index % GROUP
    ids = jnp.repeat(segments[0], GROUP)
    mask = (
        (place_of[:, None] == place_of[None, :])
        & (frame_of[:, None] >= frame_of[None, :])
        & (ids[:, None] == ids[None, :])
    ).astype(f32)
    mask_rows = jnp.concatenate([mask, mask], axis=0)
    mask_lanes = jnp.concatenate([mask.T, mask.T], axis=1)

    saved, mixed_parts = [], []
    waits = [near_one, near_two]
    for part, (first, many) in enumerate(splits):
        normed, proj, mixed, sums = spatial_forward(
            gate(scalars, *waits[part]),
            frame_tokens[part],
            embed_own[first : first + many],
            gains[0:1],
            shifts[0:1],
            space_in,
        )
        saved.append((normed, proj, sums))
        mixed_parts.append((exchange(list(mixed), direct), first))
    (
        space_rows,
        space_sum,
        normed_two,
        time_proj,
        time_mixed,
        time_sum,
        normed_three,
        time_sums,
    ) = temporal_forward(
        gate(scalars, *near_three),
        tokens,
        embed,
        mixed_parts,
        share,
        gains,
        shifts,
        mask_rows,
        middle,
    )

    def flat(array):
        return array.reshape(-1, array.shape[-1])

    upstream = flat(cotangent[0])
    act, slope = expand_forward(
        gate(scalars, *near_four), flat(normed_three), wide_bias, expand
    )
    contract_parts = weight_grad(gate(scalars, *far_four), act, upstream, "contract_grad")
    if direct:
        contract_sum = SeqSum(*contract_parts)
    (
        grad_hidden,
        grad_time_sum,
        time_low,
        gain_three,
        shift_three,
        grad_wide_bias,
        grad_out_bias,
    ) = expand_backward(scalars, upstream, slope, flat(time_sum), gains, expand, contract)

    after = contract_sum.first() if direct else ()
    expand_parts = weight_grad(
        gate(scalars, *after), flat(normed_three), grad_hidden, "expand_grad"
    )
    if direct:
        expand_sum = SeqSum(*expand_parts)
    outputs = contract_forward(
        gate(scalars, *expand_parts), act, flat(time_sum), out_bias, contract
    )

    after = (outputs,)
    if direct:
        after = (outputs, *contract_sum.second(), *expand_sum.first())
    (
        grad_time_proj,
        grad_space_sum,
        space_low,
        space_ups,
        gain_two,
        shift_two,
        frame_sum,
    ) = temporal_backward(
        gate(scalars, *after),
        grad_time_sum.reshape(frames, cells, width),
        time_low.reshape(frames, cells, width),
        space_sum,
        time_proj,
        time_sums,
        gains,
        mask_lanes,
        middle,
        tiles,
        share,
        splits,
    )
    frame_ups = [exchange(list(ups), direct) for ups in space_ups]
    after = (grad_time_proj,)
    if direct:
        contract_line = LineSum(contract_sum.total())
        after = (grad_time_proj, *expand_sum.second(), contract_line.block)
    time_in_parts = weight_grad(
        gate(scalars, *after), flat(normed_two), flat(grad_time_proj), "time_in_grad"
    )
    after = time_in_parts
    if direct:
        time_in_sum = SeqSum(*time_in_parts)
        expand_line = LineSum(expand_sum.total())
        after = (*time_in_parts, *contract_line.step(), expand_line.block)
    time_out_parts = weight_grad(gate(scalars, *after), flat(time_mixed), time_low, "time_out_grad")
    space_out_parts = weight_grad(
        gate(scalars, *time_out_parts), flat(space_rows), flat(space_low), "space_out_grad"
    )
    out_parts = [
        jnp.concatenate(pair, axis=1) for pair in zip(time_out_parts, space_out_parts)
    ]
    after = (*space_out_parts,)
    if direct:
        out_sum = SeqSum(*out_parts)
        after = (*space_out_parts, *time_in_sum.first())

    back_parts, grad_space_parts = [], []
    gain_one = shift_one = 0
    own_sums = []
    for part, (first, many) in enumerate(splits):
        if direct and part == 1:
            after = (
                *grad_space_parts,
                *time_in_sum.second(),
                *out_sum.first(),
                *contract_line.step(),
                *expand_line.step(),
            )
        grads, backs, gain_part, shift_part, own_sum = spatial_backward(
            gate(scalars, *after),
            frame_ups[part],
            frame_tokens[part],
            embed_own[first : first + many],
            gains[0:1],
            saved[part][1],
            saved[part][2],
            space_in,
        )
        gain_one, shift_one = gain_one + gain_part, shift_one + shift_part
        own_sums.append(own_sum)
        grad_space_parts.append(grads)
        back_parts.append((exchange(list(backs), direct), first))
    after = (*grad_space_parts,)
    if direct:
        time_in_line = LineSum(time_in_sum.total())
        after = (*grad_space_parts, *out_sum.second(), *contract_line.step(), *expand_line.step())
    space_in_parts = weight_grad(
        gate(scalars, *after),
        flat(jnp.concatenate([s[0] for s in saved], axis=0)),
        flat(jnp.concatenate(grad_space_parts, axis=0)),
        "space_in_grad",
    )

    own_sum = jnp.concatenate(own_sums, axis=0)
    grad_table = jnp.einsum(
        "fa,fd->ad", onehot, frame_sum[:, 0], precision=lax.Precision.HIGHEST
    ) + jnp.einsum("fa,fd->ad", onehot_own, own_sum[:, 0], precision=lax.Precision.HIGHEST)
    small_grads = jnp.concatenate(
        [
            grad_table,
            gain_one,
            gain_two,
            gain_three,
            shift_one,
            shift_two,
            shift_three,
            grad_wide_bias.reshape(-1, width),
            grad_out_bias,
        ],
        axis=0,
    )
    small_grads = sum_everywhere(small_grads) if direct else lax.psum(small_grads, ("seq", "tile"))
    input_grad = input_back(scalars, grad_space_sum, back_parts, share)

    if direct:
        space_in_sum = SeqSum(*space_in_parts)
        space_in_sum.first()
        out_line = LineSum(out_sum.total())
        time_in_line.step()
        expand_line.step()
        space_in_sum.second()
        out_line.step()
        time_in_line.step()
        space_in_line = LineSum(space_in_sum.total())
        out_line.step()
        time_in_line.step()
        out_line.step()
        for _ in range(tiles - 1):
            space_in_line.step()
        total_space_in, total_time_in, total_expand, total_contract = (
            line.sum for line in (space_in_line, time_in_line, expand_line, contract_line)
        )
        total_time_out, total_space_out = out_line.sum[:, :width], out_line.sum[:, width:]
    else:
        total_space_in, total_time_in, total_expand, total_contract = (
            plain_total(*parts)
            for parts in (space_in_parts, time_in_parts, expand_parts, contract_parts)
        )
        total_out = plain_total(*out_parts)
        total_time_out, total_space_out = total_out[:, :width], total_out[:, width:]

    here = lax.axis_index("seq")

    def own_lanes(array):
        return lax.dynamic_slice_in_dim(array, here * lanes, lanes, 1)

    wide_total = small_grads[kinds + 6 : -1].reshape(-1)
    wide_share = expand_bias.shape[0]
    return (
        outputs.reshape(inputs.shape),
        input_grad.reshape(inputs.shape),
        own_lanes(small_grads[:kinds]),
        total_space_in,
        total_space_out,
        total_time_in,
        total_time_out,
        total_expand,
        total_contract,
        lax.dynamic_slice_in_dim(wide_total, here * wide_share, wide_share, 0),
        own_lanes(small_grads[-1:]).reshape(-1),
        own_lanes(small_grads[kinds : kinds + 3]),
        own_lanes(small_grads[kinds + 3 : kinds + 6]),
    )


def solution(mesh):
    seq_first, seq_last = P("seq", None), P(None, "seq")
    stream = P("seq", None, "tile", None)
    return jax.shard_map(
        body,
        mesh=mesh,
        in_specs=(stream, seq_first, seq_first, stream, seq_last)
        + (seq_first,) * 6
        + (P("seq"), P("seq"), seq_last, seq_last),
        out_specs=(stream, stream, seq_last)
        + (seq_first,) * 6
        + (P("seq"), P("seq"), seq_last, seq_last),
        check_vma=False,
    )
```

time: 1590 us -> 855 us (0.54)
  waiting for transfers between devices: 996 us -> 236 us
  matrix products: 276 us -> 1.46 us
  Pallas kernels: 0 us -> 261 us
  starting transfers between devices: 1.44 us -> 204 us
  local copies, waits for them, and re-layouts: 149 us -> 30.9 us
  blocking collectives: 80.9 us -> 15.5 us
  other arithmetic: 64.6 us -> 94.3 us
    reduce_scatter x8 -> x0, waiting for transfers between devices: 460 us -> none  [the longest x1 122 us: body(): lax.psum_scatter(grad_frame_keys.astype(jnp.bfloat16), 'tile', scatter_di...]
    all_gather x8 -> x0, waiting for transfers between devices: 328 us -> none  [the longest x1 114 us: body(): lax.all_gather(own_values, 'tile', axis=2, tiled=True)]
    dot_general x32 -> x4, matrix products: 276 us -> 1.46 us  [the longest x1 0.93 us: body(): jnp.einsum('fa,fd->ad', onehot, frame_sum[:, 0], precision=lax.Precision....]
    pallas_call x0 -> x16, Pallas kernels: none -> 261 us  [the longest x5 49.9 us: weight_grad(): call(kernel, (width // chunk,), [pl.BlockSpec((size, height), lambda n, s...]
    ppermute x0 -> x120, waiting for transfers between devices: none -> 236 us  [the longest x64 136 us: across(): return lax.ppermute(array, 'seq', [(i, i ^ flip) for i in range(BLOCKS)])]
    ppermute x0 -> x120, starting transfers between devices: none -> 204 us  [the longest x24 76.1 us: exchange(): lax.ppermute(chunks[k], 'tile', [(i, i ^ k) for i in range(count)])]
    psum x1 -> x0, waiting for transfers between devices: 144 us -> none  [body(): lax.psum(shards[1].astype(jnp.bfloat16), 'tile').astype(jnp.float32)]
    unnamed x23 -> x0, waiting for transfers between devices: 63.3 us -> none
  transfers between devices with their start and end apart: 20 -> 120, of which waited for: 17 -> 34; matrix products, arithmetic and copies ran while one was open for 20% -> 13% of each run, Pallas kernels for 0% -> 28%
where the time goes in v1:
time: 855 us; the launch traced here: 845 us
  Pallas kernels  261 us (31%)
  waiting for transfers between devices  236 us (28%)
  starting transfers between devices  204 us (24%)
  other arithmetic  94.3 us (11%)
  local copies, waits for them, and re-layouts  30.9 us (4%)
  blocking collectives  15.5 us (2%)
    ppermute x64, waiting for transfers between devices, across(): return lax.ppermute(array, 'seq', [(i, i ^ flip) for i in range(BLOCKS)])  136 us
    ppermute x24, starting transfers between devices, exchange(): lax.ppermute(chunks[k], 'tile', [(i, i ^ k) for i in range(count)])  76.1 us
    ppermute x15, starting transfers between devices, step(): up = lax.ppermute(self.up, 'tile', [(self.hop, self.hop + 1)])  63.9 us
    ppermute x24, waiting for transfers between devices, exchange(): lax.ppermute(chunks[k], 'tile', [(i, i ^ k) for i in range(count)])  60.8 us
    pallas_call x5, Pallas kernels, weight_grad(): call(kernel, (width // chunk,), [pl.BlockSpec((size, height), lambda n, s...  49.9 us
    ppermute x64, starting transfers between devices, across(): return lax.ppermute(array, 'seq', [(i, i ^ flip) for i in range(BLOCKS)])  45.6 us
    pallas_call x1, Pallas kernels, temporal_backward(): call(kernel, (1,), [full(wide)] * 3 + [full((frames, cells, 3 * width)),...  37.3 us
    pallas_call x2, Pallas kernels, spatial_backward(): call(kernel, (1,), [tile_spec] * (2 * tiles) + [full((frames, 1, width)),...  34.4 us
  transfers between devices with their start and end apart: 120, of which 34 were waited for; matrix products, arithmetic and copies ran while one was open for 13% of the time, Pallas kernels for 28%

profile of v1, /device:TPU:0, one launch (start us, length us, event | category | flops | bytes accessed | tf_op | source)
XLA Modules:
  0.0 844.6 jit_solution(6082610707669004648)
XLA Ops:
  0.7 3.0 collective-permute-start.1
  5.2 2.9 pad_dynamic-slice_fusion
  12.7 15.5 %all-gather.1 = bf16[8,19,128]{2,1,0:T(8,128)(2,1)S(1)} all-gather(bf16[1,19,128]{2,1,0:T(8,128)(2,1)S(1)} %bitcast.302), channel_id=2, replica_groups=mesh['seq'=8,'tile'=4] {'seq'}, dimensions={0}, use_global_device_ids=true | all-gather | bytes 43776 | tf_op jit(solution)/shard_map/all_gather | solution.py:964
  30.4 3.6 collective-permute-start.12
  36.7 4.1 collective-permute-done.13.refs_10_.refs_15_
  42.9 4.4 collective-permute-done.14.refs_11_.refs_16_
  52.9 14.3 %spatial_forward.2 = (bf16[2,256,1024]{2,1,0:T(8,128)(2,1)}, bf16[2,256,3072]{2,1,0:T(8,128)(2,1)}, bf16[2,64,1024]{2,1,0:T(8,128)(2,1)}, bf16[2,64,1024]{2,1,0:...) custom-call(s32[2]{0:T(128)} %pad_add_fusion.scalars_ref, ...), custom_call_target="tpu_custom_call" | custom-call | flops 7516192768 | bytes 20971520 | tf_op jit(solution)/shard_map/spatial_forward/pallas_call | solution.py:211
  69.9 4.2 collective-permute-done.3.refs_15_.refs_9_
  74.1 2.8 collective-permute-start.21
  81.1 2.8 collective-permute-done.24.refs_2_.refs_6_
  88.6 11.3 %collective-permute-done.21.refs_4_ = bf16[2,64,1024]{2,1,0:T(8,128)(2,1)} collective-permute-done((bf16[2,64,1024]{2,1,0:T(8,128)(2,1)}, bf16[2,64,1024]{2,1,0:T(8,128)(2,1)}, u32[]{:S(2)}, u32[]{:S(2)}) %collective-permute-start.21) | collective-permute-done | bytes 262176 | tf_op jit(solution)/shard_map/ppermute | solution.py:901
  101.4 14.3 %spatial_forward.3 = (bf16[2,256,1024]{2,1,0:T(8,128)(2,1)}, bf16[2,256,3072]{2,1,0:T(8,128)(2,1)}, bf16[2,64,1024]{2,1,0:T(8,128)(2,1)}, bf16[2,64,1024]{2,1,0:...) custom-call(s32[2]{0:T(128)} %pad_add_fusion.scalars_ref, ...), custom_call_target="tpu_custom_call" | custom-call | flops 7516192768 | bytes 20971520 | tf_op jit(solution)/shard_map/spatial_forward/pallas_call | solution.py:211
  115.8 3.0 collective-permute-start.27
  119.9 8.6 %collective-permute-done.26.refs_7_ = bf16[2,64,1024]{2,1,0:T(8,128)(2,1)S(1)} collective-permute-done((bf16[2,64,1024]{2,1,0:T(8,128)(2,1)}, bf16[2,64,1024]{2,1,0:T(8,128)(2,1)S(1)}, u32[]{:S(2)}, u32[]{:S(2)}) %collective-permute-start.26) | collective-permute-done | bytes 262176 | tf_op jit(solution)/shard_map/ppermute | solution.py:901
  130.8 14.8 %collective-permute-done.30.refs_17_.refs_11_ = bf16[64,5120]{1,0:T(8,128)(2,1)S(1)} collective-permute-done((bf16[64,5120]{1,0:T(8,128)(2,1)S(1)}, bf16[64,5120]{1,0:T(8,128)(2,1)S(1)}, u32[]{:S(2)}, u32[]{:S(2)}) %collective-permute-start.30) | collective-permute-done | bytes 655392 | tf_op jit(solution)/shard_map/ppermute | solution.py:825
  148.1 8.4 collective-permute-done.28.refs_9_
  166.3 26.0 %collective-permute-done.36.refs_3_ = bf16[64,4096]{1,0:T(8,128)(2,1)} collective-permute-done((bf16[64,4096]{1,0:T(8,128)(2,1)S(1)}, bf16[64,4096]{1,0:T(8,128)(2,1)}, u32[]{:S(2)}, u32[]{:S(2)}) %collective-permute-start.36) | collective-permute-done | bytes 524320 | tf_op jit(solution)/shard_map/ppermute | solution.py:825
  194.1 30.2 %temporal_forward.1 = (bf16[13,64,1024]{2,1,0:T(8,128)(2,1)}, f32[13,64,1024]{2,1,0:T(8,128)}, bf16[13,64,1024]{2,1,0:T(8,128)(2,1)}, bf16[13,64,3072]{2,1,0:T(8...) custom-call(s32[2]{0:T(128)} %pad_add_fusion.scalars_ref, ...), custom_call_target="tpu_custom_call" | custom-call | flops 18865979392 | bytes 41943040 | tf_op jit(solution)/shard_map/temporal_forward/pallas_call | solution.py:405
  228.5 18.9 %expand_forward.1 = (bf16[832,4096]{1,0:T(8,128)(2,1)}, bf16[832,4096]{1,0:T(8,128)(2,1)}) custom-call(s32[2]{0:T(128)} %pad_add_fusion.scalars_ref, bf16[832,1024]{1,0:T(8,128)(2,1)} %bitcast.322, f32[1,4096]{1,0:T(1,128)} %bitcast.304, bf16[128,4096]{1,0:T(8,128)(2,1)} %refs_0_.1, bf16[128,4096]{1,0:T(8,128)(2,1)} %collective-permute-done.4.refs_1_, ...), custom_call_target="tpu_custom_call" | custom-call | flops 6979321856 | bytes 26214400 | tf_op jit(solution)/shard_map/expand_forward/pallas_call | solution.py:553
  247.5 13.4 %contract_grad.1 = (bf16[2048,1024]{1,0:T(8,128)(2,1)}, bf16[2048,1024]{1,0:T(8,128)(2,1)}) custom-call(s32[2]{0:T(128)} %pad_add_fusion.scalars_ref, bf16[832,4096]{1,0:T(8,128)(2,1)} %get-tuple-element.120.keep_left.send_left.act_ref, bf16[832,4096]{1,0:T(8,128)(2,1)} %get-tuple-element.120.keep_left.send_left.act_ref, bf16[832,1024]{1,0:T(8,128)(2,1)} %bitcast.311), custom_call_target="tpu_custom_call" | custom-call | flops 6979321856 | bytes 16908288 | tf_op jit(solution)/shard_map/contract_grad/pallas_call | solution.py:756
  261.9 7.8 collective-permute-done.44.refs_15_.refs_5_
  271.1 3.2 collective-permute-done.48.refs_19_.refs_9_
  275.1 28.7 %expand_backward.1 = (bf16[832,4096]{1,0:T(8,128)(2,1)}, f32[832,1024]{1,0:T(8,128)}, bf16[832,1024]{1,0:T(8,128)(2,1)}, f32[1,1024]{1,0:T(1,128)}, f32[1,1024]{...) custom-call(s32[2]{0:T(128)} %pad_add_fusion.scalars_ref, bf16[832,1024]{1,0:T(8,128)(2,1)} %bitcast.312, ...), custom_call_target="tpu_custom_call" | custom-call | flops 13958643712 | bytes 41943040 | tf_op jit(solution)/shard_map/expand_backward/pallas_call | solution.py:649
  305.8 2.9 fusion.29
  308.7 14.1 %expand_grad.1 = (bf16[512,4096]{1,0:T(8,128)(2,1)}, bf16[512,4096]{1,0:T(8,128)(2,1)}) custom-call(s32[2]{0:T(128)} %pad_add_fusion.scalars_ref, bf16[832,1024]{1,0:T(8,128)(2,1)} %bitcast.323, bf16[832,4096]{1,0:T(8,128)(2,1)} %get-tuple-element.126.right_ref), custom_call_target="tpu_custom_call" | custom-call | flops 6979321856 | bytes 16908288 | tf_op jit(solution)/shard_map/expand_grad/pallas_call | solution.py:775
  325.2 23.5 %collective-permute-done.50 = bf16[2,256,1024]{2,1,0:T(8,128)(2,1)S(1)} collective-permute-done((bf16[2,256,1024]{2,1,0:T(8,128)(2,1)}, bf16[2,256,1024]{2,1,0:T(8,128)(2,1)S(1)}, u32[]{:S(2)}, u32[]{:S(2)}) %collective-permute-start.50) | collective-permute-done | bytes 1048608 | tf_op jit(solution)/shard_map/ppermute | solution.py:825
  353.9 11.0 %collective-permute-done.54 = bf16[256,1024]{1,0:T(8,128)(2,1)S(1)} collective-permute-done((bf16[256,1024]{1,0:T(8,128)(2,1)S(1)}, bf16[256,1024]{1,0:T(8,128)(2,1)S(1)}, u32[]{:S(2)}, u32[]{:S(2)}) %collective-permute-start.54) | collective-permute-done | bytes 524320 | tf_op jit(solution)/shard_map/ppermute | solution.py:825
  370.4 6.3 collective-permute-start.56
  385.4 14.1 %contract_forward.1 = bf16[832,1024]{1,0:T(8,128)(2,1)} custom-call(s32[2]{0:T(128)} %pad_add_fusion.scalars_ref, bf16[832,4096]{1,0:T(8,128)(2,1)} %get-tuple-element.120.keep_left.send_left.act_ref, f32[832,1024]{1,0:T(8,128)} %bitcast.315, f32[1,1024]{1,0:T(1,128)} %slice_bitcast_fusion.38.bias_ref, bf16[512,1024]{1,0:T(8,128)(2,1)} %refs_0_.2, ...), custom_call_target="tpu_custom_call" | custom-call | flops 6979321856 | bytes 20971520 | tf_op jit(solution)/shard_map/contract_forward/pallas_call | solution.py:716
  399.5 3.7 fusion.6
  406.6 3.3 fusion.41
  411.8 37.3 %temporal_backward.1 = (bf16[13,64,3072]{2,1,0:T(8,128)(2,1)}, f32[13,64,1024]{2,1,0:T(8,128)}, bf16[13,64,1024]{2,1,0:T(8,128)(2,1)}, bf16[2,64,1024]{2,1,0:T(8...) custom-call(s32[2]{0:T(128)} %pad_add_fusion.scalars_ref, ...), custom_call_target="tpu_custom_call" | custom-call | flops 20992491520 | bytes 41943040 | tf_op jit(solution)/shard_map/temporal_backward/pallas_call | solution.py:502
  449.1 11.6 %time_in_grad.1 = (bf16[512,3072]{1,0:T(8,128)(2,1)}, bf16[512,3072]{1,0:T(8,128)(2,1)}) custom-call(s32[2]{0:T(128)} %pad_add_fusion.scalars_ref, bf16[832,1024]{1,0:T(8,128)(2,1)} %bitcast.320, bf16[832,3072]{1,0:T(8,128)(2,1)} %bitcast.313), custom_call_target="tpu_custom_call" | custom-call | flops 5234491392 | bytes 13107200 | tf_op jit(solution)/shard_map/time_in_grad/pallas_call | solution.py:775
  460.7 2.8 fusion.36
  466.9 25.9 %collective-permute-start.72 = (bf16[128,4096]{1,0:T(8,128)(2,1)}, bf16[128,4096]{1,0:T(8,128)(2,1)}, u32[]{:S(2)}, u32[]{:S(2)}) collective-permute-start(bf16[128,4096]{1,0:T(8,128)(2,1)} %pad_maximum_fusion.6), channel_id=1, source_target_pairs={{0,1},{4,5},{8,9},{12,13},{16,17},{20,21},{24,25},{28,29}} | collective-permute-start | bytes 3145736 | tf_op jit(solution)/shard_map/ppermute | solution.py:880
  492.8 6.2 time_out_grad.1
  499.1 6.2 space_out_grad.1
  505.3 3.2 pad_maximum_fusion.2
  522.2 7.9 collective-permute-start.61
  532.5 16.9 %collective-permute-start.62 = (bf16[2,64,1024]{2,1,0:T(8,128)(2,1)S(1)}, bf16[2,64,1024]{2,1,0:T(8,128)(2,1)S(1)}, u32[]{:S(2)}, u32[]{:S(2)}) collective-permute-start(bf16[2,64,1024]{2,1,0:T(8,128)(2,1)S(1)} %copy-done.66), channel_id=1, source_target_pairs={{0,2},{1,3},{2,0},{3,1},{4,6},{5,7},{6,4},{7,5},{8,10},{9,11},{10,... | collective-permute-start | bytes 786440 | tf_op jit(solution)/shard_map/ppermute | solution.py:901
  555.7 6.8 collective-permute-done.86
  562.5 3.4 collective-permute-start.63
  565.9 6.9 collective-permute-start.74
  579.4 16.9 %spatial_backward.2 = (bf16[2,256,3072]{2,1,0:T(8,128)(2,1)}, bf16[2,64,1024]{2,1,0:T(8,128)(2,1)}, bf16[2,64,1024]{2,1,0:T(8,128)(2,1)}, bf16[2,64,1024]{2,1,0:...) custom-call(s32[2]{0:T(128)} %pad_add_fusion.scalars_ref, ...), custom_call_target="tpu_custom_call" | custom-call | flops 9126805504 | bytes 25165824 | tf_op jit(solution)/shard_map/spatial_backward/pallas_call | solution.py:290
  605.8 17.5 %spatial_backward.3 = (bf16[2,256,3072]{2,1,0:T(8,128)(2,1)}, bf16[2,64,1024]{2,1,0:T(8,128)(2,1)}, bf16[2,64,1024]{2,1,0:T(8,128)(2,1)}, bf16[2,64,1024]{2,1,0:...) custom-call(s32[2]{0:T(128)} %pad_add_fusion.scalars_ref, ...), custom_call_target="tpu_custom_call" | custom-call | flops 9126805504 | bytes 25165824 | tf_op jit(solution)/shard_map/spatial_backward/pallas_call | solution.py:290
  628.9 6.0 pad_maximum_fusion
  638.7 11.8 %space_in_grad.1 = (bf16[512,3072]{1,0:T(8,128)(2,1)}, bf16[512,3072]{1,0:T(8,128)(2,1)}) custom-call(s32[2]{0:T(128)} %pad_add_fusion.scalars_ref, bf16[1024,1024]{1,0:T(8,128)(2,1)} %bitcast.298, bf16[1024,3072]{1,0:T(8,128)(2,1)} %bitcast.272), custom_call_target="tpu_custom_call" | custom-call | flops 6442450944 | bytes 14680064 | tf_op jit(solution)/shard_map/space_in_grad/pallas_call | solution.py:775
  650.6 5.9 fusion.1
  657.6 3.7 collective-permute-start.64
  668.2 3.9 collective-permute-start.65
  675.6 4.6 fusion.3
  680.9 9.2 %collective-permute-done.65.refs_2_ = bf16[2,64,1024]{2,1,0:T(8,128)(2,1)S(1)} collective-permute-done((bf16[2,64,1024]{2,1,0:T(8,128)(2,1)S(1)}, bf16[2,64,1024]{2,1,0:T(8,128)(2,1)S(1)}, u32[]{:S(2)}, u32[]{:S(2)}) %collective-permute-start.65) | collective-permute-done | bytes 262176 | tf_op jit(solution)/shard_map/ppermute | solution.py:901
  690.1 6.1 collective-permute-start.78
  702.2 14.5 %collective-permute-done.78.refs_6_ = bf16[2,64,1024]{2,1,0:T(8,128)(2,1)S(1)} collective-permute-done((bf16[2,64,1024]{2,1,0:T(8,128)(2,1)S(1)}, bf16[2,64,1024]{2,1,0:T(8,128)(2,1)S(1)}, u32[]{:S(2)}, u32[]{:S(2)}) %collective-permute-start.78) | collective-permute-done | bytes 262176 | tf_op jit(solution)/shard_map/ppermute | solution.py:901
  719.3 5.2 input_back.1
  733.5 12.2 %collective-permute-done.92 = bf16[2,64,3072]{2,1,0:T(8,128)(2,1)S(1)} collective-permute-done((bf16[2,64,3072]{2,1,0:T(8,128)(2,1)S(1)}, bf16[2,64,3072]{2,1,0:T(8,128)(2,1)S(1)}, u32[]{:S(2)}, u32[]{:S(2)}) %collective-permute-start.92) | collective-permute-done | bytes 786464 | tf_op jit(solution)/shard_map/ppermute | solution.py:825
  751.4 9.2 %collective-permute-start.112 = (bf16[128,3072]{1,0:T(8,128)(2,1)S(1)}, bf16[128,3072]{1,0:T(8,128)(2,1)S(1)}, u32[]{:S(2)}, u32[]{:S(2)}) collective-permute-start(bf16[128,3072]{1,0:T(8,128)(2,1)S(1)} %pad_maximum_fusion.8), channel_id=1, source_target_pairs={{0,1},{4,5},{8,9},{12,13},{16,17},{20,21},{24,25},{28,29}} | collective-permute-start | bytes 2359304 | tf_op jit(solution)/shard_map/ppermute | solution.py:880
  760.6 4.4 collective-permute-done.94
  765.7 3.5 collective-permute-done.93
  775.2 3.3 collective-permute-done.95
  779.8 9.9 %collective-permute-start.96 = (bf16[128,3072]{1,0:T(8,128)(2,1)S(1)}, bf16[128,3072]{1,0:T(8,128)(2,1)S(1)}, u32[]{:S(2)}, u32[]{:S(2)}) collective-permute-start(bf16[128,3072]{1,0:T(8,128)(2,1)S(1)} %pad_maximum_fusion.7), channel_id=1, source_target_pairs={{0,1},{4,5},{8,9},{12,13},{16,17},{20,21},{24,25},{28,29}} | collective-permute-start | bytes 2359304 | tf_op jit(solution)/shard_map/ppermute | solution.py:880
  794.0 6.7 collective-permute-done.96
  808.6 17.2 %collective-permute-done.117 = bf16[128,3072]{1,0:T(8,128)(2,1)S(1)} collective-permute-done((bf16[128,3072]{1,0:T(8,128)(2,1)S(1)}, bf16[128,3072]{1,0:T(8,128)(2,1)S(1)}, u32[]{:S(2)}, u32[]{:S(2)}) %collective-permute-start.117) | collective-permute-done | bytes 786464 | tf_op jit(solution)/shard_map/ppermute | solution.py:881
  827.7 14.7 %collective-permute-done.101 = bf16[128,3072]{1,0:T(8,128)(2,1)S(1)} collective-permute-done((bf16[128,3072]{1,0:T(8,128)(2,1)S(1)}, bf16[128,3072]{1,0:T(8,128)(2,1)S(1)}, u32[]{:S(2)}, u32[]{:S(2)}) %collective-permute-start.101) | collective-permute-done | bytes 786464 | tf_op jit(solution)/shard_map/ppermute | solution.py:881
  (447 shorter events, 195.9 us)
Async XLA Ops:
  0.7 27.5 %collective-permute-start.1 = (bf16[128,3072]{1,0:T(8,128)(2,1)}, bf16[128,3072]{1,0:T(8,128)(2,1)}, u32[]{:S(2)}, u32[]{:S(2)}) collective-permute-start(bf16[128,3072]{1,0:T(8,128)(2,1)} %refs_12_.1), channel_id=1, source_target_pairs={{0,16},{4,20},{8,24},{12,28},{16,0},{20,4},{24,8},{28,12},{1,17},{... | collective-permute-start | bytes 2359304 | tf_op jit(solution)/shard_map/ppermute | solution.py:825
  3.7 39.1 %collective-permute-start.15 = (bf16[128,3072]{1,0:T(8,128)(2,1)}, bf16[128,3072]{1,0:T(8,128)(2,1)}, u32[]{:S(2)}, u32[]{:S(2)}) collective-permute-start(bf16[128,3072]{1,0:T(8,128)(2,1)} %refs_12_.1), channel_id=1, source_target_pairs={{0,4},{4,0},{8,12},{12,8},{16,20},{20,16},{24,28},{28,24},{1,5},{5... | collective-permute-start | bytes 2359304 | tf_op jit(solution)/shard_map/ppermute | solution.py:825
  3.7 26.7 %collective-permute-start = (bf16[128,3072]{1,0:T(8,128)(2,1)}, bf16[128,3072]{1,0:T(8,128)(2,1)}, u32[]{:S(2)}, u32[]{:S(2)}) collective-permute-start(bf16[128,3072]{1,0:T(8,128)(2,1)} %refs_12_.1), channel_id=1, source_target_pairs={{0,8},{4,12},{8,0},{12,4},{16,24},{20,28},{24,16},{28,20},{1,9},{5... | collective-permute-start | bytes 2359304 | tf_op jit(solution)/shard_map/ppermute | solution.py:825
  8.1 27.0 %collective-permute-start.10 = (bf16[2,64,1024]{2,1,0:T(8,128)(2,1)}, bf16[2,64,1024]{2,1,0:T(8,128)(2,1)}, u32[]{:S(2)}, u32[]{:S(2)}) collective-permute-start(bf16[2,64,1024]{2,1,0:T(8,128)(2,1)} %get-tuple-element.212), channel_id=1, source_target_pairs={{0,1},{1,0},{2,3},{3,2},{4,5},{5,4},{6,7},{7,6},{8,9},{9,8},{10,11... | collective-permute-start | bytes 786440 | tf_op jit(solution)/shard_map/ppermute | solution.py:901
  9.8 31.1 %collective-permute-start.11 = (bf16[2,64,1024]{2,1,0:T(8,128)(2,1)S(1)}, bf16[2,64,1024]{2,1,0:T(8,128)(2,1)}, u32[]{:S(2)}, u32[]{:S(2)}) collective-permute-start(bf16[2,64,1024]{2,1,0:T(8,128)(2,1)S(1)} %get-tuple-element.213), channel_id=1, source_target_pairs={{0,2},{1,3},{2,0},{3,1},{4,6},{5,7},{6,4},{7,5},{8,10},{9,11},{10,... | collective-permute-start | bytes 786440 | tf_op jit(solution)/shard_map/ppermute | solution.py:901
  40.9 33.2 %collective-permute-start.3 = (bf16[128,5120]{1,0:T(8,128)(2,1)S(1)}, bf16[128,5120]{1,0:T(8,128)(2,1)}, u32[]{:S(2)}, u32[]{:S(2)}) collective-permute-start(bf16[128,5120]{1,0:T(8,128)(2,1)S(1)} %pad_maximum_fusion.4.refs_13_.refs_7_), channel_id=1, source_target_pairs={{0,16},{4,20},{8,24},{12,28},{16,0},{20,4},{24,8},{28,12},{1,17},{... | collective-permute-start | bytes 3932168 | tf_op jit(solution)/shard_map/ppermute | solution.py:825
  41.4 32.7 %collective-permute-start.2 = (bf16[128,5120]{1,0:T(8,128)(2,1)S(1)}, bf16[128,5120]{1,0:T(8,128)(2,1)}, u32[]{:S(2)}, u32[]{:S(2)}) collective-permute-start(bf16[128,5120]{1,0:T(8,128)(2,1)S(1)} %pad_maximum_fusion.4.refs_13_.refs_7_), channel_id=1, source_target_pairs={{0,8},{4,12},{8,0},{12,4},{16,24},{20,28},{24,16},{28,20},{1,9},{5... | collective-permute-start | bytes 3932168 | tf_op jit(solution)/shard_map/ppermute | solution.py:825
  50.6 28.9 %collective-permute-start.23 = (bf16[2,64,1024]{2,1,0:T(8,128)(2,1)}, bf16[2,64,1024]{2,1,0:T(8,128)(2,1)}, u32[]{:S(2)}, u32[]{:S(2)}) collective-permute-start(bf16[2,64,1024]{2,1,0:T(8,128)(2,1)} %get-tuple-element.216), channel_id=1, source_target_pairs={{0,1},{1,0},{2,3},{3,2},{4,5},{5,4},{6,7},{7,6},{8,9},{9,8},{10,11... | collective-permute-start | bytes 786440 | tf_op jit(solution)/shard_map/ppermute | solution.py:901
  52.9 62.9 %collective-permute-start.31 = (bf16[128,5120]{1,0:T(8,128)(2,1)S(1)}, bf16[128,5120]{1,0:T(8,128)(2,1)}, u32[]{:S(2)}, u32[]{:S(2)}) collective-permute-start(bf16[128,5120]{1,0:T(8,128)(2,1)S(1)} %pad_maximum_fusion.4.refs_13_.refs_7_), channel_id=1, source_target_pairs={{0,4},{4,0},{8,12},{12,8},{16,20},{20,16},{24,28},{28,24},{1,5},{5... | collective-permute-start | bytes 3932168 | tf_op jit(solution)/shard_map/ppermute | solution.py:825
  74.1 25.8 %collective-permute-start.21 = (bf16[2,64,1024]{2,1,0:T(8,128)(2,1)}, bf16[2,64,1024]{2,1,0:T(8,128)(2,1)}, u32[]{:S(2)}, u32[]{:S(2)}) collective-permute-start(bf16[2,64,1024]{2,1,0:T(8,128)(2,1)} %get-tuple-element.112), channel_id=1, source_target_pairs={{0,2},{1,3},{2,0},{3,1},{4,6},{5,7},{6,4},{7,5},{8,10},{9,11},{10,... | collective-permute-start | bytes 786440 | tf_op jit(solution)/shard_map/ppermute | solution.py:901
  79.5 36.2 %collective-permute-start.22 = (bf16[2,64,1024]{2,1,0:T(8,128)(2,1)}, bf16[2,64,1024]{2,1,0:T(8,128)(2,1)}, u32[]{:S(2)}, u32[]{:S(2)}) collective-permute-start(bf16[2,64,1024]{2,1,0:T(8,128)(2,1)} %get-tuple-element.113), channel_id=1, source_target_pairs={{0,3},{1,2},{2,1},{3,0},{4,7},{5,6},{6,5},{7,4},{8,11},{9,10},{10,... | collective-permute-start | bytes 786440 | tf_op jit(solution)/shard_map/ppermute | solution.py:901
  83.9 61.8 %collective-permute-start.5 = (bf16[128,4096]{1,0:T(8,128)(2,1)}, bf16[128,4096]{1,0:T(8,128)(2,1)}, u32[]{:S(2)}, u32[]{:S(2)}) collective-permute-start(bf16[128,4096]{1,0:T(8,128)(2,1)} %refs_0_.1), channel_id=1, source_target_pairs={{0,16},{4,20},{8,24},{12,28},{16,0},{20,4},{24,8},{28,12},{1,17},{... | collective-permute-start | bytes 3145736 | tf_op jit(solution)/shard_map/ppermute | solution.py:825
  87.2 59.0 %collective-permute-start.4 = (bf16[128,4096]{1,0:T(8,128)(2,1)}, bf16[128,4096]{1,0:T(8,128)(2,1)}, u32[]{:S(2)}, u32[]{:S(2)}) collective-permute-start(bf16[128,4096]{1,0:T(8,128)(2,1)} %refs_0_.1), channel_id=1, source_target_pairs={{0,8},{4,12},{8,0},{12,4},{16,24},{20,28},{24,16},{28,20},{1,9},{5... | collective-permute-start | bytes 3145736 | tf_op jit(solution)/shard_map/ppermute | solution.py:825
  99.9 30.9 %collective-permute-start.29 = (bf16[64,5120]{1,0:T(8,128)(2,1)}, bf16[64,5120]{1,0:T(8,128)(2,1)}, u32[]{:S(2)}, u32[]{:S(2)}) collective-permute-start(bf16[64,5120]{1,0:T(8,128)(2,1)} %slice.449), channel_id=1, source_target_pairs={{0,8},{4,12},{8,0},{12,4},{16,24},{20,28},{24,16},{28,20},{1,9},{5... | collective-permute-start | bytes 1966088 | tf_op jit(solution)/shard_map/ppermute | solution.py:825
  128.5 33.1 %collective-permute-start.33 = (bf16[128,5120]{1,0:T(8,128)(2,1)}, bf16[128,5120]{1,0:T(8,128)(2,1)S(1)}, u32[]{:S(2)}, u32[]{:S(2)}) collective-permute-start(bf16[128,5120]{1,0:T(8,128)(2,1)} %collective-permute-done.3.refs_15_.refs_9_), channel_id=1, source_target_pairs={{0,4},{4,0},{8,12},{12,8},{16,20},{20,16},{24,28},{28,24},{1,5},{5... | collective-permute-start | bytes 3932168 | tf_op jit(solution)/shard_map/ppermute | solution.py:825
  130.8 26.4 %collective-permute-start.34 = (bf16[64,5120]{1,0:T(8,128)(2,1)}, bf16[64,5120]{1,0:T(8,128)(2,1)S(1)}, u32[]{:S(2)}, u32[]{:S(2)}) collective-permute-start(bf16[64,5120]{1,0:T(8,128)(2,1)} %collective-permute-done.29.refs_16_.refs_10_), channel_id=1, source_target_pairs={{0,4},{4,0},{8,12},{12,8},{16,20},{20,16},{24,28},{28,24},{1,5},{5... | collective-permute-start | bytes 1966088 | tf_op jit(solution)/shard_map/ppermute | solution.py:825
  156.6 37.0 %collective-permute-start.8 = (bf16[512,1024]{1,0:T(8,128)(2,1)}, bf16[512,1024]{1,0:T(8,128)(2,1)}, u32[]{:S(2)}, u32[]{:S(2)}) collective-permute-start(bf16[512,1024]{1,0:T(8,128)(2,1)} %refs_0_.2), channel_id=1, source_target_pairs={{0,8},{4,12},{8,0},{12,4},{16,24},{20,28},{24,16},{28,20},{1,9},{5... | collective-permute-start | bytes 3145736 | tf_op jit(solution)/shard_map/ppermute | solution.py:825
  158.0 36.0 %collective-permute-start.6 = (bf16[512,1024]{1,0:T(8,128)(2,1)}, bf16[512,1024]{1,0:T(8,128)(2,1)}, u32[]{:S(2)}, u32[]{:S(2)}) collective-permute-start(bf16[512,1024]{1,0:T(8,128)(2,1)} %refs_0_.2), channel_id=1, source_target_pairs={{0,16},{4,20},{8,24},{12,28},{16,0},{20,4},{24,8},{28,12},{1,17},{... | collective-permute-start | bytes 3145736 | tf_op jit(solution)/shard_map/ppermute | solution.py:825
  161.5 30.8 %collective-permute-start.36 = (bf16[64,4096]{1,0:T(8,128)(2,1)S(1)}, bf16[64,4096]{1,0:T(8,128)(2,1)}, u32[]{:S(2)}, u32[]{:S(2)}) collective-permute-start(bf16[64,4096]{1,0:T(8,128)(2,1)S(1)} %slice.452), channel_id=1, source_target_pairs={{0,8},{4,12},{8,0},{12,4},{16,24},{20,28},{24,16},{28,20},{1,9},{5... | collective-permute-start | bytes 1572872 | tf_op jit(solution)/shard_map/ppermute | solution.py:825
  162.2 31.3 %collective-permute-start.37 = (bf16[64,4096]{1,0:T(8,128)(2,1)S(1)}, bf16[64,4096]{1,0:T(8,128)(2,1)}, u32[]{:S(2)}, u32[]{:S(2)}) collective-permute-start(bf16[64,4096]{1,0:T(8,128)(2,1)S(1)} %slice.453), channel_id=1, source_target_pairs={{0,16},{4,20},{8,24},{12,28},{16,0},{20,4},{24,8},{28,12},{1,17},{... | collective-permute-start | bytes 1572872 | tf_op jit(solution)/shard_map/ppermute | solution.py:825
  166.3 60.2 %collective-permute-start.38 = (bf16[128,4096]{1,0:T(8,128)(2,1)}, bf16[128,4096]{1,0:T(8,128)(2,1)}, u32[]{:S(2)}, u32[]{:S(2)}) collective-permute-start(bf16[128,4096]{1,0:T(8,128)(2,1)} %refs_0_.1), channel_id=1, source_target_pairs={{0,4},{4,0},{8,12},{12,8},{16,20},{20,16},{24,28},{28,24},{1,5},{5... | collective-permute-start | bytes 3145736 | tf_op jit(solution)/shard_map/ppermute | solution.py:825
  192.3 36.2 %collective-permute-start.40 = (bf16[128,4096]{1,0:T(8,128)(2,1)}, bf16[128,4096]{1,0:T(8,128)(2,1)}, u32[]{:S(2)}, u32[]{:S(2)}) collective-permute-start(bf16[128,4096]{1,0:T(8,128)(2,1)} %collective-permute-done.5.refs_2_), channel_id=1, source_target_pairs={{0,4},{4,0},{8,12},{12,8},{16,20},{20,16},{24,28},{28,24},{1,5},{5... | collective-permute-start | bytes 3145736 | tf_op jit(solution)/shard_map/ppermute | solution.py:825
  193.5 35.0 %collective-permute-start.39 = (bf16[128,4096]{1,0:T(8,128)(2,1)}, bf16[128,4096]{1,0:T(8,128)(2,1)}, u32[]{:S(2)}, u32[]{:S(2)}) collective-permute-start(bf16[128,4096]{1,0:T(8,128)(2,1)} %collective-permute-done.4.refs_1_), channel_id=1, source_target_pairs={{0,4},{4,0},{8,12},{12,8},{16,20},{20,16},{24,28},{28,24},{1,5},{5... | collective-permute-start | bytes 3145736 | tf_op jit(solution)/shard_map/ppermute | solution.py:825
  193.5 34.4 %collective-permute-start.41 = (bf16[64,4096]{1,0:T(8,128)(2,1)}, bf16[64,4096]{1,0:T(8,128)(2,1)}, u32[]{:S(2)}, u32[]{:S(2)}) collective-permute-start(bf16[64,4096]{1,0:T(8,128)(2,1)} %collective-permute-done.36.refs_3_), channel_id=1, source_target_pairs={{0,4},{4,0},{8,12},{12,8},{16,20},{20,16},{24,28},{28,24},{1,5},{5... | collective-permute-start | bytes 1572872 | tf_op jit(solution)/shard_map/ppermute | solution.py:825
  194.0 34.5 %collective-permute-start.42 = (bf16[64,4096]{1,0:T(8,128)(2,1)}, bf16[64,4096]{1,0:T(8,128)(2,1)}, u32[]{:S(2)}, u32[]{:S(2)}) collective-permute-start(bf16[64,4096]{1,0:T(8,128)(2,1)} %collective-permute-done.37.refs_4_), channel_id=1, source_target_pairs={{0,4},{4,0},{8,12},{12,8},{16,20},{20,16},{24,28},{28,24},{1,5},{5... | collective-permute-start | bytes 1572872 | tf_op jit(solution)/shard_map/ppermute | solution.py:825
  260.8 43.0 %collective-permute-start.43 = (bf16[2048,1024]{1,0:T(8,128)(2,1)}, bf16[2048,1024]{1,0:T(8,128)(2,1)}, u32[]{:S(2)}, u32[]{:S(2)}) collective-permute-start(bf16[2048,1024]{1,0:T(8,128)(2,1)} %get-tuple-element.122), channel_id=1, source_target_pairs={{0,4},{4,0},{8,12},{12,8},{16,20},{20,16},{24,28},{28,24},{1,5},{5... | collective-permute-start | bytes 12582920 | tf_op jit(solution)/shard_map/ppermute | solution.py:825
  322.9 56.9 %collective-permute-start.51 = (bf16[512,4096]{1,0:T(8,128)(2,1)}, bf16[512,4096]{1,0:T(8,128)(2,1)S(1)}, u32[]{:S(2)}, u32[]{:S(2)}) collective-permute-start(bf16[512,4096]{1,0:T(8,128)(2,1)} %get-tuple-element.128), channel_id=1, source_target_pairs={{0,4},{4,0},{8,12},{12,8},{16,20},{20,16},{24,28},{28,24},{1,5},{5... | collective-permute-start | bytes 12582920 | tf_op jit(solution)/shard_map/ppermute | solution.py:825
  323.0 25.6 %collective-permute-start.50 = (bf16[2,256,1024]{2,1,0:T(8,128)(2,1)}, bf16[2,256,1024]{2,1,0:T(8,128)(2,1)S(1)}, u32[]{:S(2)}, u32[]{:S(2)}) collective-permute-start(bf16[2,256,1024]{2,1,0:T(8,128)(2,1)} %fusion.29), channel_id=1, source_target_pairs={{0,8},{4,12},{8,0},{12,4},{16,24},{20,28},{24,16},{28,20},{1,9},{5... | collective-permute-start | bytes 3145736 | tf_op jit(solution)/shard_map/ppermute | solution.py:825
  324.4 25.1 %collective-permute-start.49 = (bf16[2,256,1024]{2,1,0:T(8,128)(2,1)S(1)}, bf16[2,256,1024]{2,1,0:T(8,128)(2,1)S(1)}, u32[]{:S(2)}, u32[]{:S(2)}) collective-permute-start(bf16[2,256,1024]{2,1,0:T(8,128)(2,1)S(1)} %fusion.30), channel_id=1, source_target_pairs={{0,16},{4,20},{8,24},{12,28},{16,0},{20,4},{24,8},{28,12},{1,17},{... | collective-permute-start | bytes 3145736 | tf_op jit(solution)/shard_map/ppermute | solution.py:825
  370.4 29.1 %collective-permute-start.56 = (bf16[512,1024]{1,0:T(8,128)(2,1)}, bf16[512,1024]{1,0:T(8,128)(2,1)}, u32[]{:S(2)}, u32[]{:S(2)}) collective-permute-start(bf16[512,1024]{1,0:T(8,128)(2,1)} %pad_maximum_fusion.5), channel_id=1, source_target_pairs={{0,1},{4,5},{8,9},{12,13},{16,17},{20,21},{24,25},{28,29}} | collective-permute-start | bytes 3145736 | tf_op jit(solution)/shard_map/ppermute | solution.py:880
  382.5 23.3 %collective-permute-start.53 = (bf16[2,64,4096]{2,1,0:T(8,128)(2,1)}, bf16[2,64,4096]{2,1,0:T(8,128)(2,1)}, u32[]{:S(2)}, u32[]{:S(2)}) collective-permute-start(bf16[2,64,4096]{2,1,0:T(8,128)(2,1)} %fusion.31), channel_id=1, source_target_pairs={{0,8},{4,12},{8,0},{12,4},{16,24},{20,28},{24,16},{28,20},{1,9},{5... | collective-permute-start | bytes 3145736 | tf_op jit(solution)/shard_map/ppermute | solution.py:825
  383.7 22.9 %collective-permute-start.52 = (bf16[2,64,4096]{2,1,0:T(8,128)(2,1)}, bf16[2,64,4096]{2,1,0:T(8,128)(2,1)}, u32[]{:S(2)}, u32[]{:S(2)}) collective-permute-start(bf16[2,64,4096]{2,1,0:T(8,128)(2,1)} %fusion.32), channel_id=1, source_target_pairs={{0,16},{4,20},{8,24},{12,28},{16,0},{20,4},{24,8},{28,12},{1,17},{... | collective-permute-start | bytes 3145736 | tf_op jit(solution)/shard_map/ppermute | solution.py:825
  403.2 111.1 %collective-permute-start.70 = (bf16[512,1024]{1,0:T(8,128)(2,1)}, bf16[512,1024]{1,0:T(8,128)(2,1)}, u32[]{:S(2)}, u32[]{:S(2)}) collective-permute-start(bf16[512,1024]{1,0:T(8,128)(2,1)} %get-tuple-element.226), channel_id=1, source_target_pairs={{1,2},{5,6},{9,10},{13,14},{17,18},{21,22},{25,26},{29,30}} | collective-permute-start | bytes 3145736 | tf_op jit(solution)/shard_map/ppermute | solution.py:880
  409.9 50.8 %collective-permute-start.58 = (bf16[64,4096]{1,0:T(8,128)(2,1)}, bf16[64,4096]{1,0:T(8,128)(2,1)}, u32[]{:S(2)}, u32[]{:S(2)}) collective-permute-start(bf16[64,4096]{1,0:T(8,128)(2,1)} %get-tuple-element.197), channel_id=1, source_target_pairs={{0,16},{4,20},{8,24},{12,28},{16,0},{20,4},{24,8},{28,12},{1,17},{... | collective-permute-start | bytes 1572872 | tf_op jit(solution)/shard_map/ppermute | solution.py:825
  410.8 49.9 %collective-permute-start.59 = (bf16[64,4096]{1,0:T(8,128)(2,1)}, bf16[64,4096]{1,0:T(8,128)(2,1)}, u32[]{:S(2)}, u32[]{:S(2)}) collective-permute-start(bf16[64,4096]{1,0:T(8,128)(2,1)} %get-tuple-element.198), channel_id=1, source_target_pairs={{0,8},{4,12},{8,0},{12,4},{16,24},{20,28},{24,16},{28,20},{1,9},{5... | collective-permute-start | bytes 1572872 | tf_op jit(solution)/shard_map/ppermute | solution.py:825
  465.3 52.2 %collective-permute-start.73 = (bf16[128,4096]{1,0:T(8,128)(2,1)}, bf16[128,4096]{1,0:T(8,128)(2,1)}, u32[]{:S(2)}, u32[]{:S(2)}) collective-permute-start(bf16[128,4096]{1,0:T(8,128)(2,1)} %pad_maximum_fusion.6), channel_id=1, source_target_pairs={{3,2},{7,6},{11,10},{15,14},{19,18},{23,22},{27,26},{31,30}} | collective-permute-start | bytes 3145736 | tf_op jit(solution)/shard_map/ppermute | solution.py:881
  466.9 50.5 %collective-permute-start.72 = (bf16[128,4096]{1,0:T(8,128)(2,1)}, bf16[128,4096]{1,0:T(8,128)(2,1)}, u32[]{:S(2)}, u32[]{:S(2)}) collective-permute-start(bf16[128,4096]{1,0:T(8,128)(2,1)} %pad_maximum_fusion.6), channel_id=1, source_target_pairs={{0,1},{4,5},{8,9},{12,13},{16,17},{20,21},{24,25},{28,29}} | collective-permute-start | bytes 3145736 | tf_op jit(solution)/shard_map/ppermute | solution.py:880
  513.0 121.9 %collective-permute-start.88 = (bf16[512,1024]{1,0:T(8,128)(2,1)}, bf16[512,1024]{1,0:T(8,128)(2,1)}, u32[]{:S(2)}, u32[]{:S(2)}) collective-permute-start(bf16[512,1024]{1,0:T(8,128)(2,1)} %get-tuple-element.225), channel_id=1, source_target_pairs={{1,0},{5,4},{9,8},{13,12},{17,16},{21,20},{25,24},{29,28}} | collective-permute-start | bytes 3145736 | tf_op jit(solution)/shard_map/ppermute | solution.py:881
  517.0 35.5 %collective-permute-start.60 = (bf16[512,3072]{1,0:T(8,128)(2,1)}, bf16[512,3072]{1,0:T(8,128)(2,1)S(1)}, u32[]{:S(2)}, u32[]{:S(2)}) collective-permute-start(bf16[512,3072]{1,0:T(8,128)(2,1)} %get-tuple-element.141), channel_id=1, source_target_pairs={{0,4},{4,0},{8,12},{12,8},{16,20},{20,16},{24,28},{28,24},{1,5},{5... | collective-permute-start | bytes 9437192 | tf_op jit(solution)/shard_map/ppermute | solution.py:825
  520.5 28.9 %collective-permute-start.89 = (bf16[128,4096]{1,0:T(8,128)(2,1)S(1)}, bf16[128,4096]{1,0:T(8,128)(2,1)S(1)}, u32[]{:S(2)}, u32[]{:S(2)}) collective-permute-start(bf16[128,4096]{1,0:T(8,128)(2,1)S(1)} %get-tuple-element.224), channel_id=1, source_target_pairs={{1,2},{5,6},{9,10},{13,14},{17,18},{21,22},{25,26},{29,30}} | collective-permute-start | bytes 3145736 | tf_op jit(solution)/shard_map/ppermute | solution.py:880
  522.2 52.7 %collective-permute-start.61 = (bf16[2,64,1024]{2,1,0:T(8,128)(2,1)S(1)}, bf16[2,64,1024]{2,1,0:T(8,128)(2,1)S(1)}, u32[]{:S(2)}, u32[]{:S(2)}) collective-permute-start(bf16[2,64,1024]{2,1,0:T(8,128)(2,1)S(1)} %copy-done.68), channel_id=1, source_target_pairs={{0,1},{1,0},{2,3},{3,2},{4,5},{5,4},{6,7},{7,6},{8,9},{9,8},{10,11... | collective-permute-start | bytes 786440 | tf_op jit(solution)/shard_map/ppermute | solution.py:901
  532.5 44.9 %collective-permute-start.62 = (bf16[2,64,1024]{2,1,0:T(8,128)(2,1)S(1)}, bf16[2,64,1024]{2,1,0:T(8,128)(2,1)S(1)}, u32[]{:S(2)}, u32[]{:S(2)}) collective-permute-start(bf16[2,64,1024]{2,1,0:T(8,128)(2,1)S(1)} %copy-done.66), channel_id=1, source_target_pairs={{0,2},{1,3},{2,0},{3,1},{4,6},{5,7},{6,4},{7,5},{8,10},{9,11},{10,... | collective-permute-start | bytes 786440 | tf_op jit(solution)/shard_map/ppermute | solution.py:901
  565.9 36.2 %collective-permute-start.74 = (bf16[2,64,1024]{2,1,0:T(8,128)(2,1)}, bf16[2,64,1024]{2,1,0:T(8,128)(2,1)}, u32[]{:S(2)}, u32[]{:S(2)}) collective-permute-start(bf16[2,64,1024]{2,1,0:T(8,128)(2,1)} %get-tuple-element.165), channel_id=1, source_target_pairs={{0,1},{1,0},{2,3},{3,2},{4,5},{5,4},{6,7},{7,6},{8,9},{9,8},{10,11... | collective-permute-start | bytes 786440 | tf_op jit(solution)/shard_map/ppermute | solution.py:901
  574.9 28.8 %collective-permute-start.75 = (bf16[2,64,1024]{2,1,0:T(8,128)(2,1)}, bf16[2,64,1024]{2,1,0:T(8,128)(2,1)}, u32[]{:S(2)}, u32[]{:S(2)}) collective-permute-start(bf16[2,64,1024]{2,1,0:T(8,128)(2,1)} %get-tuple-element.166), channel_id=1, source_target_pairs={{0,2},{1,3},{2,0},{3,1},{4,6},{5,7},{6,4},{7,5},{8,10},{9,11},{10,... | collective-permute-start | bytes 786440 | tf_op jit(solution)/shard_map/ppermute | solution.py:901
  597.8 38.3 %collective-permute-start.87 = (bf16[512,1024]{1,0:T(8,128)(2,1)}, bf16[512,1024]{1,0:T(8,128)(2,1)}, u32[]{:S(2)}, u32[]{:S(2)}) collective-permute-start(bf16[512,1024]{1,0:T(8,128)(2,1)} %fusion.5), channel_id=1, source_target_pairs={{2,3},{6,7},{10,11},{14,15},{18,19},{22,23},{26,27},{30,31}} | collective-permute-start | bytes 3145736 | tf_op jit(solution)/shard_map/ppermute | solution.py:880
  602.1 70.0 %collective-permute-start.118 = (bf16[128,4096]{1,0:T(8,128)(2,1)}, bf16[128,4096]{1,0:T(8,128)(2,1)}, u32[]{:S(2)}, u32[]{:S(2)}) collective-permute-start(bf16[128,4096]{1,0:T(8,128)(2,1)} %get-tuple-element.219), channel_id=1, source_target_pairs={{2,3},{6,7},{10,11},{14,15},{18,19},{22,23},{26,27},{30,31}} | collective-permute-start | bytes 3145736 | tf_op jit(solution)/shard_map/ppermute | solution.py:880
  603.7 69.2 %collective-permute-start.119 = (bf16[128,4096]{1,0:T(8,128)(2,1)}, bf16[128,4096]{1,0:T(8,128)(2,1)}, u32[]{:S(2)}, u32[]{:S(2)}) collective-permute-start(bf16[128,4096]{1,0:T(8,128)(2,1)} %get-tuple-element.220), channel_id=1, source_target_pairs={{1,0},{5,4},{9,8},{13,12},{17,16},{21,20},{25,24},{29,28}} | collective-permute-start | bytes 3145736 | tf_op jit(solution)/shard_map/ppermute | solution.py:881
  634.9 22.7 %collective-permute-start.102 = (bf16[64,2048]{1,0:T(8,128)(2,1)}, bf16[64,2048]{1,0:T(8,128)(2,1)}, u32[]{:S(2)}, u32[]{:S(2)}) collective-permute-start(bf16[64,2048]{1,0:T(8,128)(2,1)} %get-tuple-element.209), channel_id=1, source_target_pairs={{0,16},{4,20},{8,24},{12,28},{16,0},{20,4},{24,8},{28,12},{1,17},{... | collective-permute-start | bytes 786440 | tf_op jit(solution)/shard_map/ppermute | solution.py:825
  636.0 25.3 %collective-permute-start.103 = (bf16[64,2048]{1,0:T(8,128)(2,1)}, bf16[64,2048]{1,0:T(8,128)(2,1)}, u32[]{:S(2)}, u32[]{:S(2)}) collective-permute-start(bf16[64,2048]{1,0:T(8,128)(2,1)} %get-tuple-element.210), channel_id=1, source_target_pairs={{0,8},{4,12},{8,0},{12,4},{16,24},{20,28},{24,16},{28,20},{1,9},{5... | collective-permute-start | bytes 786440 | tf_op jit(solution)/shard_map/ppermute | solution.py:825
  650.5 77.5 %collective-permute-start.91 = (bf16[512,3072]{1,0:T(8,128)(2,1)}, bf16[512,3072]{1,0:T(8,128)(2,1)}, u32[]{:S(2)}, u32[]{:S(2)}) collective-permute-start(bf16[512,3072]{1,0:T(8,128)(2,1)} %get-tuple-element.192), channel_id=1, source_target_pairs={{0,4},{4,0},{8,12},{12,8},{16,20},{20,16},{24,28},{28,24},{1,5},{5... | collective-permute-start | bytes 9437192 | tf_op jit(solution)/shard_map/ppermute | solution.py:825
  668.2 21.8 %collective-permute-start.65 = (bf16[2,64,1024]{2,1,0:T(8,128)(2,1)S(1)}, bf16[2,64,1024]{2,1,0:T(8,128)(2,1)S(1)}, u32[]{:S(2)}, u32[]{:S(2)}) collective-permute-start(bf16[2,64,1024]{2,1,0:T(8,128)(2,1)S(1)} %copy-done.61), channel_id=1, source_target_pairs={{0,2},{1,3},{2,0},{3,1},{4,6},{5,7},{6,4},{7,5},{8,10},{9,11},{10,... | collective-permute-start | bytes 786440 | tf_op jit(solution)/shard_map/ppermute | solution.py:901
  672.9 23.3 %collective-permute-start.104 = (bf16[128,2048]{1,0:T(8,128)(2,1)S(1)}, bf16[128,2048]{1,0:T(8,128)(2,1)S(1)}, u32[]{:S(2)}, u32[]{:S(2)}) collective-permute-start(bf16[128,2048]{1,0:T(8,128)(2,1)S(1)} %pad_maximum_fusion.9), channel_id=1, source_target_pairs={{0,1},{4,5},{8,9},{12,13},{16,17},{20,21},{24,25},{28,29}} | collective-permute-start | bytes 1572872 | tf_op jit(solution)/shard_map/ppermute | solution.py:880
  674.9 22.6 %collective-permute-start.105 = (bf16[128,2048]{1,0:T(8,128)(2,1)S(1)}, bf16[128,2048]{1,0:T(8,128)(2,1)S(1)}, u32[]{:S(2)}, u32[]{:S(2)}) collective-permute-start(bf16[128,2048]{1,0:T(8,128)(2,1)S(1)} %pad_maximum_fusion.9), channel_id=1, source_target_pairs={{3,2},{7,6},{11,10},{15,14},{19,18},{23,22},{27,26},{31,30}} | collective-permute-start | bytes 1572872 | tf_op jit(solution)/shard_map/ppermute | solution.py:881
  690.1 26.7 %collective-permute-start.78 = (bf16[2,64,1024]{2,1,0:T(8,128)(2,1)S(1)}, bf16[2,64,1024]{2,1,0:T(8,128)(2,1)S(1)}, u32[]{:S(2)}, u32[]{:S(2)}) collective-permute-start(bf16[2,64,1024]{2,1,0:T(8,128)(2,1)S(1)} %copy-done.63), channel_id=1, source_target_pairs={{0,2},{1,3},{2,0},{3,1},{4,6},{5,7},{6,4},{7,5},{8,10},{9,11},{10,... | collective-permute-start | bytes 786440 | tf_op jit(solution)/shard_map/ppermute | solution.py:901
  696.2 21.6 %collective-permute-start.79 = (bf16[2,64,1024]{2,1,0:T(8,128)(2,1)S(1)}, bf16[2,64,1024]{2,1,0:T(8,128)(2,1)S(1)}, u32[]{:S(2)}, u32[]{:S(2)}) collective-permute-start(bf16[2,64,1024]{2,1,0:T(8,128)(2,1)S(1)} %copy-done.62), channel_id=1, source_target_pairs={{0,3},{1,2},{2,1},{3,0},{4,7},{5,6},{6,5},{7,4},{8,11},{9,10},{10,... | collective-permute-start | bytes 786440 | tf_op jit(solution)/shard_map/ppermute | solution.py:901
  697.5 27.0 %collective-permute-start.84 = (f32[19,1024]{1,0:T(8,128)}, f32[19,1024]{1,0:T(8,128)}, u32[]{:S(2)}, u32[]{:S(2)}) collective-permute-start(f32[19,1024]{1,0:T(8,128)} %add.558), channel_id=1, source_target_pairs={{0,2},{1,3},{2,0},{3,1},{4,6},{5,7},{6,4},{7,5},{8,10},{9,11},{10,... | collective-permute-start | bytes 233480 | tf_op jit(solution)/shard_map/ppermute | solution.py:912
  701.3 46.5 %collective-permute-start.110 = (bf16[64,3072]{1,0:T(8,128)(2,1)}, bf16[64,3072]{1,0:T(8,128)(2,1)}, u32[]{:S(2)}, u32[]{:S(2)}) collective-permute-start(bf16[64,3072]{1,0:T(8,128)(2,1)} %get-tuple-element.205), channel_id=1, source_target_pairs={{0,16},{4,20},{8,24},{12,28},{16,0},{20,4},{24,8},{28,12},{1,17},{... | collective-permute-start | bytes 1179656 | tf_op jit(solution)/shard_map/ppermute | solution.py:825
  716.8 32.2 %collective-permute-start.111 = (bf16[64,3072]{1,0:T(8,128)(2,1)S(1)}, bf16[64,3072]{1,0:T(8,128)(2,1)}, u32[]{:S(2)}, u32[]{:S(2)}) collective-permute-start(bf16[64,3072]{1,0:T(8,128)(2,1)S(1)} %get-tuple-element.206), channel_id=1, source_target_pairs={{0,8},{4,12},{8,0},{12,4},{16,24},{20,28},{24,16},{28,20},{1,9},{5... | collective-permute-start | bytes 1179656 | tf_op jit(solution)/shard_map/ppermute | solution.py:825
  717.8 54.0 %collective-permute-start.106 = (bf16[128,2048]{1,0:T(8,128)(2,1)}, bf16[128,2048]{1,0:T(8,128)(2,1)}, u32[]{:S(2)}, u32[]{:S(2)}) collective-permute-start(bf16[128,2048]{1,0:T(8,128)(2,1)} %get-tuple-element.237), channel_id=1, source_target_pairs={{1,2},{5,6},{9,10},{13,14},{17,18},{21,22},{25,26},{29,30}} | collective-permute-start | bytes 1572872 | tf_op jit(solution)/shard_map/ppermute | solution.py:880
  724.5 47.4 %collective-permute-start.107 = (bf16[128,2048]{1,0:T(8,128)(2,1)}, bf16[128,2048]{1,0:T(8,128)(2,1)S(1)}, u32[]{:S(2)}, u32[]{:S(2)}) collective-permute-start(bf16[128,2048]{1,0:T(8,128)(2,1)} %get-tuple-element.238), channel_id=1, source_target_pairs={{2,1},{6,5},{10,9},{14,13},{18,17},{22,21},{26,25},{30,29}} | collective-permute-start | bytes 1572872 | tf_op jit(solution)/shard_map/ppermute | solution.py:881
  751.4 38.3 %collective-permute-start.112 = (bf16[128,3072]{1,0:T(8,128)(2,1)S(1)}, bf16[128,3072]{1,0:T(8,128)(2,1)S(1)}, u32[]{:S(2)}, u32[]{:S(2)}) collective-permute-start(bf16[128,3072]{1,0:T(8,128)(2,1)S(1)} %pad_maximum_fusion.8), channel_id=1, source_target_pairs={{0,1},{4,5},{8,9},{12,13},{16,17},{20,21},{24,25},{28,29}} | collective-permute-start | bytes 2359304 | tf_op jit(solution)/shard_map/ppermute | solution.py:880
  765.0 25.5 %collective-permute-start.113 = (bf16[128,3072]{1,0:T(8,128)(2,1)S(1)}, bf16[128,3072]{1,0:T(8,128)(2,1)S(1)}, u32[]{:S(2)}, u32[]{:S(2)}) collective-permute-start(bf16[128,3072]{1,0:T(8,128)(2,1)S(1)} %pad_maximum_fusion.8), channel_id=1, source_target_pairs={{3,2},{7,6},{11,10},{15,14},{19,18},{23,22},{27,26},{31,30}} | collective-permute-start | bytes 2359304 | tf_op jit(solution)/shard_map/ppermute | solution.py:881
  803.7 22.1 %collective-permute-start.117 = (bf16[128,3072]{1,0:T(8,128)(2,1)S(1)}, bf16[128,3072]{1,0:T(8,128)(2,1)S(1)}, u32[]{:S(2)}, u32[]{:S(2)}) collective-permute-start(bf16[128,3072]{1,0:T(8,128)(2,1)S(1)} %get-tuple-element.228), channel_id=1, source_target_pairs={{1,0},{5,4},{9,8},{13,12},{17,16},{21,20},{25,24},{29,28}} | collective-permute-start | bytes 2359304 | tf_op jit(solution)/shard_map/ppermute | solution.py:881
  807.3 35.2 %collective-permute-start.101 = (bf16[128,3072]{1,0:T(8,128)(2,1)S(1)}, bf16[128,3072]{1,0:T(8,128)(2,1)S(1)}, u32[]{:S(2)}, u32[]{:S(2)}) collective-permute-start(bf16[128,3072]{1,0:T(8,128)(2,1)S(1)} %get-tuple-element.232), channel_id=1, source_target_pairs={{1,0},{5,4},{9,8},{13,12},{17,16},{21,20},{25,24},{29,28}} | collective-permute-start | bytes 2359304 | tf_op jit(solution)/shard_map/ppermute | solution.py:881
  (132 other events, 1670.2 us)

commit v2 on v1

v2 whole, which is shorter than its diff:
```python
import functools
import math

import jax
import jax.numpy as jnp
from jax import lax
from jax.experimental import pallas as pl
from jax.experimental.pallas import tpu as pltpu
from jax.sharding import PartitionSpec as P

HEAD = 64
PAIR = 2 * HEAD
BLOCKS = 8
GROUP = 16
CHUNK = 1024
SET = 4
WIDE = 512
VMEM = 64000 * 1024

epsilon = 1e-05
masked_score = -1e30
score_scale = HEAD ** (-0.5)
f32 = jnp.float32
bf16 = jnp.bfloat16
ANY = pl.BlockSpec(memory_space=pl.ANY)


def dot_nn(left, right):
    return lax.dot_general(left, right, (((1,), (0,)), ((), ())), preferred_element_type=f32)


def dot_nt(left, right):
    return lax.dot_general(left, right, (((1,), (1,)), ((), ())), preferred_element_type=f32)


def dot_tn(left, right):
    return lax.dot_general(left, right, (((0,), (0,)), ((), ())), preferred_element_type=f32)


def flipped(block):
    return block.astype(f32).T.astype(block.dtype)


def norm_unit(hidden):
    centred = hidden - jnp.mean(hidden, axis=-1, keepdims=True)
    inverse = lax.rsqrt(jnp.mean(centred * centred, axis=-1, keepdims=True) + epsilon)
    return centred * inverse, inverse


def norm_back(upstream, unit, inverse, gain_row):
    scaled = upstream * gain_row
    mean_first = jnp.mean(scaled, axis=-1, keepdims=True)
    mean_second = jnp.mean(scaled * unit, axis=-1, keepdims=True)
    return inverse * (scaled - mean_first - unit * mean_second)


def column_sum(block):
    return jnp.sum(block, axis=0, keepdims=True)


def half_lanes(block, half):
    lanes = lax.broadcasted_iota(jnp.int32, block.shape, 1)
    return jnp.where((lanes < HEAD) == (half == 0), block, jnp.zeros_like(block))


def pair_rows(block):
    return jnp.concatenate([half_lanes(block, 0), half_lanes(block, 1)], axis=0)


def pick_lanes(stacked):
    size = stacked.shape[0] // 2
    lanes = lax.broadcasted_iota(jnp.int32, (size, stacked.shape[1]), 1)
    return jnp.where(lanes < HEAD, stacked[:size], stacked[size:])


def attend(query, key, value, mask):
    scores = dot_nt(pair_rows(query * jnp.asarray(score_scale, bf16)), key)
    if mask is not None:
        scores = jnp.where(mask, scores, masked_score)
    top = jnp.max(scores, axis=1, keepdims=True)
    powered = jnp.exp(scores - top)
    total = jnp.sum(powered, axis=1, keepdims=True)
    mixed = dot_nn(powered.astype(bf16), value) / total
    return pick_lanes(mixed).astype(bf16), top + jnp.log(total)


def attend_back(query, key, value, upstream, sums, mask):
    query = pair_rows(query * jnp.asarray(score_scale, bf16))
    upstream = pair_rows(upstream)
    scores = dot_nt(key, query)
    if mask is not None:
        scores = jnp.where(mask, scores, masked_score)
    soft = jnp.exp(scores - sums)
    grad_soft = dot_nt(value, upstream)
    inner = jnp.sum(soft * grad_soft, axis=0, keepdims=True)
    grad_scores = (soft * (grad_soft - inner)).astype(bf16)
    grad_value = dot_nn(soft.astype(bf16), upstream)
    grad_key = dot_nn(grad_scores, query)
    grad_query = pick_lanes(dot_tn(grad_scores, key)) * score_scale
    return grad_query.astype(bf16), grad_key.astype(bf16), grad_value.astype(bf16)


def lane_slices(index, width):
    base = pl.multiple_of(index * SET * PAIR, SET * PAIR)
    return [
        [pl.ds(base + (pair * PAIR + part * width), PAIR) for part in range(3)]
        for pair in range(SET)
    ]


def attend_set(index, width, load, store, mask, sums_store):
    columns = None
    for pair, lanes in enumerate(lane_slices(index, width)):
        out, sums = attend(*(load(lane) for lane in lanes), mask)
        store(lanes[0], out)
        size = out.shape[0]
        if columns is None:
            columns = jnp.zeros((size, PAIR), f32)
            spots = lax.broadcasted_iota(jnp.int32, columns.shape, 1)
        for half in (0, 1):
            part = sums[half * size : (half + 1) * size]
            columns = jnp.where(spots == 2 * pair + half, part, columns)
    sums_store(columns.T[: 2 * SET])


def attend_back_set(index, width, load, load_up, store, mask, sums):
    for pair, lanes in enumerate(lane_slices(index, width)):
        row = jnp.concatenate([sums[2 * pair : 2 * pair + 1], sums[2 * pair + 1 : 2 * pair + 2]], axis=1)
        grads = attend_back(*(load(lane) for lane in lanes), load_up(lanes[0]), row, mask)
        for lane, grad in zip(lanes, grads):
            store(lane, grad)


def weight_copies(scalars, places, refs, whole, sems, rows):
    copies = []
    for index, (place, ref) in enumerate(zip(places, refs)):
        start = pl.multiple_of((place ^ scalars[0]) * rows, 16)
        copies.append(
            pltpu.make_async_copy(ref, whole.at[pl.ds(start, ref.shape[0])], sems.at[index])
        )
    return copies


def call(kernel, grid, in_specs, out_specs, out_shape, scratch, flops, moved, name):
    return pl.pallas_call(
        kernel,
        out_shape=out_shape,
        grid_spec=pltpu.PrefetchScalarGridSpec(
            num_scalar_prefetch=1,
            grid=grid,
            in_specs=in_specs,
            out_specs=out_specs,
            scratch_shapes=scratch,
        ),
        compiler_params=pltpu.CompilerParams(vmem_limit_bytes=VMEM),
        cost_estimate=pl.CostEstimate(flops=flops, bytes_accessed=moved, transcendentals=0),
        name=name,
    )


def shape(dims, dtype=bf16):
    return jax.ShapeDtypeStruct(tuple(dims), dtype)


def full(dims):
    return pl.BlockSpec(tuple(dims), lambda i, s: (0,) * len(dims))


def rows_of(block):
    return block.reshape(block.shape[0] * block.shape[1], block.shape[2])


def spatial_forward(scalars, tokens, part, many, embed, gain, shift, weight):
    arrays, places, rows = weight
    tiles, _, cells, width = tokens.shape
    length, count = tiles * cells, len(arrays)
    heads, sets = width // HEAD, width // (PAIR * SET)

    def kernel(scalars_ref, *refs):
        token_ref, embed_ref, gain_ref, shift_ref, *refs = refs
        pieces, refs = refs[:count], refs[count:]
        normed_ref, proj_ref, mixed_ref, sums_ref, whole, sems = refs
        copies = weight_copies(scalars_ref, places, pieces, whole, sems, rows)
        for copy in copies:
            copy.start()
        for frame in range(many):
            hidden = rows_of(token_ref[:, frame]).astype(f32)
            unit, _ = norm_unit(hidden + embed_ref[frame])
            normed_ref[frame] = (unit * gain_ref[...] + shift_ref[...]).astype(bf16)
        for copy in copies:
            copy.wait()
        for start in range(0, 3 * width, CHUNK):
            out = dot_nn(rows_of(normed_ref[...]), whole[:, start : start + CHUNK])
            proj_ref[:, :, start : start + CHUNK] = out.astype(bf16).reshape(many, length, CHUNK)

        def run(index, carry):
            frame, lane_set = index // sets, index % sets

            def store(lane, value):
                mixed_ref[:, frame, :, lane] = value.reshape(tiles, cells, PAIR)

            def sums_store(value):
                spot = pl.multiple_of(lane_set * 2 * SET, 2 * SET)
                sums_ref[frame, pl.ds(spot, 2 * SET)] = value

            attend_set(
                lane_set, width, lambda lane: proj_ref[frame, :, lane], store, None, sums_store
            )
            return carry

        lax.fori_loop(0, many * sets, run, 0)

    return call(
        kernel,
        (1,),
        [
            pl.BlockSpec((tiles, many, cells, width), lambda i, s: (0, part, 0, 0)),
            pl.BlockSpec((many, 1, width), lambda i, s: (part, 0, 0)),
            full((1, width)),
            full((1, width)),
        ]
        + [ANY] * count,
        [
            full((many, length, width)),
            full((many, length, 3 * width)),
            full((tiles, many, cells, width)),
            full((many, heads, length)),
        ],
        [
            shape((many, length, width)),
            shape((many, length, 3 * width)),
            shape((tiles, many, cells, width)),
            shape((many, heads, length), f32),
        ],
        [pltpu.VMEM((width, 3 * width), bf16), pltpu.SemaphoreType.DMA((count,))],
        2 * many * length * width * (3 * width + 2 * length) * 2,
        20 << 20,
        "spatial_forward",
    )(scalars, tokens, embed, gain, shift, *arrays)


def spatial_backward(scalars, upstream, tokens, part, many, embed, gain, proj, sums, weight):
    arrays, places, rows = weight
    tiles, _, cells, width = tokens.shape
    length, count = tiles * cells, len(arrays)
    heads, sets = width // HEAD, width // (PAIR * SET)

    def kernel(scalars_ref, *refs):
        up_ref, token_ref, embed_ref, gain_ref, proj_ref, sums_ref, *refs = refs
        pieces, refs = refs[:count], refs[count:]
        grad_ref, back_ref, gain_grad, shift_grad, frame_sum, whole, sems = refs
        copies = weight_copies(scalars_ref, places, pieces, whole, sems, rows)
        for copy in copies:
            copy.start()

        def run(index, carry):
            frame, lane_set = index // sets, index % sets

            def store(lane, value):
                grad_ref[frame, :, lane] = value

            spot = pl.multiple_of(lane_set * 2 * SET, 2 * SET)
            attend_back_set(
                lane_set,
                width,
                lambda lane: proj_ref[frame, :, lane],
                lambda lane: rows_of(up_ref[:, frame, :, lane]),
                store,
                None,
                sums_ref[frame, pl.ds(spot, 2 * SET)],
            )
            return carry

        lax.fori_loop(0, many * sets, run, 0)
        for copy in copies:
            copy.wait()
        grad_normed = dot_nt(rows_of(grad_ref[...]), whole[...])
        gains, shifts = 0, 0
        for frame in range(many):
            hidden = rows_of(token_ref[:, frame]).astype(f32)
            unit, inverse = norm_unit(hidden + embed_ref[frame])
            grad = grad_normed[frame * length : (frame + 1) * length]
            back = norm_back(grad, unit, inverse, gain_ref[...])
            gains, shifts = gains + column_sum(grad * unit), shifts + column_sum(grad)
            frame_sum[frame] = column_sum(back)
            back_ref[:, frame] = back.astype(bf16).reshape(tiles, cells, width)
        gain_grad[...], shift_grad[...] = gains, shifts

    return call(
        kernel,
        (1,),
        [
            full((tiles, many, cells, width)),
            pl.BlockSpec((tiles, many, cells, width), lambda i, s: (0, part, 0, 0)),
            pl.BlockSpec((many, 1, width), lambda i, s: (part, 0, 0)),
            full((1, width)),
            full((many, length, 3 * width)),
            full((many, heads, length)),
        ]
        + [ANY] * count,
        [
            full((many, length, 3 * width)),
            full((tiles, many, cells, width)),
            full((1, width)),
            full((1, width)),
            full((many, 1, width)),
        ],
        [
            shape((many, length, 3 * width)),
            shape((tiles, many, cells, width)),
            shape((1, width), f32),
            shape((1, width), f32),
            shape((many, 1, width), f32),
        ],
        [pltpu.VMEM((width, 3 * width), bf16), pltpu.SemaphoreType.DMA((count,))],
        2 * many * length * width * (3 * width + 5 * length) * 2,
        24 << 20,
        "spatial_backward",
    )(scalars, upstream, tokens, embed, gain, proj, sums, *arrays)


def temporal_forward(scalars, tokens, embed, mixed_parts, share, gains, shifts, mask, middle):
    frames, cells, width = tokens.shape
    tiles, many = mixed_parts[0].shape[:2]
    count = len(mixed_parts)
    heads, sets, size = width // HEAD, width // (PAIR * SET), frames * GROUP
    groups = cells // GROUP
    cuts = (0, width, 4 * width, 5 * width)

    def kernel(scalars_ref, *refs):
        token_ref, embed_ref, *refs = refs
        part_refs, refs = refs[:count], refs[count:]
        gain_ref, shift_ref, mask_ref, middle_ref, *refs = refs
        outs, sums_ref, kept, refs = refs[:7], refs[7], refs[8:15], refs[15:]
        whole, sems, gathered, out_sems = refs
        space, first, normed, proj, mixed, second, last = kept
        copies = [
            pltpu.make_async_copy(
                middle_ref.at[:, start:stop], whole.at[:, start:stop], sems.at[index]
            )
            for index, (start, stop) in enumerate(zip(cuts, cuts[1:]))
        ]
        flushes = [
            pltpu.make_async_copy(ref, out, out_sems.at[index])
            for index, (ref, out) in enumerate(zip(kept, outs))
        ]
        for copy in copies:
            copy.start()
        for index, ref in enumerate(part_refs):
            for tile in range(tiles):
                start = tile * share + index * many
                gathered[start : start + many] = ref[tile]
        space[...] = gathered[:frames]
        flushes[0].start()
        copies[0].wait()
        hidden = rows_of(token_ref[...].astype(f32) + embed_ref[...])
        hidden = hidden + dot_nn(rows_of(space[...]), whole[:, :width])
        first[...] = hidden.reshape(first.shape)
        flushes[1].start()
        unit, _ = norm_unit(hidden)
        normed[...] = (unit * gain_ref[1:2] + shift_ref[1:2]).astype(bf16).reshape(normed.shape)
        flushes[2].start()
        copies[1].wait()
        for start in range(0, 3 * width, CHUNK):
            out = dot_nn(rows_of(normed[...]), whole[:, width + start : width + start + CHUNK])
            proj[:, :, start : start + CHUNK] = out.astype(bf16).reshape(frames, cells, CHUNK)
        flushes[3].start()
        allowed = mask_ref[...] > 0

        def run(index, carry):
            group, lane_set = index // sets, index % sets
            here = pl.ds(pl.multiple_of(group * GROUP, GROUP), GROUP)

            def store(lane, value):
                mixed[:, here, lane] = value.reshape(frames, GROUP, PAIR)

            def sums_store(value):
                spot = pl.multiple_of(lane_set * 2 * SET, 2 * SET)
                sums_ref[group, pl.ds(spot, 2 * SET)] = value

            attend_set(
                lane_set,
                width,
                lambda lane: rows_of(proj[:, here, lane]),
                store,
                allowed,
                sums_store,
            )
            return carry

        lax.fori_loop(0, groups * sets, run, 0)
        flushes[4].start()
        copies[2].wait()
        hidden = rows_of(first[...]) + dot_nn(rows_of(mixed[...]), whole[:, 4 * width :])
        second[...] = hidden.reshape(second.shape)
        flushes[5].start()
        unit, _ = norm_unit(hidden)
        last[...] = (unit * gain_ref[2:3] + shift_ref[2:3]).astype(bf16).reshape(last.shape)
        flushes[6].start()
        for flush in flushes:
            flush.wait()

    wide = (frames, cells, width)
    kept = [
        (wide, bf16),
        (wide, f32),
        (wide, bf16),
        ((frames, cells, 3 * width), bf16),
        (wide, bf16),
        (wide, f32),
        (wide, bf16),
    ]
    return call(
        kernel,
        (1,),
        [full(wide), full((frames, 1, width))]
        + [full(array.shape) for array in mixed_parts]
        + [full((3, width)), full((3, width)), full((2 * size, size)), ANY],
        [ANY] * 7 + [full((groups, heads, size))],
        [shape(*k) for k in kept] + [shape((groups, heads, size), f32)],
        [pltpu.VMEM(*k) for k in kept]
        + [
            pltpu.VMEM((width, 5 * width), bf16),
            pltpu.SemaphoreType.DMA((3,)),
            pltpu.VMEM((share * tiles, cells, width), bf16),
            pltpu.SemaphoreType.DMA((7,)),
        ],
        2 * frames * cells * width * (5 * width + 2 * size) * 2,
        40 << 20,
        "temporal_forward",
    )(scalars, tokens, embed, *mixed_parts, gains, shifts, mask, middle)


def temporal_backward(
    scalars, upstream, upstream_low, hidden, proj, sums, gains, mask, middle, tiles, share, count
):
    frames, cells, width = upstream.shape
    heads, sets, size = width // HEAD, width // (PAIR * SET), frames * GROUP
    groups, many = cells // GROUP, share // count
    cuts = (0, width, 4 * width, 5 * width)

    def kernel(scalars_ref, *refs):
        up_ref, low_ref, hidden_ref, proj_ref, sums_ref, gain_ref, mask_ref, *refs = refs
        middle_ref, grad_out, first_out, low_out, *refs = refs
        part_refs, refs = refs[:count], refs[count:]
        gain_grad, shift_grad, frame_sum, grads, first, first_low, *refs = refs
        whole, sems, mixed, out_sems = refs
        copies = [
            pltpu.make_async_copy(
                middle_ref.at[:, start:stop], whole.at[:, start:stop], sems.at[index]
            )
            for index, (start, stop) in enumerate(zip(cuts, cuts[1:]))
        ]
        flushes = [
            pltpu.make_async_copy(ref, out, out_sems.at[index])
            for index, (ref, out) in enumerate(
                ((grads, grad_out), (first, first_out), (first_low, low_out))
            )
        ]
        for copy in copies[::-1]:
            copy.start()
        copies[2].wait()
        out = dot_nt(rows_of(low_ref[...]), whole[:, 4 * width :])
        mixed[...] = out.astype(bf16).reshape(mixed.shape)
        allowed = mask_ref[...] > 0

        def run(index, carry):
            group, lane_set = index // sets, index % sets
            here = pl.ds(pl.multiple_of(group * GROUP, GROUP), GROUP)

            def store(lane, value):
                grads[:, here, lane] = value.reshape(frames, GROUP, PAIR)

            spot = pl.multiple_of(lane_set * 2 * SET, 2 * SET)
            attend_back_set(
                lane_set,
                width,
                lambda lane: rows_of(proj_ref[:, here, lane]),
                lambda lane: rows_of(mixed[:, here, lane]),
                store,
                allowed,
                sums_ref[group, pl.ds(spot, 2 * SET)],
            )
            return carry

        lax.fori_loop(0, groups * sets, run, 0)
        flushes[0].start()
        copies[1].wait()
        grad_normed = dot_nt(rows_of(grads[...]), whole[:, width : 4 * width])
        unit, inverse = norm_unit(rows_of(hidden_ref[...]))
        gain_grad[...] = column_sum(grad_normed * unit)
        shift_grad[...] = column_sum(grad_normed)
        out = rows_of(up_ref[...]) + norm_back(grad_normed, unit, inverse, gain_ref[1:2])
        out = out.reshape(first.shape)
        first[...] = out
        first_low[...] = out.astype(bf16)
        flushes[1].start()
        flushes[2].start()
        frame_sum[...] = jnp.sum(out, axis=1, keepdims=True)
        copies[0].wait()
        space = dot_nt(rows_of(first_low[...]), whole[:, :width]).astype(bf16)
        space = space.reshape(frames, cells, width)
        for index, ref in enumerate(part_refs):
            for tile in range(tiles):
                start = tile * share + index * many
                have = max(0, min(many, frames - start))
                if have:
                    ref[tile, :have] = space[start : start + have]
                if have < many:
                    ref[tile, have:] = jnp.zeros((many - have, cells, width), bf16)
        for flush in flushes:
            flush.wait()

    wide = (frames, cells, width)
    kept = [((frames, cells, 3 * width), bf16), (wide, f32), (wide, bf16)]
    outs = call(
        kernel,
        (1,),
        [full(wide)] * 3
        + [full((frames, cells, 3 * width)), full((groups, heads, size))]
        + [full((3, width)), full((size, 2 * size)), ANY],
        [ANY] * 3
        + [full((tiles, many, cells, width))] * count
        + [full((1, width)), full((1, width)), full((frames, 1, width))],
        [shape(*k) for k in kept]
        + [shape((tiles, many, cells, width))] * count
        + [shape((1, width), f32)] * 2
        + [shape((frames, 1, width), f32)],
        [pltpu.VMEM(*k) for k in kept]
        + [
            pltpu.VMEM((width, 5 * width), bf16),
            pltpu.SemaphoreType.DMA((3,)),
            pltpu.VMEM(wide, bf16),
            pltpu.SemaphoreType.DMA((3,)),
        ],
        2 * frames * cells * width * (5 * width + 5 * size) * 2,
        40 << 20,
        "temporal_backward",
    )(scalars, upstream, upstream_low, hidden, proj, sums, gains, mask, middle)
    return outs[0], outs[1], outs[2], outs[3 : 3 + count], *outs[3 + count :]


def expand_forward(scalars, normed, bias, weight):
    size, width = normed.shape
    hidden = weight.shape[1]
    root = math.sqrt(2 / math.pi)

    def kernel(scalars_ref, normed_ref, bias_ref, weight_ref, act_ref, slope_ref):
        value = dot_nn(normed_ref[...], weight_ref[...]) + bias_ref[...]
        square = value * value
        gate = 0.5 + 0.5 * jnp.tanh(value * (root + (root * 0.044715) * square))
        act = value * gate
        act_ref[...] = act.astype(bf16)
        slope = gate + act * (1.0 - gate) * (2 * root + (6 * root * 0.044715) * square)
        slope_ref[...] = slope.astype(bf16)

    def columns(lines):
        return pl.BlockSpec((lines, WIDE), lambda n, s: (0, n))

    return call(
        kernel,
        (hidden // WIDE,),
        [full((size, width)), columns(1), columns(width)],
        [columns(size)] * 2,
        [shape((size, hidden)), shape((size, hidden))],
        [],
        2 * size * width * hidden,
        25 << 20,
        "expand_forward",
    )(scalars, normed, bias, weight)


def expand_backward(scalars, upstream, slope, hidden, gain, expand, contract):
    size, width = upstream.shape
    inner = slope.shape[1]
    steps = 4
    chunk = inner // steps

    def kernel(scalars_ref, up_ref, slope_ref, hidden_ref, gain_ref, expand_ref, contract_ref, *refs):
        grad_ref, out_ref, low_ref, gain_grad, shift_grad, bias_grad, out_bias, total = refs
        grad = dot_nt(up_ref[...], contract_ref[...]) * slope_ref[...].astype(f32)
        grad_ref[...] = grad.astype(bf16)
        bias_grad[...] = column_sum(grad)
        part = dot_nt(grad_ref[...], expand_ref[...])

        @pl.when(pl.program_id(0) == 0)
        def _():
            total[...] = part

        @pl.when(pl.program_id(0) > 0)
        def _():
            total[...] += part

        @pl.when(pl.program_id(0) == steps - 1)
        def _():
            unit, inverse = norm_unit(hidden_ref[...])
            gain_grad[...] = column_sum(total[...] * unit)
            shift_grad[...] = column_sum(total[...])
            up = up_ref[...].astype(f32)
            out_bias[...] = column_sum(up)
            out = up + norm_back(total[...], unit, inverse, gain_ref[2:3])
            out_ref[...] = out
            low_ref[...] = out.astype(bf16)

    def columns(lines):
        return pl.BlockSpec((lines, chunk), lambda n, s: (0, n))

    once = pl.BlockSpec((size, width), lambda n, s: (0, 0), pipeline_mode=pl.Buffered(1))
    return call(
        kernel,
        (steps,),
        [
            once,
            columns(size),
            once,
            full((3, width)),
            columns(width),
            pl.BlockSpec((chunk, width), lambda n, s: (n, 0)),
        ],
        [columns(size), full((size, width)), full((size, width))]
        + [full((1, width)), full((1, width)), columns(1), full((1, width))],
        [
            shape((size, inner)),
            shape((size, width), f32),
            shape((size, width)),
            shape((1, width), f32),
            shape((1, width), f32),
            shape((1, inner), f32),
            shape((1, width), f32),
        ],
        [pltpu.VMEM((size, width), f32)],
        4 * size * width * inner,
        40 << 20,
        "expand_backward",
    )(scalars, upstream, slope, hidden, gain, expand, contract)


def contract_forward(scalars, act, hidden, bias, contract):
    size, inner = act.shape
    width = hidden.shape[1]
    steps = 4
    chunk = inner // steps

    def kernel(scalars_ref, act_ref, hidden_ref, bias_ref, contract_ref, out_ref, total):
        part = dot_nn(act_ref[...], contract_ref[...])

        @pl.when(pl.program_id(0) == 0)
        def _():
            total[...] = part + (hidden_ref[...] + bias_ref[...])

        @pl.when(pl.program_id(0) > 0)
        def _():
            total[...] += part

        @pl.when(pl.program_id(0) == steps - 1)
        def _():
            out_ref[...] = total[...].astype(bf16)

    return call(
        kernel,
        (steps,),
        [
            pl.BlockSpec((size, chunk), lambda n, s: (0, n)),
            full((size, width)),
            full((1, width)),
            pl.BlockSpec((chunk, width), lambda n, s: (n, 0)),
        ],
        [full((size, width))],
        [shape((size, width))],
        [pltpu.VMEM((size, width), f32)],
        2 * size * width * inner,
        20 << 20,
        "contract_forward",
    )(scalars, act, hidden, bias, contract)[0]


def contract_grad(scalars, left, right):
    size, height = left.shape
    width = right.shape[1]
    rows = height // 4

    def kernel(scalars_ref, left_ref, right_ref, out_ref):
        out_ref[...] = dot_tn(left_ref[...], right_ref[...]).astype(bf16)

    return call(
        kernel,
        (4,),
        [pl.BlockSpec((size, rows), lambda j, s: (0, j)), full((size, width))],
        [pl.BlockSpec((rows, width), lambda j, s: (j, 0))],
        [shape((height, width))],
        [],
        2 * size * height * width,
        (size * (height + width) + height * width) * 2,
        "contract_grad",
    )(scalars, left, right)[0]


def weight_grad(scalars, pairs, split, name):
    pairs = [(left, right) for left, right in pairs]
    lefts = [array for left, _ in pairs for array in left]
    rights = [array for _, right in pairs for array in right]
    height = lefts[0].shape[1]
    widths = [right[0].shape[1] for _, right in pairs]
    sizes = [sum(array.shape[0] for array in left) for left, _ in pairs]
    rows, half = height // BLOCKS, BLOCKS // 2
    chunk = CHUNK
    first = [sum(widths[:index]) // chunk for index in range(len(widths))]
    steps = sum(widths) // chunk

    def kernel(scalars_ref, *refs):
        left_refs, refs = refs[: len(lefts)], refs[len(lefts) :]
        right_refs, refs = refs[: len(rights)], refs[len(rights) :]
        out_refs, turned = refs[:-1], refs[-1]
        at = 0
        for index, (left, _) in enumerate(pairs):
            here = range(at, at + len(left))
            at += len(left)
            last = first[index] + widths[index] // chunk

            @pl.when(pl.program_id(0) == first[index])
            def _(here=here):
                for spot in range(BLOCKS):
                    lanes = pl.ds(spot * rows, rows)
                    if split:
                        owner = 2 * (spot % half) + spot // half
                        start = (owner ^ scalars_ref[0]) * rows
                        lanes = pl.ds(pl.multiple_of(start, rows), rows)
                    start = 0
                    for part in here:
                        ref = left_refs[part]
                        stop = start + ref.shape[0]
                        turned[spot * rows : (spot + 1) * rows, start:stop] = flipped(ref[:, lanes])
                        start = stop

            @pl.when((pl.program_id(0) >= first[index]) & (pl.program_id(0) < last))
            def _(here=here):
                start, out = 0, None
                for part in here:
                    ref = right_refs[part]
                    stop = start + ref.shape[0]
                    term = dot_nn(turned[:, start:stop], ref[...])
                    out = term if out is None else out + term
                    start = stop
                out = out.astype(bf16)
                if split:
                    out_refs[0][...] = out[: half * rows]
                    out_refs[1][...] = out[half * rows :]
                else:
                    out_refs[0][...] = out

    def right_spec(array, index):
        last = widths[index] // chunk - 1
        start = first[index]
        return pl.BlockSpec(
            (array.shape[0], chunk), lambda n, s: (0, jnp.clip(n - start, 0, last))
        )

    lines = half * rows if split else height
    count = 2 if split else 1
    return call(
        kernel,
        (steps,),
        [full(array.shape) for array in lefts]
        + [right_spec(array, index) for index, (_, right) in enumerate(pairs) for array in right],
        [pl.BlockSpec((lines, chunk), lambda n, s: (0, n))] * count,
        [shape((lines, sum(widths)))] * count,
        [pltpu.VMEM((height, max(sizes)), bf16)],
        2 * height * sum(size * width for size, width in zip(sizes, widths)),
        sum(array.size * 2 for array in lefts + rights) + height * sum(widths) * 2,
        name,
    )(scalars, *lefts, *rights)


def input_back(scalars, upstream, back_parts, share):
    frames, cells, width = upstream.shape
    tiles, many = back_parts[0].shape[:2]
    count = len(back_parts)

    def kernel(scalars_ref, up_ref, *refs):
        part_refs, (out_ref,) = refs[:count], refs[count:]
        for index, ref in enumerate(part_refs):
            for tile in range(tiles):
                start = tile * share + index * many
                have = max(0, min(many, frames - start))
                if have:
                    out = up_ref[start : start + have] + ref[tile, :have].astype(f32)
                    out_ref[start : start + have] = out.astype(bf16)

    spec = pl.BlockSpec((frames, GROUP, width), lambda g, s: (0, g, 0))
    part_spec = pl.BlockSpec((tiles, many, GROUP, width), lambda g, s: (0, 0, g, 0))
    return call(
        kernel,
        (cells // GROUP,),
        [spec] + [part_spec] * count,
        [spec],
        [shape(upstream.shape)],
        [],
        0,
        8 * frames * cells * width,
        "input_back",
    )(scalars, upstream, *back_parts)[0]


CORE, XCHIP, YCHIP = 1, 2, 4


def gate(value, *after):
    return lax.optimization_barrier((value, after))[0]


def across(array, flip):
    return lax.ppermute(array, "seq", [(i, i ^ flip) for i in range(BLOCKS)])


def gather_pieces(shard, small, tokens):
    chips = [(shard, 0), (across(shard, XCHIP), XCHIP), (across(shard, YCHIP), YCHIP)]
    chips.append((across(gate(shard, small), XCHIP | YCHIP), XCHIP | YCHIP))
    pieces = chips + [(across(gate(array, tokens), CORE), owner | CORE) for array, owner in chips]
    return [p[0] for p in pieces], [p[1] for p in pieces], shard.shape[0]


def exchange(array):
    return lax.all_to_all(array, "tile", 0, 0)


def core_sum(keep, received):
    return (keep.astype(f32) + received.astype(f32)).astype(bf16).reshape(4, -1, keep.shape[1])


def chip_parts(blocks):
    flips = (XCHIP, YCHIP, XCHIP | YCHIP)
    return [across(blocks[spot + 1], flip) for spot, flip in enumerate(flips)]


def chip_sum(blocks, parts):
    total = blocks[0].astype(f32)
    for part in parts:
        total = total + part.astype(f32)
    return total.astype(bf16)


def toward(array, pairs):
    return lax.ppermute(array, "tile", pairs)


class LineSum:
    def __init__(self, block):
        self.block = block
        self.first = toward(block, [(0, 1), (3, 2)])

    def middle(self):
        self.near = (self.block.astype(f32) + self.first.astype(f32)).astype(bf16)
        self.second = toward(self.near, [(1, 2), (2, 1)])
        return self.near

    def last(self):
        self.sum = (self.near.astype(f32) + self.second.astype(f32)).astype(bf16)
        self.third = toward(self.sum, [(1, 0), (2, 3)])
        return self.sum

    def total(self):
        tile = lax.axis_index("tile")
        return jnp.where((tile == 1) | (tile == 2), self.sum, self.third).astype(f32)


def sum_everywhere(array):
    for flip in (CORE, XCHIP, YCHIP):
        array = array + across(array, flip)
    for flip in (1, 2):
        array = array + lax.ppermute(array, "tile", [(i, i ^ flip) for i in range(4)])
    return array


def body(
    inputs,
    actions,
    segments,
    cotangent,
    action_table,
    spatial_inward,
    spatial_outward,
    temporal_inward,
    temporal_outward,
    expand_weight,
    contract_weight,
    expand_bias,
    contract_bias,
    norm_gain,
    norm_shift,
):
    seqs, tiles = lax.axis_size("seq"), lax.axis_size("tile")
    direct = seqs == BLOCKS and tiles == 4
    _, frames, cells, width = inputs.shape
    share = -(-frames // tiles)
    count = 2 if share % 2 == 0 else 1
    many = share // count
    kinds = action_table.shape[0]
    lanes = action_table.shape[1]
    me = lax.axis_index("seq").astype(jnp.int32) if direct else jnp.int32(0)
    scalars = me.reshape(1)

    tokens = inputs[0]
    padded = jnp.pad(tokens, ((0, share * tiles - frames), (0, 0), (0, 0)))
    frame_tokens = exchange(padded.reshape(tiles, share, cells, width))

    small = jnp.concatenate(
        [
            action_table,
            norm_gain,
            norm_shift,
            expand_bias.reshape(-1, lanes),
            contract_bias.reshape(1, lanes),
        ],
        axis=0,
    )
    small = lax.all_gather(small, "seq", axis=0)
    small = small.astype(f32)

    def joined(start, stop):
        return small[:, start:stop].transpose(1, 0, 2).reshape(stop - start, -1)

    table = joined(0, kinds)
    gains = joined(kinds, kinds + 3)
    shifts = joined(kinds + 3, kinds + 6)
    wide_bias = small[:, kinds + 6 : -1].reshape(1, -1)
    out_bias = small[:, -1].reshape(1, -1)

    def gathered(shard):
        return lax.all_gather(shard, "seq", axis=0, tiled=True)

    middle = jnp.concatenate([spatial_outward, temporal_inward, temporal_outward], axis=1)
    if direct:
        space_in = gather_pieces(spatial_inward, small, frame_tokens)
        middle = gathered(gate(middle, *space_in[0][1:3]))
        expand = gathered(gate(expand_weight, *space_in[0][4:]))
    else:
        space_in = ([gathered(spatial_inward)], [0], width // BLOCKS)
        middle, expand = gathered(middle), gathered(expand_weight)

    onehot = (actions[0][:, None] == jnp.arange(kinds, dtype=jnp.int32)[None, :]).astype(f32)
    embed = jnp.dot(onehot, table, precision=lax.Precision.HIGHEST)
    onehot_own = lax.dynamic_slice_in_dim(
        jnp.pad(onehot, ((0, share * tiles - frames), (0, 0))),
        lax.axis_index("tile") * share,
        share,
        0,
    )
    embed_own = jnp.dot(onehot_own, table, precision=lax.Precision.HIGHEST)
    embed, embed_own = embed[:, None, :], embed_own[:, None, :]

    index = jnp.arange(frames * GROUP, dtype=jnp.int32)
    frame_of, place_of = index // GROUP, index % GROUP
    ids = jnp.repeat(segments[0], GROUP)
    mask = (
        (place_of[:, None] == place_of[None, :])
        & (frame_of[:, None] >= frame_of[None, :])
        & (ids[:, None] == ids[None, :])
    ).astype(f32)
    mask_rows = jnp.concatenate([mask, mask], axis=0)
    mask_lanes = jnp.concatenate([mask.T, mask.T], axis=1)

    saved, mixed_parts = [], []
    for part in range(count):
        normed, proj, mixed, sums = spatial_forward(
            scalars, frame_tokens, part, many, embed_own, gains[0:1], shifts[0:1], space_in
        )
        saved.append((normed, proj, sums))
        mixed_parts.append(exchange(mixed))
    contract = gathered(gate(contract_weight, mixed))
    (
        space_rows,
        space_sum,
        normed_two,
        time_proj,
        time_mixed,
        time_sum,
        normed_three,
        time_sums,
    ) = temporal_forward(
        scalars, tokens, embed, mixed_parts, share, gains, shifts, mask_rows, middle
    )

    def flat(array):
        return array.reshape(-1, array.shape[-1])

    upstream = flat(cotangent[0])
    act, slope = expand_forward(scalars, flat(normed_three), wide_bias, expand)
    grad_contract = contract_grad(scalars, act, upstream)
    contract_block = lax.psum_scatter(grad_contract, "seq", scatter_dimension=0, tiled=True)
    (
        grad_hidden,
        grad_time_sum,
        time_low,
        gain_three,
        shift_three,
        grad_wide_bias,
        grad_out_bias,
    ) = expand_backward(
        gate(scalars, grad_contract), upstream, slope, flat(time_sum), gains, expand, contract
    )
    grad_expand = weight_grad(
        scalars, [([flat(normed_three)], [grad_hidden])], False, "expand_grad"
    )[0]
    expand_block = lax.psum_scatter(grad_expand, "seq", scatter_dimension=0, tiled=True)

    (
        grad_time_proj,
        grad_space_sum,
        space_low,
        space_ups,
        gain_two,
        shift_two,
        frame_sum,
    ) = temporal_backward(
        gate(scalars, grad_expand),
        grad_time_sum.reshape(frames, cells, width),
        time_low.reshape(frames, cells, width),
        space_sum,
        time_proj,
        time_sums,
        gains,
        mask_lanes,
        middle,
        tiles,
        share,
        count,
    )
    frame_ups = [exchange(ups) for ups in space_ups]
    time_parts = weight_grad(
        gate(scalars, grad_space_sum),
        [
            ([flat(time_mixed)], [time_low]),
            ([flat(space_rows)], [flat(space_low)]),
            ([flat(normed_two)], [flat(grad_time_proj)]),
        ],
        direct,
        "time_grad",
    )
    back_parts, grad_space_parts = [], []
    gain_one = shift_one = 0
    own_sums = []
    after = time_parts
    if direct:
        time_received = across(time_parts[1], CORE)
        after = (*time_parts, expand_block)
    for part in range(count):
        grads, backs, gain_part, shift_part, own_sum = spatial_backward(
            gate(scalars, *after),
            frame_ups[part],
            frame_tokens,
            part,
            many,
            embed_own,
            gains[0:1],
            saved[part][1],
            saved[part][2],
            space_in,
        )
        gain_one, shift_one = gain_one + gain_part, shift_one + shift_part
        own_sums.append(own_sum)
        grad_space_parts.append(grads)
        back_parts.append(exchange(backs))
        after = (grads,)
        if direct and part == 0:
            time_blocks = core_sum(gate(time_parts[0], grads), time_received)
            contract_line = LineSum(gate(contract_block, grads))
            time_chips = chip_parts(time_blocks)
            after = (grads, time_blocks)
    space_in_parts = weight_grad(
        gate(scalars, *after),
        [([flat(s[0]) for s in saved], [flat(g) for g in grad_space_parts])],
        direct,
        "space_in_grad",
    )
    after = space_in_parts
    if direct:
        space_received = across(space_in_parts[1], CORE)
        contract_line.block = gate(contract_line.block, *space_in_parts)
        expand_line = LineSum(gate(expand_block, contract_line.middle()))
        after = (*space_in_parts, expand_line.block)
    outputs = contract_forward(gate(scalars, *after), act, flat(time_sum), out_bias, contract)

    own_sum = jnp.concatenate(own_sums, axis=0)
    grad_table = jnp.einsum(
        "fa,fd->ad", onehot, frame_sum[:, 0], precision=lax.Precision.HIGHEST
    ) + jnp.einsum("fa,fd->ad", onehot_own, own_sum[:, 0], precision=lax.Precision.HIGHEST)
    small_grads = jnp.concatenate(
        [
            grad_table,
            gain_one,
            gain_two,
            gain_three,
            shift_one,
            shift_two,
            shift_three,
            grad_wide_bias.reshape(-1, width),
            grad_out_bias,
        ],
        axis=0,
    )
    small_grads = sum_everywhere(small_grads) if direct else lax.psum(small_grads, ("seq", "tile"))

    input_grad = input_back(scalars, grad_space_sum, back_parts, share)

    if direct:
        space_blocks = core_sum(gate(space_in_parts[0], outputs), space_received)
        space_chips = chip_parts(space_blocks)
        time_line = LineSum(chip_sum(gate(time_blocks, space_blocks), time_chips))
        contract_line.last()
        expand_line.middle()
        expand_line.last()
        time_line.middle()
        time_line.last()
        space_line = LineSum(chip_sum(space_blocks, space_chips))
        space_line.middle()
        space_line.last()
        total_contract, total_expand, total_time, total_space_in = (
            line.total() for line in (contract_line, expand_line, time_line, space_line)
        )
    else:

        def plain_total(array):
            shard = lax.psum_scatter(array, "seq", scatter_dimension=0, tiled=True)
            return lax.psum(shard, "tile").astype(f32)

        total_contract, total_expand = (
            lax.psum(block, "tile").astype(f32) for block in (contract_block, expand_block)
        )
        total_time, total_space_in = plain_total(time_parts[0]), plain_total(space_in_parts[0])

    here = lax.axis_index("seq")

    def own_lanes(array):
        return lax.dynamic_slice_in_dim(array, here * lanes, lanes, 1)

    wide_total = small_grads[kinds + 6 : -1].reshape(-1)
    wide_share = expand_bias.shape[0]
    return (
        outputs.reshape(inputs.shape),
        input_grad.reshape(inputs.shape),
        own_lanes(small_grads[:kinds]),
        total_space_in,
        total_time[:, width : 2 * width],
        total_time[:, 2 * width :],
        total_time[:, :width],
        total_expand,
        total_contract,
        lax.dynamic_slice_in_dim(wide_total, here * wide_share, wide_share, 0),
        own_lanes(small_grads[-1:]).reshape(-1),
        own_lanes(small_grads[kinds : kinds + 3]),
        own_lanes(small_grads[kinds + 3 : kinds + 6]),
    )


def solution(mesh):
    seq_first, seq_last = P("seq", None), P(None, "seq")
    stream = P("seq", None, "tile", None)
    return jax.shard_map(
        body,
        mesh=mesh,
        in_specs=(stream, seq_first, seq_first, stream, seq_last)
        + (seq_first,) * 6
        + (P("seq"), P("seq"), seq_last, seq_last),
        out_specs=(stream, stream, seq_last)
        + (seq_first,) * 6
        + (P("seq"), P("seq"), seq_last, seq_last),
        check_vma=False,
    )
```

time: 855 us -> 664 us (0.78)
  starting transfers between devices: 204 us -> 82.7 us
  other arithmetic: 94.3 us -> 36.1 us
  Pallas kernels: 261 us -> 242 us
  waiting for transfers between devices: 236 us -> 251 us
  between operations: 2.25 us -> 15 us
  local copies, waits for them, and re-layouts: 30.9 us -> 18.8 us
    ppermute x54 -> x12, starting transfers between devices: 156 us -> 27.7 us  [toward(): return lax.ppermute(array, 'tile', pairs)]
    all_to_all x0 -> x7, waiting for transfers between devices: none -> 83 us  [exchange(): return lax.all_to_all(array, 'tile', 0, 0)]
    ppermute x64 -> x18, waiting for transfers between devices: 136 us -> 84.9 us  [across(): return lax.ppermute(array, 'seq', [(i, i ^ flip) for i in range(BLOCKS)])]
    ppermute x54 -> x12, waiting for transfers between devices: 99.5 us -> 56.4 us  [toward(): return lax.ppermute(array, 'tile', pairs)]
    all_to_all x0 -> x7, starting transfers between devices: none -> 32.2 us  [exchange(): return lax.all_to_all(array, 'tile', 0, 0)]
    ppermute x64 -> x18, starting transfers between devices: 45.6 us -> 18 us  [across(): return lax.ppermute(array, 'seq', [(i, i ^ flip) for i in range(BLOCKS)])]
    ppermute x2, waiting for transfers between devices: 0.01 us -> 16.7 us  [sum_everywhere(): lax.ppermute(array, 'tile', [(i, i ^ flip) for i in range(4)])]
    add x5 -> x0, other arithmetic: 15.9 us -> none  [step(): self.sum = self.sum + up.astype(f32) + down.astype(f32)]
  transfers between devices with their start and end apart: 120 -> 44, of which waited for: 34 -> 25; matrix products, arithmetic and copies ran while one was open for 13% -> 8% of each run, Pallas kernels for 28% -> 31%
where the time goes in v2:
time: 664 us; the launch traced here: 655 us
  waiting for transfers between devices  251 us (38%)
  Pallas kernels  242 us (36%)
  starting transfers between devices  82.7 us (12%)
  other arithmetic  36.1 us (5%)
  local copies, waits for them, and re-layouts  18.8 us (3%)
  between operations  15 us (2%)
  blocking collectives  9.16 us (1%)
    ppermute x18, waiting for transfers between devices, across(): return lax.ppermute(array, 'seq', [(i, i ^ flip) for i in range(BLOCKS)])  84.9 us
    all_to_all x7, waiting for transfers between devices, exchange(): return lax.all_to_all(array, 'tile', 0, 0)  83 us
    ppermute x12, waiting for transfers between devices, toward(): return lax.ppermute(array, 'tile', pairs)  56.4 us
    pallas_call x3, Pallas kernels, weight_grad(): call(kernel, (steps,), [full(array.shape) for array in lefts] + [right_sp...  44.5 us
    pallas_call x1, Pallas kernels, temporal_backward(): call(kernel, (1,), [full(wide)] * 3 + [full((frames, cells, 3 * width)),...  35.2 us
    pallas_call x2, Pallas kernels, spatial_backward(): call(kernel, (1,), [full((tiles, many, cells, width)), pl.BlockSpec((tile...  32.8 us
    all_to_all x7, starting transfers between devices, exchange(): return lax.all_to_all(array, 'tile', 0, 0)  32.2 us
    ppermute x12, starting transfers between devices, toward(): return lax.ppermute(array, 'tile', pairs)  27.7 us
  transfers between devices with their start and end apart: 44, of which 25 were waited for; matrix products, arithmetic and copies ran while one was open for 8% of the time, Pallas kernels for 31%

profile of v2, /device:TPU:0, one launch (start us, length us, event | category | flops | bytes accessed | tf_op | source)
XLA Modules:
  0.0 655.5 jit_solution(7298025799499261366)
XLA Ops:
  7.2 3.0 collective-permute-start
  10.2 1.5 collective-permute-start.1
  11.8 2.4 pad_maximum_fusion
  14.2 13.8 %collective-permute-done.refs_5_.refs_7_ = bf16[128,3072]{1,0:T(8,128)(2,1)S(1)} collective-permute-done((bf16[128,3072]{1,0:T(8,128)(2,1)}, bf16[128,3072]{1,0:T(8,128)(2,1)S(1)}, u32[]{:S(2)}, u32[]{:S(2)}) %collective-permute-start) | collective-permute-done | bytes 786464 | tf_op jit(solution)/shard_map/ppermute | solution.py:812
  29.5 1.6 pad.11
  31.2 5.0 all-to-all-start
  36.4 9.2 %all-gather.1 = bf16[8,19,128]{2,1,0:T(8,128)(2,1)S(1)} all-gather(bf16[1,19,128]{2,1,0:T(8,128)(2,1)S(1)} %bitcast.70), channel_id=2, replica_groups=mesh['seq'=8,'tile'=4] {'seq'}, dimensions={0}, use_global_device_ids=true | all-gather | bytes 43776 | tf_op jit(solution)/shard_map/all_gather | solution.py:916
  45.6 1.5 collective-permute-start.2
  47.1 25.7 %collective-permute-done.2.refs_7_.refs_9_ = bf16[128,3072]{1,0:T(8,128)(2,1)} collective-permute-done((bf16[128,3072]{1,0:T(8,128)(2,1)S(1)}, bf16[128,3072]{1,0:T(8,128)(2,1)}, u32[]{:S(2)}, u32[]{:S(2)}) %collective-permute-start.2) | collective-permute-done | bytes 786464 | tf_op jit(solution)/shard_map/ppermute | solution.py:812
  72.9 10.5 %all-to-all-done.refs_0_.refs_1_ = bf16[4,4,64,1024]{3,2,1,0:T(8,128)(2,1)} async-done(((bf16[4,4,64,1024]{3,2,1,0:T(8,128)(2,1)}), bf16[4,4,64,1024]{3,2,1,0:T(8,128)(2,1)}, u32[]{:S(2)}, u32[]{:S(2)}) %all-to-all-start) | async-done | bytes 2097184 | tf_op jit(solution)/shard_map/all_to_all | solution.py:823
  84.3 2.7 collective-permute-done.6.refs_11_.refs_13_
  92.1 13.6 %spatial_forward.3 = (bf16[2,256,1024]{2,1,0:T(8,128)(2,1)}, bf16[2,256,3072]{2,1,0:T(8,128)(2,1)}, bf16[4,2,64,1024]{3,2,1,0:T(8,128)(2,1)}, f32[2,16,256]{2,1,0:T(8,128)}) custom-call(s32[1]{0:T(128)} %bitcast.scalars_ref, bf16[4,4,64,1024]{3,2,1,0:T(8,128)(2,1)} %all-to-all-done.refs_0_.refs_1_, f32[4,1,1024]{2,1,0:T(1,128)} %broadcast_in_dim.7.refs_1_.refs_2_, ...), custom_call_target="tpu_custom_call" | custom-call | flops 7516192768 | bytes 20971520 | tf_op jit(solution)/shard_map/spatial_forward/pallas_call | solution.py:213
  105.7 3.5 all-to-all-start.2
  109.3 13.4 %spatial_forward.2 = (bf16[2,256,1024]{2,1,0:T(8,128)(2,1)}, bf16[2,256,3072]{2,1,0:T(8,128)(2,1)}, bf16[4,2,64,1024]{3,2,1,0:T(8,128)(2,1)}, f32[2,16,256]{2,1,0:T(8,128)}) custom-call(s32[1]{0:T(128)} %bitcast.scalars_ref, bf16[4,4,64,1024]{3,2,1,0:T(8,128)(2,1)} %all-to-all-done.refs_0_.refs_1_, f32[4,1,1024]{2,1,0:T(1,128)} %broadcast_in_dim.7.refs_1_.refs_2_, ...), custom_call_target="tpu_custom_call" | custom-call | flops 7516192768 | bytes 20971520 | tf_op jit(solution)/shard_map/spatial_forward/pallas_call | solution.py:213
  122.7 12.8 %all-to-all-done.2.refs_3_ = bf16[4,2,64,1024]{3,2,1,0:T(8,128)(2,1)S(1)} async-done(((bf16[4,2,64,1024]{3,2,1,0:T(8,128)(2,1)}), bf16[4,2,64,1024]{3,2,1,0:T(8,128)(2,1)S(1)}, u32[]{:S(2)}, u32[]{:S(2)}) %all-to-all-start.2) | async-done | bytes 1048608 | tf_op jit(solution)/shard_map/all_to_all | solution.py:823
  135.6 4.2 all-to-all-start.1
  142.6 22.7 %all-to-all-done.1.refs_2_ = bf16[4,2,64,1024]{3,2,1,0:T(8,128)(2,1)} async-done(((bf16[4,2,64,1024]{3,2,1,0:T(8,128)(2,1)}), bf16[4,2,64,1024]{3,2,1,0:T(8,128)(2,1)}, u32[]{:S(2)}, u32[]{:S(2)}) %all-to-all-start.1) | async-done | bytes 1048608 | tf_op jit(solution)/shard_map/all_to_all | solution.py:823
  165.4 27.6 %temporal_forward.1 = (bf16[13,64,1024]{2,1,0:T(8,128)(2,1)}, f32[13,64,1024]{2,1,0:T(8,128)}, bf16[13,64,1024]{2,1,0:T(8,128)(2,1)}, bf16[13,64,3072]{2,1,0:T(8...) custom-call(s32[1]{0:T(128)} %bitcast.scalars_ref, ...), custom_call_target="tpu_custom_call" | custom-call | flops 18865979392 | bytes 41943040 | tf_op jit(solution)/shard_map/temporal_forward/pallas_call | solution.py:413
  193.0 17.4 %expand_forward.1 = (bf16[832,4096]{1,0:T(8,128)(2,1)}, bf16[832,4096]{1,0:T(8,128)(2,1)}) custom-call(s32[1]{0:T(128)} %bitcast.scalars_ref, bf16[832,1024]{1,0:T(8,128)(2,1)} %bitcast.92, f32[1,4096]{1,0:T(1,128)} %bitcast.72, bf16[1024,4096]{1,0:T(8,128)(2,1)} %all-gather.8.cloned.1.call-done.weight_ref.expand_ref), custom_call_target="tpu_custom_call" | custom-call | flops 6979321856 | bytes 26214400 | tf_op jit(solution)/shard_map/expand_forward/pallas_call | solution.py:560
  210.4 12.8 %contract_grad.1 = bf16[4096,1024]{1,0:T(8,128)(2,1)} custom-call(s32[1]{0:T(128)} %bitcast.scalars_ref, bf16[832,4096]{1,0:T(8,128)(2,1)} %get-tuple-element.90.left_ref.act_ref, bf16[832,1024]{1,0:T(8,128)(2,1)} %bitcast.79), custom_call_target="tpu_custom_call" | custom-call | flops 6979321856 | bytes 16908288 | tf_op jit(solution)/shard_map/contract_grad/pallas_call | solution.py:685
  223.2 27.0 %expand_backward.1 = (bf16[832,4096]{1,0:T(8,128)(2,1)}, f32[832,1024]{1,0:T(8,128)}, bf16[832,1024]{1,0:T(8,128)(2,1)}, f32[1,1024]{1,0:T(1,128)}, f32[1,1024]{...) custom-call(s32[1]{0:T(128)} %bitcast.scalars_ref, bf16[832,1024]{1,0:T(8,128)(2,1)} %bitcast.80, ...), custom_call_target="tpu_custom_call" | custom-call | flops 13958643712 | bytes 41943040 | tf_op jit(solution)/shard_map/expand_backward/pallas_call | solution.py:609
  250.2 13.5 %expand_grad.1 = bf16[1024,4096]{1,0:T(8,128)(2,1)} custom-call(s32[1]{0:T(128)} %bitcast.scalars_ref, bf16[832,1024]{1,0:T(8,128)(2,1)} %bitcast.93, bf16[832,4096]{1,0:T(8,128)(2,1)} %get-tuple-element.95.refs_1_), custom_call_target="tpu_custom_call" | custom-call | flops 6979321856 | bytes 16908288 | tf_op jit(solution)/shard_map/expand_grad/pallas_call | solution.py:760
  265.2 35.2 %temporal_backward.1 = (bf16[13,64,3072]{2,1,0:T(8,128)(2,1)}, f32[13,64,1024]{2,1,0:T(8,128)}, bf16[13,64,1024]{2,1,0:T(8,128)(2,1)}, bf16[4,2,64,1024]{3,2,1,0...) custom-call(s32[1]{0:T(128)} %bitcast.scalars_ref, ...), custom_call_target="tpu_custom_call" | custom-call | flops 20992491520 | bytes 41943040 | tf_op jit(solution)/shard_map/temporal_backward/pallas_call | solution.py:516
  300.4 19.5 %time_grad.1 = (bf16[512,5120]{1,0:T(8,128)(2,1)}, bf16[512,5120]{1,0:T(8,128)(2,1)}) custom-call(s32[1]{0:T(128)} %bitcast.scalars_ref, bf16[832,1024]{1,0:T(8,128)(2,1)} %bitcast.90, bf16[832,1024]{1,0:T(8,128)(2,1)} %bitcast.88, bf16[832,1024]{1,0:T(8,128)(2,1)} %bitcast.89, bf16[832,1024]{1,0:T(8,128)(2,1)} %get-tuple-element.98.refs_3_, ...), custom_call_target="tpu_custom_call" | custom-call | flops 8724152320 | bytes 24117248 | tf_op jit(solution)/shard_map/time_grad/pallas_call | solution.py:760
  320.0 4.3 all-to-all-start.3
  325.8 8.9 %reduce-scatter.3.cloned.1.call-done = bf16[128,4096]{1,0:T(8,128)(2,1)} async-done(((bf16[1024,4096]{1,0:T(8,128)(2,1)}), bf16[128,4096]{1,0:T(8,128)(2,1)}) %reduce-scatter.3.cloned.1.call-update) | async-done | bytes 1048592 | tf_op jit(solution)/shard_map/reduce_scatter | solution.py:1004
  334.7 15.8 %all-to-all-done.3.refs_0_ = bf16[4,2,64,1024]{3,2,1,0:T(8,128)(2,1)S(1)} async-done(((bf16[4,2,64,1024]{3,2,1,0:T(8,128)(2,1)}), bf16[4,2,64,1024]{3,2,1,0:T(8,128)(2,1)S(1)}, u32[]{:S(2)}, u32[]{:S(2)}) %all-to-all-start.3) | async-done | bytes 1048608 | tf_op jit(solution)/shard_map/all_to_all | solution.py:823
  351.5 3.7 all-to-all-start.4
  355.2 16.3 %spatial_backward.2 = (bf16[2,256,3072]{2,1,0:T(8,128)(2,1)}, bf16[4,2,64,1024]{3,2,1,0:T(8,128)(2,1)}, f32[1,1024]{1,0:T(1,128)}, f32[1,1024]{1,0:T(1,128)}, f32[2,1,1024]{2,1,0:T(1,128)}) custom-call(s32[1]{0:T(128)} %bitcast.scalars_ref, bf16[4,2,64,1024]{3,2,1,0:T(8,128)(2,1)} %copy-done.5, bf16[4,4,64,1024]{3,2,1,0:T(8,128)(2,1)} %all-to-all-done.refs_0_.refs_1_, ...), custom_call_target="tpu_custom_call" | custom-call | flops 9126805504 | bytes 25165824 | tf_op jit(solution)/shard_map/spatial_backward/pallas_call | solution.py:289
  371.5 8.5 %add_convert_fusion = bf16[512,5120]{1,0:T(8,128)(2,1)} fusion(bf16[512,5120]{1,0:T(8,128)(2,1)} %collective-permute-done.7, bf16[512,5120]{1,0:T(8,128)(2,1)} %get-tuple-element.116), kind=kLoop, calls=%fused_computation | loop fusion | flops 10485760 | bytes 15728640 | tf_op jit(solution)/shard_map/convert_element_type | solution.py:827
  381.7 16.5 %spatial_backward.3 = (bf16[2,256,3072]{2,1,0:T(8,128)(2,1)}, bf16[4,2,64,1024]{3,2,1,0:T(8,128)(2,1)}, f32[1,1024]{1,0:T(1,128)}, f32[1,1024]{1,0:T(1,128)}, f32[2,1,1024]{2,1,0:T(1,128)}) custom-call(s32[1]{0:T(128)} %bitcast.scalars_ref, bf16[4,2,64,1024]{3,2,1,0:T(8,128)(2,1)} %copy-done.4, bf16[4,4,64,1024]{3,2,1,0:T(8,128)(2,1)} %all-to-all-done.refs_0_.refs_1_, ...), custom_call_target="tpu_custom_call" | custom-call | flops 9126805504 | bytes 25165824 | tf_op jit(solution)/shard_map/spatial_backward/pallas_call | solution.py:289
  402.1 1.5 collective-permute-start.10
  403.7 6.0 collective-permute-done.10
  409.7 2.2 collective-permute-start.11
  412.4 2.0 collective-permute-done.11
  414.4 1.5 collective-permute-start.12
  416.0 4.1 fusion.14
  420.1 3.4 collective-permute-start.8
  427.0 4.5 all-to-all-start.6
  431.6 3.0 collective-permute-start.13
  434.6 11.5 %space_in_grad.1 = (bf16[512,3072]{1,0:T(8,128)(2,1)}, bf16[512,3072]{1,0:T(8,128)(2,1)}) custom-call(s32[1]{0:T(128)} %bitcast.scalars_ref, bf16[512,1024]{1,0:T(8,128)(2,1)} %bitcast.96, bf16[512,1024]{1,0:T(8,128)(2,1)} %bitcast.95, bf16[512,3072]{1,0:T(8,128)(2,1)} %bitcast.85, bf16[512,3072]{1,0:T(8,128)(2,1)} %bitcast.86), custom_call_target="tpu_custom_call" | custom-call | flops 6442450944 | bytes 14680064 | tf_op jit(solution)/shard_map/space_in_grad/pallas_call | solution.py:760
  446.0 16.7 %collective-permute-done.13 = f32[19,1024]{1,0:T(8,128)S(1)} collective-permute-done((f32[19,1024]{1,0:T(8,128)S(1)}, f32[19,1024]{1,0:T(8,128)S(1)}, u32[]{:S(2)}, u32[]{:S(2)}) %collective-permute-start.13) | collective-permute-done | bytes 77856 | tf_op jit(solution)/shard_map/ppermute | solution.py:870
  465.8 2.9 add_convert_fusion.7
  468.7 1.7 collective-permute-start.30
  470.3 6.8 %all-to-all-start.5 = ((bf16[4,2,64,1024]{3,2,1,0:T(8,128)(2,1)}), bf16[4,2,64,1024]{3,2,1,0:T(8,128)(2,1)}, u32[]{:S(2)}, u32[]{:S(2)}) async-start(bf16[4,2,64,1024]{3,2,1,0:T(8,128)(2,1)} %get-tuple-element.131), calls=%async_computation.7 | async-start | bytes 2097152 | tf_op jit(solution)/shard_map/all_to_all | solution.py:823
  477.2 4.9 collective-permute-start.27
  482.1 3.3 fusion.2
  485.4 2.4 collective-permute-start.24
  487.8 13.9 %contract_forward.1 = bf16[832,1024]{1,0:T(8,128)(2,1)} custom-call(s32[1]{0:T(128)} %bitcast.scalars_ref, bf16[832,4096]{1,0:T(8,128)(2,1)} %get-tuple-element.90.left_ref.act_ref, f32[832,1024]{1,0:T(8,128)} %bitcast.83, f32[1,1024]{1,0:T(1,128)} %slice_bitcast_fusion.9.bias_ref, bf16[4096,1024]{1,0:T(8,128)(2,1)} %all-gather.10.cloned.1.call-done.contract_ref), custom_call_target="tpu_custom_call" | custom-call | flops 6979321856 | bytes 20971520 | tf_op jit(solution)/shard_map/contract_forward/pallas_call | solution.py:659
  501.6 20.5 %all-to-all-done.5.refs_0_ = bf16[4,2,64,1024]{3,2,1,0:T(8,128)(2,1)} async-done(((bf16[4,2,64,1024]{3,2,1,0:T(8,128)(2,1)}), bf16[4,2,64,1024]{3,2,1,0:T(8,128)(2,1)}, u32[]{:S(2)}, u32[]{:S(2)}) %all-to-all-start.5) | async-done | bytes 1048608 | tf_op jit(solution)/shard_map/all_to_all | solution.py:823
  522.2 4.3 input_back.1
  526.5 1.9 add_convert_fusion.4
  529.7 1.8 add_convert_fusion.6
  532.4 12.8 %collective-permute-done.24 = bf16[128,5120]{1,0:T(8,128)(2,1)} collective-permute-done((bf16[128,5120]{1,0:T(8,128)(2,1)S(1)}, bf16[128,5120]{1,0:T(8,128)(2,1)}, u32[]{:S(2)}, u32[]{:S(2)}) %collective-permute-start.24) | collective-permute-done | bytes 1310752 | tf_op jit(solution)/shard_map/ppermute | solution.py:843
  545.2 1.6 add_convert_fusion.3
  547.6 3.1 add_convert_fusion.1
  550.8 1.5 collective-permute-start.15
  557.8 13.5 %collective-permute-done.15 = bf16[128,3072]{1,0:T(8,128)(2,1)S(1)} collective-permute-done((bf16[128,3072]{1,0:T(8,128)(2,1)S(1)}, bf16[128,3072]{1,0:T(8,128)(2,1)S(1)}, u32[]{:S(2)}, u32[]{:S(2)}) %collective-permute-start.15) | collective-permute-done | bytes 786464 | tf_op jit(solution)/shard_map/ppermute | solution.py:812
  571.3 14.6 %collective-permute-done.16 = bf16[128,3072]{1,0:T(8,128)(2,1)S(1)} collective-permute-done((bf16[128,3072]{1,0:T(8,128)(2,1)S(1)}, bf16[128,3072]{1,0:T(8,128)(2,1)S(1)}, u32[]{:S(2)}, u32[]{:S(2)}) %collective-permute-start.16) | collective-permute-done | bytes 786464 | tf_op jit(solution)/shard_map/ppermute | solution.py:812
  586.0 1.8 collective-permute-done.17
  588.3 7.8 %collective-permute-start.18 = (bf16[128,3072]{1,0:T(8,128)(2,1)S(1)}, bf16[128,3072]{1,0:T(8,128)(2,1)S(1)}, u32[]{:S(2)}, u32[]{:S(2)}) collective-permute-start(bf16[128,3072]{1,0:T(8,128)(2,1)S(1)} %add_convert_fusion.10), channel_id=1, source_target_pairs={{0,1},{3,2},{4,5},{7,6},{8,9},{11,10},{12,13},{15,14},{16,17},{19,... | collective-permute-start | bytes 2359304 | tf_op jit(solution)/shard_map/ppermute | solution.py:843
  597.7 13.2 %collective-permute-done.18 = bf16[128,3072]{1,0:T(8,128)(2,1)S(1)} collective-permute-done((bf16[128,3072]{1,0:T(8,128)(2,1)S(1)}, bf16[128,3072]{1,0:T(8,128)(2,1)S(1)}, u32[]{:S(2)}, u32[]{:S(2)}) %collective-permute-start.18) | collective-permute-done | bytes 786464 | tf_op jit(solution)/shard_map/ppermute | solution.py:843
  614.8 11.8 %collective-permute-done.26 = bf16[128,5120]{1,0:T(8,128)(2,1)S(1)} collective-permute-done((bf16[128,5120]{1,0:T(8,128)(2,1)S(1)}, bf16[128,5120]{1,0:T(8,128)(2,1)S(1)}, u32[]{:S(2)}, u32[]{:S(2)}) %collective-permute-start.26) | collective-permute-done | bytes 1310752 | tf_op jit(solution)/shard_map/ppermute | solution.py:843
  629.1 18.1 %collective-permute-done.20 = bf16[128,3072]{1,0:T(8,128)(2,1)S(1)} collective-permute-done((bf16[128,3072]{1,0:T(8,128)(2,1)S(1)}, bf16[128,3072]{1,0:T(8,128)(2,1)S(1)}, u32[]{:S(2)}, u32[]{:S(2)}) %collective-permute-start.20) | collective-permute-done | bytes 786464 | tf_op jit(solution)/shard_map/ppermute | solution.py:843
  (169 shorter events, 45.5 us)
Async XLA Ops:
  7.2 22.3 %copy-start.2 = (bf16[1,13,64,1024]{3,2,1,0:T(8,128)(2,1)S(1)}, bf16[1,13,64,1024]{3,2,1,0:T(8,128)(2,1)}, u32[]{:S(2)}) copy-start(bf16[1,13,64,1024]{3,2,1,0:T(8,128)(2,1)} %param.15) | copy-start | bytes 5111812
  7.2 158.2 %all-gather.6.cloned.1.call-start = ((), (), s32[]{:S(2)}) async-start(), calls=%async_computation.9 | async-start | bytes 11796480 | tf_op jit(solution)/shard_map/all_gather | solution.py:929
  7.2 20.8 %collective-permute-start = (bf16[128,3072]{1,0:T(8,128)(2,1)}, bf16[128,3072]{1,0:T(8,128)(2,1)S(1)}, u32[]{:S(2)}, u32[]{:S(2)}) collective-permute-start(bf16[128,3072]{1,0:T(8,128)(2,1)} %refs_6_.3), channel_id=1, source_target_pairs={{0,8},{4,12},{8,0},{12,4},{16,24},{20,28},{24,16},{28,20},{1,9},{5... | collective-permute-start | bytes 2359304 | tf_op jit(solution)/shard_map/ppermute | solution.py:812
  10.2 19.2 %collective-permute-start.1 = (bf16[128,3072]{1,0:T(8,128)(2,1)}, bf16[128,3072]{1,0:T(8,128)(2,1)S(1)}, u32[]{:S(2)}, u32[]{:S(2)}) collective-permute-start(bf16[128,3072]{1,0:T(8,128)(2,1)} %refs_6_.3), channel_id=1, source_target_pairs={{0,16},{4,20},{8,24},{12,28},{16,0},{20,4},{24,8},{28,12},{1,17},{... | collective-permute-start | bytes 2359304 | tf_op jit(solution)/shard_map/ppermute | solution.py:812
  31.1 5.1 copy-start.17
  31.1 5.1 copy-start.18
  31.1 14.4 %copy-start.23 = (bf16[128,3072]{1,0:T(8,128)(2,1)S(1)}, bf16[128,3072]{1,0:T(8,128)(2,1)}, u32[]{:S(2)}) copy-start(bf16[128,3072]{1,0:T(8,128)(2,1)} %refs_6_.3) | copy-start | bytes 2359300
  31.2 52.2 %copy-start.25 = (bf16[128,3072]{1,0:T(8,128)(2,1)S(1)}, bf16[128,3072]{1,0:T(8,128)(2,1)}, u32[]{:S(2)}) copy-start(bf16[128,3072]{1,0:T(8,128)(2,1)} %copy-done.24) | copy-start | bytes 2359300
  31.2 52.7 %copy-start.27 = (bf16[128,3072]{1,0:T(8,128)(2,1)S(1)}, bf16[128,3072]{1,0:T(8,128)(2,1)}, u32[]{:S(2)}) copy-start(bf16[128,3072]{1,0:T(8,128)(2,1)} %copy-done.26) | copy-start | bytes 2359300
  31.2 58.9 %copy-start.9 = (s32[1,13]{1,0:T(1,128)S(1)}, s32[1,13]{1,0:T(1,128)}, u32[]{:S(2)}) copy-start(s32[1,13]{1,0:T(1,128)} %param.16) | copy-start | bytes 160
  31.2 52.1 %all-to-all-start = ((bf16[4,4,64,1024]{3,2,1,0:T(8,128)(2,1)}), bf16[4,4,64,1024]{3,2,1,0:T(8,128)(2,1)}, u32[]{:S(2)}, u32[]{:S(2)}) async-start(bf16[4,4,64,1024]{3,2,1,0:T(8,128)(2,1)} %bitcast.8), calls=%async_computation | async-start | bytes 4194304 | tf_op jit(solution)/shard_map/all_to_all | solution.py:823
  36.2 156.8 %all-gather.8.cloned.1.call-start = ((), (), s32[]{:S(2)}) async-start(), calls=%async_computation.10 | async-start | bytes 9437184 | tf_op jit(solution)/shard_map/all_gather | solution.py:929
  45.6 27.3 %collective-permute-start.2 = (bf16[128,3072]{1,0:T(8,128)(2,1)S(1)}, bf16[128,3072]{1,0:T(8,128)(2,1)}, u32[]{:S(2)}, u32[]{:S(2)}) collective-permute-start(bf16[128,3072]{1,0:T(8,128)(2,1)S(1)} %copy-done.23), channel_id=1, source_target_pairs={{0,24},{4,28},{8,16},{12,20},{16,8},{20,12},{24,0},{28,4},{1,25},{... | collective-permute-start | bytes 2359304 | tf_op jit(solution)/shard_map/ppermute | solution.py:812
  83.3 3.7 collective-permute-start.6
  83.3 4.4 collective-permute-start.4
  83.8 5.2 collective-permute-start.5
  83.9 6.1 collective-permute-start.3
  90.0 133.2 %all-gather.10.cloned.1.call-start = ((), (), s32[]{:S(2)}) async-start(), calls=%async_computation.11 | async-start | bytes 9437184 | tf_op jit(solution)/shard_map/all_gather | solution.py:929
  105.7 29.8 %all-to-all-start.2 = ((bf16[4,2,64,1024]{3,2,1,0:T(8,128)(2,1)}), bf16[4,2,64,1024]{3,2,1,0:T(8,128)(2,1)S(1)}, u32[]{:S(2)}, u32[]{:S(2)}) async-start(bf16[4,2,64,1024]{3,2,1,0:T(8,128)(2,1)} %get-tuple-element.86), calls=%async_computation.2 | async-start | bytes 2097152 | tf_op jit(solution)/shard_map/all_to_all | solution.py:823
  122.7 18.8 %copy-start.22 = (s32[1,13]{1,0:T(1,128)S(1)}, s32[1,13]{1,0:T(1,128)}, u32[]{:S(2)}) copy-start(s32[1,13]{1,0:T(1,128)} %param.17) | copy-start | bytes 160
  135.6 29.8 %copy-start.3 = (bf16[4,2,64,1024]{3,2,1,0:T(8,128)(2,1)}, bf16[4,2,64,1024]{3,2,1,0:T(8,128)(2,1)S(1)}, u32[]{:S(2)}) copy-start(bf16[4,2,64,1024]{3,2,1,0:T(8,128)(2,1)S(1)} %all-to-all-done.2.refs_3_) | copy-start | bytes 3145732
  135.6 29.8 %all-to-all-start.1 = ((bf16[4,2,64,1024]{3,2,1,0:T(8,128)(2,1)}), bf16[4,2,64,1024]{3,2,1,0:T(8,128)(2,1)}, u32[]{:S(2)}, u32[]{:S(2)}) async-start(bf16[4,2,64,1024]{3,2,1,0:T(8,128)(2,1)} %get-tuple-element.85), calls=%async_computation.1 | async-start | bytes 2097152 | tf_op jit(solution)/shard_map/all_to_all | solution.py:823
  139.8 194.9 %reduce-scatter.3.cloned.1.call-start = ((), (), s32[]{:S(2)}) async-start(), calls=%async_computation.12 | async-start | bytes 9437184 | tf_op jit(solution)/shard_map/reduce_scatter | solution.py:1004
  263.7 156.4 %reduce-scatter.5.cloned.1.call-start = ((), (), s32[]{:S(2)}) async-start(), calls=%async_computation.13 | async-start | bytes 9437184 | tf_op jit(solution)/shard_map/reduce_scatter | solution.py:989
  319.9 5.6 copy-start.6
  319.9 51.6 %collective-permute-start.7 = (bf16[512,5120]{1,0:T(8,128)(2,1)}, bf16[512,5120]{1,0:T(8,128)(2,1)}, u32[]{:S(2)}, u32[]{:S(2)}) collective-permute-start(bf16[512,5120]{1,0:T(8,128)(2,1)} %get-tuple-element.110), channel_id=1, source_target_pairs={{0,4},{4,0},{8,12},{12,8},{16,20},{20,16},{24,28},{28,24},{1,5},{5... | collective-permute-start | bytes 15728648 | tf_op jit(solution)/shard_map/ppermute | solution.py:812
  320.0 30.5 %all-to-all-start.3 = ((bf16[4,2,64,1024]{3,2,1,0:T(8,128)(2,1)}), bf16[4,2,64,1024]{3,2,1,0:T(8,128)(2,1)S(1)}, u32[]{:S(2)}, u32[]{:S(2)}) async-start(bf16[4,2,64,1024]{3,2,1,0:T(8,128)(2,1)} %get-tuple-element.112), calls=%async_computation.4 | async-start | bytes 2097152 | tf_op jit(solution)/shard_map/all_to_all | solution.py:823
  351.5 29.1 %all-to-all-start.4 = ((bf16[4,2,64,1024]{3,2,1,0:T(8,128)(2,1)}), bf16[4,2,64,1024]{3,2,1,0:T(8,128)(2,1)S(1)}, u32[]{:S(2)}, u32[]{:S(2)}) async-start(bf16[4,2,64,1024]{3,2,1,0:T(8,128)(2,1)} %get-tuple-element.118), calls=%async_computation.5 | async-start | bytes 2097152 | tf_op jit(solution)/shard_map/all_to_all | solution.py:823
  381.6 16.6 %copy-start.16 = (f32[1,1024]{1,0:T(1,128)S(1)}, f32[1,1024]{1,0:T(1,128)}, u32[]{:S(2)}) copy-start(f32[1,1024]{1,0:T(1,128)} %get-tuple-element.140) | copy-start | bytes 12292
  381.6 17.3 %copy-start.15 = (f32[1,1024]{1,0:T(1,128)S(1)}, f32[1,1024]{1,0:T(1,128)}, u32[]{:S(2)}) copy-start(f32[1,1024]{1,0:T(1,128)} %get-tuple-element.136) | copy-start | bytes 12292
  381.6 17.9 %copy-start.8 = (f32[2,1,1024]{2,1,0:T(1,128)S(1)}, f32[2,1,1024]{2,1,0:T(1,128)}, u32[]{:S(2)}) copy-start(f32[2,1,1024]{2,1,0:T(1,128)} %get-tuple-element.134) | copy-start | bytes 24580
  381.6 18.9 %copy-start.10 = (f32[1,1024]{1,0:T(1,128)S(1)}, f32[1,1024]{1,0:T(1,128)}, u32[]{:S(2)}) copy-start(f32[1,1024]{1,0:T(1,128)} %get-tuple-element.139) | copy-start | bytes 12292
  381.6 18.9 %copy-start.11 = (f32[1,1024]{1,0:T(1,128)S(1)}, f32[1,1024]{1,0:T(1,128)}, u32[]{:S(2)}) copy-start(f32[1,1024]{1,0:T(1,128)} %get-tuple-element.143) | copy-start | bytes 12292
  381.6 18.9 %copy-start.12 = (f32[1,1024]{1,0:T(1,128)S(1)}, f32[1,1024]{1,0:T(1,128)}, u32[]{:S(2)}) copy-start(f32[1,1024]{1,0:T(1,128)} %get-tuple-element.145) | copy-start | bytes 12292
  381.6 18.9 %copy-start.13 = (f32[1,1024]{1,0:T(1,128)S(1)}, f32[1,1024]{1,0:T(1,128)}, u32[]{:S(2)}) copy-start(f32[1,1024]{1,0:T(1,128)} %get-tuple-element.138) | copy-start | bytes 12292
  381.6 18.9 %copy-start.14 = (f32[1,1024]{1,0:T(1,128)S(1)}, f32[1,1024]{1,0:T(1,128)}, u32[]{:S(2)}) copy-start(f32[1,1024]{1,0:T(1,128)} %get-tuple-element.142) | copy-start | bytes 12292
  400.7 1.4 collective-permute-start.9
  402.1 7.5 %collective-permute-start.10 = (f32[19,1024]{1,0:T(8,128)S(1)}, f32[19,1024]{1,0:T(8,128)S(1)}, u32[]{:S(2)}, u32[]{:S(2)}) collective-permute-start(f32[19,1024]{1,0:T(8,128)S(1)} %add.122), channel_id=1, source_target_pairs={{0,8},{4,12},{8,0},{12,4},{16,24},{20,28},{24,16},{28,20},{1,9},{5... | collective-permute-start | bytes 233480 | tf_op jit(solution)/shard_map/ppermute | solution.py:812
  409.7 4.8 collective-permute-start.11
  414.4 17.1 %collective-permute-start.12 = (f32[19,1024]{1,0:T(8,128)S(1)}, f32[19,1024]{1,0:T(8,128)S(1)}, u32[]{:S(2)}, u32[]{:S(2)}) collective-permute-start(f32[19,1024]{1,0:T(8,128)S(1)} %add.124), channel_id=1, source_target_pairs={{0,1},{1,0},{2,3},{3,2},{4,5},{5,4},{6,7},{7,6},{8,9},{9,8},{10,11... | collective-permute-start | bytes 233480 | tf_op jit(solution)/shard_map/ppermute | solution.py:870
  420.1 45.7 %collective-permute-start.8 = (bf16[512,1024]{1,0:T(8,128)(2,1)}, bf16[512,1024]{1,0:T(8,128)(2,1)}, u32[]{:S(2)}, u32[]{:S(2)}) collective-permute-start(bf16[512,1024]{1,0:T(8,128)(2,1)} %reduce-scatter.5.cloned.1.call-done), channel_id=1, source_target_pairs={{0,1},{3,2},{4,5},{7,6},{8,9},{11,10},{12,13},{15,14},{16,17},{19,... | collective-permute-start | bytes 3145736 | tf_op jit(solution)/shard_map/ppermute | solution.py:843
  423.5 53.6 %collective-permute-start.21 = (bf16[128,5120]{1,0:T(8,128)(2,1)}, bf16[128,5120]{1,0:T(8,128)(2,1)}, u32[]{:S(2)}, u32[]{:S(2)}) collective-permute-start(bf16[128,5120]{1,0:T(8,128)(2,1)} %get-tuple-element.147), channel_id=1, source_target_pairs={{0,8},{4,12},{8,0},{12,4},{16,24},{20,28},{24,16},{28,20},{1,9},{5... | collective-permute-start | bytes 3932168 | tf_op jit(solution)/shard_map/ppermute | solution.py:812
  424.4 57.7 %collective-permute-start.22 = (bf16[128,5120]{1,0:T(8,128)(2,1)}, bf16[128,5120]{1,0:T(8,128)(2,1)}, u32[]{:S(2)}, u32[]{:S(2)}) collective-permute-start(bf16[128,5120]{1,0:T(8,128)(2,1)} %get-tuple-element.149), channel_id=1, source_target_pairs={{0,16},{4,20},{8,24},{12,28},{16,0},{20,4},{24,8},{28,12},{1,17},{... | collective-permute-start | bytes 3932168 | tf_op jit(solution)/shard_map/ppermute | solution.py:812
  425.9 56.2 %collective-permute-start.23 = (bf16[128,5120]{1,0:T(8,128)(2,1)}, bf16[128,5120]{1,0:T(8,128)(2,1)}, u32[]{:S(2)}, u32[]{:S(2)}) collective-permute-start(bf16[128,5120]{1,0:T(8,128)(2,1)} %get-tuple-element.148), channel_id=1, source_target_pairs={{0,24},{4,28},{8,16},{12,20},{16,8},{20,12},{24,0},{28,4},{1,25},{... | collective-permute-start | bytes 3932168 | tf_op jit(solution)/shard_map/ppermute | solution.py:812
  427.0 43.3 %all-to-all-start.6 = ((bf16[4,2,64,1024]{3,2,1,0:T(8,128)(2,1)}), bf16[4,2,64,1024]{3,2,1,0:T(8,128)(2,1)S(1)}, u32[]{:S(2)}, u32[]{:S(2)}) async-start(bf16[4,2,64,1024]{3,2,1,0:T(8,128)(2,1)} %get-tuple-element.132), calls=%async_computation.8 | async-start | bytes 2097152 | tf_op jit(solution)/shard_map/all_to_all | solution.py:823
  431.6 31.2 %collective-permute-start.13 = (f32[19,1024]{1,0:T(8,128)S(1)}, f32[19,1024]{1,0:T(8,128)S(1)}, u32[]{:S(2)}, u32[]{:S(2)}) collective-permute-start(f32[19,1024]{1,0:T(8,128)S(1)} %add.125), channel_id=1, source_target_pairs={{0,2},{1,3},{2,0},{3,1},{4,6},{5,7},{6,4},{7,5},{8,10},{9,11},{10,... | collective-permute-start | bytes 233480 | tf_op jit(solution)/shard_map/ppermute | solution.py:870
  462.8 84.8 %collective-permute-start.14 = (bf16[512,3072]{1,0:T(8,128)(2,1)}, bf16[512,3072]{1,0:T(8,128)(2,1)}, u32[]{:S(2)}, u32[]{:S(2)}) collective-permute-start(bf16[512,3072]{1,0:T(8,128)(2,1)} %get-tuple-element.126), channel_id=1, source_target_pairs={{0,4},{4,0},{8,12},{12,8},{16,20},{20,16},{24,28},{28,24},{1,5},{5... | collective-permute-start | bytes 9437192 | tf_op jit(solution)/shard_map/ppermute | solution.py:812
  468.7 57.8 %collective-permute-start.30 = (bf16[512,1024]{1,0:T(8,128)(2,1)}, bf16[512,1024]{1,0:T(8,128)(2,1)}, u32[]{:S(2)}, u32[]{:S(2)}) collective-permute-start(bf16[512,1024]{1,0:T(8,128)(2,1)} %add_convert_fusion.7), channel_id=1, source_target_pairs={{1,2},{2,1},{5,6},{6,5},{9,10},{10,9},{13,14},{14,13},{17,18},{18,... | collective-permute-start | bytes 3145736 | tf_op jit(solution)/shard_map/ppermute | solution.py:843
  470.3 11.7 %copy-start = (bf16[4,2,64,1024]{3,2,1,0:T(8,128)(2,1)}, bf16[4,2,64,1024]{3,2,1,0:T(8,128)(2,1)S(1)}, u32[]{:S(2)}) copy-start(bf16[4,2,64,1024]{3,2,1,0:T(8,128)(2,1)S(1)} %all-to-all-done.6.refs_1_) | copy-start | bytes 3145732
  470.3 51.8 %all-to-all-start.5 = ((bf16[4,2,64,1024]{3,2,1,0:T(8,128)(2,1)}), bf16[4,2,64,1024]{3,2,1,0:T(8,128)(2,1)}, u32[]{:S(2)}, u32[]{:S(2)}) async-start(bf16[4,2,64,1024]{3,2,1,0:T(8,128)(2,1)} %get-tuple-element.131), calls=%async_computation.7 | async-start | bytes 2097152 | tf_op jit(solution)/shard_map/all_to_all | solution.py:823
  477.2 52.6 %collective-permute-start.27 = (bf16[128,4096]{1,0:T(8,128)(2,1)}, bf16[128,4096]{1,0:T(8,128)(2,1)}, u32[]{:S(2)}, u32[]{:S(2)}) collective-permute-start(bf16[128,4096]{1,0:T(8,128)(2,1)} %reduce-scatter.3.cloned.1.call-done), channel_id=1, source_target_pairs={{0,1},{3,2},{4,5},{7,6},{8,9},{11,10},{12,13},{15,14},{16,17},{19,... | collective-permute-start | bytes 3145736 | tf_op jit(solution)/shard_map/ppermute | solution.py:843
  485.4 59.8 %collective-permute-start.24 = (bf16[128,5120]{1,0:T(8,128)(2,1)S(1)}, bf16[128,5120]{1,0:T(8,128)(2,1)}, u32[]{:S(2)}, u32[]{:S(2)}) collective-permute-start(bf16[128,5120]{1,0:T(8,128)(2,1)S(1)} %fusion.2), channel_id=1, source_target_pairs={{0,1},{3,2},{4,5},{7,6},{8,9},{11,10},{12,13},{15,14},{16,17},{19,... | collective-permute-start | bytes 3932168 | tf_op jit(solution)/shard_map/ppermute | solution.py:843
  528.4 26.7 %collective-permute-start.31 = (bf16[512,1024]{1,0:T(8,128)(2,1)S(1)}, bf16[512,1024]{1,0:T(8,128)(2,1)S(1)}, u32[]{:S(2)}, u32[]{:S(2)}) collective-permute-start(bf16[512,1024]{1,0:T(8,128)(2,1)S(1)} %add_convert_fusion.4), channel_id=1, source_target_pairs={{1,0},{2,3},{5,4},{6,7},{9,8},{10,11},{13,12},{14,15},{17,16},{18,... | collective-permute-start | bytes 3145736 | tf_op jit(solution)/shard_map/ppermute | solution.py:843
  531.5 16.0 %copy-start.1 = (bf16[512,3072]{1,0:T(8,128)(2,1)S(1)}, bf16[512,3072]{1,0:T(8,128)(2,1)}, u32[]{:S(2)}) copy-start(bf16[512,3072]{1,0:T(8,128)(2,1)} %get-tuple-element.146) | copy-start | bytes 9437188
  531.5 21.4 %collective-permute-start.28 = (bf16[128,4096]{1,0:T(8,128)(2,1)S(1)}, bf16[128,4096]{1,0:T(8,128)(2,1)S(1)}, u32[]{:S(2)}, u32[]{:S(2)}) collective-permute-start(bf16[128,4096]{1,0:T(8,128)(2,1)S(1)} %add_convert_fusion.6), channel_id=1, source_target_pairs={{1,2},{2,1},{5,6},{6,5},{9,10},{10,9},{13,14},{14,13},{17,18},{18,... | collective-permute-start | bytes 3145736 | tf_op jit(solution)/shard_map/ppermute | solution.py:843
  546.8 49.3 %collective-permute-start.25 = (bf16[128,5120]{1,0:T(8,128)(2,1)S(1)}, bf16[128,5120]{1,0:T(8,128)(2,1)S(1)}, u32[]{:S(2)}, u32[]{:S(2)}) collective-permute-start(bf16[128,5120]{1,0:T(8,128)(2,1)S(1)} %add_convert_fusion.3), channel_id=1, source_target_pairs={{1,2},{2,1},{5,6},{6,5},{9,10},{10,9},{13,14},{14,13},{17,18},{18,... | collective-permute-start | bytes 3932168 | tf_op jit(solution)/shard_map/ppermute | solution.py:843
  550.8 20.5 %collective-permute-start.15 = (bf16[128,3072]{1,0:T(8,128)(2,1)S(1)}, bf16[128,3072]{1,0:T(8,128)(2,1)S(1)}, u32[]{:S(2)}, u32[]{:S(2)}) collective-permute-start(bf16[128,3072]{1,0:T(8,128)(2,1)S(1)} %get-tuple-element.150), channel_id=1, source_target_pairs={{0,8},{4,12},{8,0},{12,4},{16,24},{20,28},{24,16},{28,20},{1,9},{5... | collective-permute-start | bytes 2359304 | tf_op jit(solution)/shard_map/ppermute | solution.py:812
  552.3 33.6 %collective-permute-start.16 = (bf16[128,3072]{1,0:T(8,128)(2,1)S(1)}, bf16[128,3072]{1,0:T(8,128)(2,1)S(1)}, u32[]{:S(2)}, u32[]{:S(2)}) collective-permute-start(bf16[128,3072]{1,0:T(8,128)(2,1)S(1)} %get-tuple-element.152), channel_id=1, source_target_pairs={{0,16},{4,20},{8,24},{12,28},{16,0},{20,4},{24,8},{28,12},{1,17},{... | collective-permute-start | bytes 2359304 | tf_op jit(solution)/shard_map/ppermute | solution.py:812
  553.0 34.8 %collective-permute-start.17 = (bf16[128,3072]{1,0:T(8,128)(2,1)S(1)}, bf16[128,3072]{1,0:T(8,128)(2,1)S(1)}, u32[]{:S(2)}, u32[]{:S(2)}) collective-permute-start(bf16[128,3072]{1,0:T(8,128)(2,1)S(1)} %get-tuple-element.151), channel_id=1, source_target_pairs={{0,24},{4,28},{8,16},{12,20},{16,8},{20,12},{24,0},{28,4},{1,25},{... | collective-permute-start | bytes 2359304 | tf_op jit(solution)/shard_map/ppermute | solution.py:812
  555.1 56.7 %collective-permute-start.29 = (bf16[128,4096]{1,0:T(8,128)(2,1)S(1)}, bf16[128,4096]{1,0:T(8,128)(2,1)S(1)}, u32[]{:S(2)}, u32[]{:S(2)}) collective-permute-start(bf16[128,4096]{1,0:T(8,128)(2,1)S(1)} %add_convert_fusion.5), channel_id=1, source_target_pairs={{1,0},{2,3},{5,4},{6,7},{9,8},{10,11},{13,12},{14,15},{17,16},{18,... | collective-permute-start | bytes 3145736 | tf_op jit(solution)/shard_map/ppermute | solution.py:843
  588.3 22.7 %collective-permute-start.18 = (bf16[128,3072]{1,0:T(8,128)(2,1)S(1)}, bf16[128,3072]{1,0:T(8,128)(2,1)S(1)}, u32[]{:S(2)}, u32[]{:S(2)}) collective-permute-start(bf16[128,3072]{1,0:T(8,128)(2,1)S(1)} %add_convert_fusion.10), channel_id=1, source_target_pairs={{0,1},{3,2},{4,5},{7,6},{8,9},{11,10},{12,13},{15,14},{16,17},{19,... | collective-permute-start | bytes 2359304 | tf_op jit(solution)/shard_map/ppermute | solution.py:843
  596.4 30.2 %collective-permute-start.26 = (bf16[128,5120]{1,0:T(8,128)(2,1)S(1)}, bf16[128,5120]{1,0:T(8,128)(2,1)S(1)}, u32[]{:S(2)}, u32[]{:S(2)}) collective-permute-start(bf16[128,5120]{1,0:T(8,128)(2,1)S(1)} %add_convert_fusion.2), channel_id=1, source_target_pairs={{1,0},{2,3},{5,4},{6,7},{9,8},{10,11},{13,12},{14,15},{17,16},{18,... | collective-permute-start | bytes 3932168 | tf_op jit(solution)/shard_map/ppermute | solution.py:843
  611.1 2.2 collective-permute-start.19
  613.5 33.7 %collective-permute-start.20 = (bf16[128,3072]{1,0:T(8,128)(2,1)S(1)}, bf16[128,3072]{1,0:T(8,128)(2,1)S(1)}, u32[]{:S(2)}, u32[]{:S(2)}) collective-permute-start(bf16[128,3072]{1,0:T(8,128)(2,1)S(1)} %add_convert_fusion.8), channel_id=1, source_target_pairs={{1,0},{2,3},{5,4},{6,7},{9,8},{10,11},{13,12},{14,15},{17,16},{18,... | collective-permute-start | bytes 2359304 | tf_op jit(solution)/shard_map/ppermute | solution.py:843
  (11 other events, 31.2 us)
Sparse Core Ops, SparseCore 0:
  29.6 80.5 all-gather.5
  112.1 54.3 all-gather.7
  168.4 54.3 all-gather.9
  263.8 70.8 reduce-scatter.2
  338.4 73.2 reduce-scatter.4
